TPU v7x, 128 devices: a whole 4x4x4 slice. The times are simulated.
128 devices in a mesh: rec: 4 (over y), ctx: 32 (over x, z, core).
Axes of the slice: x: 4, y: 4, z: 4, core: 2. Of those that a mesh axis runs over, the one named last changes fastest.
Arguments:
- queries: bfloat16 [4, 1024, 2048], P('rec', 'ctx'), may hold values from -360 to 360
- grad_out: bfloat16 [4, 1024, 2048], P('rec', 'ctx'), may hold values from -6 to 6
- keys: bfloat16 [4096, 2048], P('ctx'), may hold values from -13 to 13
- values: bfloat16 [4096, 2048], P('ctx'), may hold values from -6 to 6
- surv_index: int32 [4, 1024], P('rec'), may hold values from 0 to 127, as said below
- counts: int32 [4, 32], P('rec'), may hold values from 1 to 32, as said below
Outputs:
- query_grad: bfloat16 [4, 1024, 2048], P('rec', 'ctx')
- key_grad: bfloat16 [4096, 2048], P('ctx', 'rec')
- value_grad: bfloat16 [4096, 2048], P('ctx', 'rec')
Inputs may be any that keep to these rules, and one draw needn't show every extreme that they name: `surv_index`: in each depth and index of ctx the live slots come first and hold distinct positions in increasing order; the other slots hold 0. In each depth and index of ctx whose 32 slots are all live, one live slot holds position 127. `counts`: in every depth some index of ctx has all 32 slots live.
All inputs are finite; a program needn't handle non-finite values.
Results may differ from a plain program's by a relative error of at most 0.0051.
Values may be sent and summed in bfloat16 or wider, within the bound.
No kernel may reach another device: no remote copies, remote signals or barrier semaphores. Data moves between devices by JAX's collectives and lax.ppermute only.
A program may use at most 64 MiB of HBM per device.

v0:
```python
import math

import jax
import jax.numpy as jnp
from jax import lax
from jax.sharding import Mesh
from jax.sharding import PartitionSpec as P

HEADS = 16
HEAD_DIM = 128
CTX = ("ctx_0", "ctx_1", "ctx_2")


NEG_FILL = -1e30


def sent_together(arrays, axis, dim, along):
    both = jnp.concatenate(arrays, axis=along)
    out, at, outs = (lax.all_gather(both, axis, axis=dim, tiled=True), 0, [])
    for a in arrays:
        outs.append(lax.slice_in_dim(out, at, at + a.shape[along], axis=along))
        at += a.shape[along]
    return tuple(outs)


def all_in_one(shard, axis):
    leaves = jax.tree.leaves(shard)
    order = sorted(range(len(leaves)), key=lambda k: -leaves[k].size)
    width = (1, *leaves[order[0]].shape)[-1]
    lines = [
        jnp.pad(leaves[k].reshape(-1), (0, -leaves[k].size % width)).reshape(-1, width)
        for k in order
    ]
    both, at, found = (lax.all_gather(jnp.concatenate(lines), axis), 0, {})
    for k, line in zip(order, lines):
        slab = both[:, at : at + len(line)].reshape(len(both), -1)
        found[k] = slab[:, : leaves[k].size].reshape(-1, *leaves[k].shape)
        at += len(line)
    numbers = iter(range(len(leaves)))
    return jax.tree.map(lambda _: found[next(numbers)], shard)


def joined_all(shard, axes, combine):
    for axis in axes:
        pieces = all_in_one(shard, axis)
        shard = jax.tree.map(lambda part: part[0], pieces)
        for k in range(1, lax.axis_size(axis)):
            shard = combine(shard, jax.tree.map(lambda part: part[k], pieces))
    return shard


def cut_along(shard, dim, count):
    before, after = (shard.shape[:dim], shard.shape[dim + 1 :])
    return jnp.moveaxis(shard.reshape(*before, count, -1, *after), dim, 0)


def sent_and_summed(shard, axis, dim):
    count = lax.axis_size(axis)
    blocks = lax.all_to_all(cut_along(shard, dim, count), axis, 0, 0, tiled=True)
    return jnp.sum(blocks, axis=0)


def in_one_piece(arrays, axis, dim, along):
    both = jnp.concatenate(arrays, axis=along)
    out, at, outs = (sent_and_summed(both, axis, dim), 0, [])
    for a in arrays:
        outs.append(lax.slice_in_dim(out, at, at + a.shape[along], axis=along))
        at += a.shape[along]
    return tuple(outs)


def combine_triple(first_stats, second_stats):
    joint_max = jnp.maximum(first_stats[0], second_stats[0])
    left_scale = jnp.exp(first_stats[0] - joint_max)
    right_scale = jnp.exp(second_stats[0] - joint_max)
    return (
        joint_max,
        first_stats[1] * left_scale + second_stats[1] * right_scale,
        first_stats[2] * left_scale + second_stats[2] * right_scale,
    )


def body(queries, grad_out, keys, values, surv_index, counts):
    ctx_count = lax.axis_size(CTX)
    my_index = lax.axis_index(CTX)
    cap_here = queries.shape[1]
    feature_cols = queries.shape[2]
    tok_here = keys.shape[0]
    all_slots = cap_here * ctx_count
    block_rows = min(512, all_slots)
    block_count = all_slots // block_rows
    factor = 1.0 / math.sqrt(HEAD_DIM)
    gathered_q, gathered_g = sent_together((queries[0], grad_out[0]), CTX, 0, 1)
    slot_ids = jnp.arange(all_slots)
    is_live = slot_ids % cap_here < jnp.repeat(counts[0], cap_here)
    query_pos = slot_ids // cap_here * tok_here + surv_index[0]
    gathered_g = jnp.where(is_live[:, None], gathered_g, jnp.zeros_like(gathered_g))
    key_pos = my_index * tok_here + jnp.arange(tok_here)
    keys_split = keys.reshape(tok_here, HEADS, HEAD_DIM)
    value_pieces = values.reshape(tok_here, HEADS, HEAD_DIM)
    query_blocks = gathered_q.reshape(block_count, block_rows, HEADS, HEAD_DIM)
    gradient_tiles = gathered_g.reshape(block_count, block_rows, HEADS, HEAD_DIM)
    pos_blocks = query_pos.reshape(block_count, block_rows)

    def block_scores(query_block, pos_block):
        score_matrix = factor * jnp.einsum(
            "rhd,khd->hrk", query_block, keys_split, preferred_element_type=jnp.float32
        )
        visible = key_pos[None, None, :] <= pos_block[None, :, None]
        return (score_matrix, visible)

    def weight_grads(grad_block):
        return jnp.einsum(
            "rhd,khd->hrk", grad_block, value_pieces, preferred_element_type=jnp.float32
        )

    def as_rows(stacked):
        return stacked.transpose(1, 0, 2).reshape(HEADS, all_slots)

    def as_blocks(per_row):
        return per_row.reshape(HEADS, block_count, block_rows).transpose(1, 0, 2)

    def local_moments(operands):
        query_block, grad_block, pos_block = operands
        score_matrix, visible = block_scores(query_block, pos_block)
        row_max = jnp.max(jnp.where(visible, score_matrix, NEG_FILL), axis=2)
        shifted = jnp.where(visible, jnp.exp(score_matrix - row_max[:, :, None]), 0.0)
        row_sum = jnp.sum(shifted, axis=2)
        row_weighted = jnp.sum(shifted * weight_grads(grad_block), axis=2)
        return (row_max, row_sum, row_weighted)

    part_max, part_sum, part_weighted = lax.map(
        local_moments, (query_blocks, gradient_tiles, pos_blocks)
    )
    row_max, row_sum, row_weighted = joined_all(
        (as_rows(part_max), as_rows(part_sum), as_rows(part_weighted)), CTX, combine_triple
    )
    log_total = row_max + jnp.log(row_sum)
    row_delta = row_weighted / row_sum
    log_blocks = as_blocks(log_total)
    delta_blocks = as_blocks(row_delta)

    def block_grads(query_block, grad_block, pos_block, log_block, delta_block):
        score_matrix, visible = block_scores(query_block, pos_block)
        weights = jnp.where(visible, jnp.exp(score_matrix - log_block[:, :, None]), 0.0)
        grad_weights = weight_grads(grad_block)
        grad_scores = (weights * (grad_weights - delta_block[:, :, None])).astype(jnp.bfloat16)
        return (weights, grad_scores)

    def query_product(grad_scores):
        return factor * jnp.einsum(
            "hrk,khd->rhd", grad_scores, keys_split, preferred_element_type=jnp.float32
        )

    def final_block(totals, operands):
        query_block, grad_block, pos_block, log_block, delta_block = operands
        weights, grad_scores = block_grads(
            query_block, grad_block, pos_block, log_block, delta_block
        )
        low_weights = weights.astype(jnp.bfloat16)
        key_part = totals[0] + factor * jnp.einsum(
            "hrk,rhd->khd", grad_scores, query_block, preferred_element_type=jnp.float32
        )
        value_part = totals[1] + jnp.einsum(
            "hrk,rhd->khd", low_weights, grad_block, preferred_element_type=jnp.float32
        )
        return ((key_part, value_part), grad_scores)

    empty_sum = jnp.zeros((tok_here, HEADS, HEAD_DIM), jnp.float32)

    def final_with_query(totals, operands):
        new_totals, grad_scores = final_block(totals, operands)
        return (new_totals, query_product(grad_scores))

    sums, query_terms = lax.scan(
        final_with_query,
        (empty_sum, empty_sum),
        (query_blocks, gradient_tiles, pos_blocks, log_blocks, delta_blocks),
    )
    query_terms = query_terms.reshape(all_slots, feature_cols)
    own_rows = lax.psum_scatter(query_terms, CTX, scatter_dimension=0, tiled=True)
    key_cols, value_cols = in_one_piece(
        (sums[0].reshape(tok_here, feature_cols), sums[1].reshape(tok_here, feature_cols)),
        "rec",
        1,
        0,
    )
    return (
        own_rows.astype(jnp.bfloat16)[None],
        key_cols.astype(jnp.bfloat16),
        value_cols.astype(jnp.bfloat16),
    )


def solution(mesh):
    split = Mesh(
        mesh.devices.reshape(mesh.shape["rec"], 4, 4, 2), ("rec", "ctx_0", "ctx_1", "ctx_2")
    )
    return jax.shard_map(
        body,
        mesh=split,
        in_specs=(
            P("rec", CTX, None),
            P("rec", CTX, None),
            P(CTX, None),
            P(CTX, None),
            P("rec", None),
            P("rec", None),
        ),
        out_specs=(P("rec", CTX, None), P(CTX, "rec"), P(CTX, "rec")),
        check_vma=False,
    )
```

profile of v0, /device:TPU:0, one launch (start us, length us, event | category | flops | bytes accessed | tf_op | source)
XLA Modules:
  0.0 264.1 jit_solution(17109194322119815515)
XLA Ops:
  7.2 1.7 pad_maximum_fusion
  9.6 1.3 reduce.3
  11.7 1.3 copy.32
  13.3 1.3 copy.33
  15.7 49.9 %all-gather.5.cloned.1.call-done = bf16[1024,4096]{1,0:T(8,128)(2,1)} async-done(((bf16[32,4096]{1,0:T(8,128)(2,1)}), bf16[1024,4096]{1,0:T(8,128)(2,1)}) %all-gather.5.cloned.1.call-update) | async-done | bytes 8388624 | tf_op jit(solution)/shard_map/all_gather | solution.py:19
  65.6 4.0 %fusion.54 = (bf16[128,8,16,128]{3,1,2,0:T(8,128)(2,1)S(1)}, bf16[128,8,16,128]{3,1,2,0:T(8,128)(2,1)S(1)}) fusion(bf16[1024,4096]{1,0:T(8,128)(2,1)} %all-gather.5.cloned.1.call-done, pred[1024]{0:T(1024)(128)(4,1)S(1)} %fusion.98), kind=kLoop, calls=%fused_computation.59 | loop fusion | flops 2097152 | bytes 16778240
  69.6 1.4 copy.61
  71.0 3.0 %copy.36 = bf16[2,512,16,128]{3,1,2,0:T(8,128)(2,1)} copy(bf16[2,512,16,128]{3,2,1,0:T(8,128)(2,1)S(1)} %bitcast.399) | data formatting | bytes 8388608
  74.0 1.4 copy.60
  75.5 3.1 %copy.41 = bf16[2,512,16,128]{3,1,2,0:T(8,128)(2,1)} copy(bf16[2,512,16,128]{3,2,1,0:T(8,128)(2,1)S(1)} %bitcast.400) | data formatting | bytes 8388608
  78.5 10.1 %while.30 = (s32[]{:T(128)}, f32[2,16,512]{2,1,0:T(8,128)S(1)}, f32[2,16,512]{2,1,0:T(8,128)S(1)}, f32[2,16,512]{2,1,0:T(8,128)S(1)}, s32[2,512]{1,0:T(2,128)S(1...) while((s32[]{:T(128)}, f32[2,16,512]{2,1,0:T(8,128)S(1)}, ...), condition=%wide.region_4.5_spmd.clone, body=%wide.region_0.4_spmd.clone.sunk | while | flops 549494912 | bytes 37330116 | solution.py:132
  78.7 2.6 select_reduce_fusion.2
  82.2 1.3 multiply_reduce_fusion.2
  83.7 2.6 select_reduce_fusion.2
  88.7 14.0 %all-gather = f32[192,1024]{1,0:T(8,128)S(1)} all-gather(f32[48,1024]{1,0:T(8,128)S(1)} %pad_maximum_fusion.1), channel_id=2, replica_groups=mesh['rec'=4,'ctx_0'=4,'ctx_1'=4,'ctx_2'=2] {'ctx_0'}, dimensions={0}, use_global_device_ids=true | all-gather | bytes 983040 | tf_op jit(solution)/shard_map/all_gather | solution.py:34
  102.8 14.2 %all-gather.1 = f32[192,1024]{1,0:T(8,128)S(1)} all-gather(f32[48,1024]{1,0:T(8,128)S(1)} %pad_maximum_fusion.2), channel_id=3, replica_groups=mesh['rec'=4,'ctx_0'=4,'ctx_1'=4,'ctx_2'=2] {'ctx_1'}, dimensions={0}, use_global_device_ids=true | all-gather | bytes 983040 | tf_op jit(solution)/shard_map/all_gather | solution.py:34
  117.1 2.3 all-gather.2
  120.0 33.0 %while.31 = (s32[]{:T(128)}, f32[128,16,128]{0,2,1:T(8,128)S(1)}, f32[128,16,128]{0,2,1:T(8,128)S(1)}, f32[2,512,16,128]{3,2,1,0:T(8,128)}, bf16[2,512,16,128]{3...) while((s32[]{:T(128)}, f32[128,16,128]{0,2,1:T(8,128)S(1)}, ...), condition=%wide.region_6.7_spmd.clone, body=%wide.region_5.6_spmd.clone.sunk | while | flops 1355088000 | bytes 140549472 | solution.py:175
  120.3 2.5 fusion.144
  122.8 2.5 fusion.146
  125.4 2.7 %multiply_convert_fusion.2 = bf16[16,512,128]{2,1,0:T(8,128)(2,1)S(1)} fusion(f32[16,512,128]{2,1,0:T(8,128)S(1)} %fusion.144, bf16[128,16,128]{2,0,1:T(8,128)(2,1)S(1)} %copy-done.5, f32[16,512]{1,0:T(8,128)S(1)} %bitcast.412, f32[16,512]{1,0:T(8,128)S(1)} %bitcast.414, pred[512,128]{1,0:T(8,128)(4,1)S(1)} %broadcast_compare_fusion.5, ...), kind=kOutput, calls=%fused_computation.21.clone.1 | convolution fusion | flops 274726912 | bytes 9043972 | tf_op jit(solution)/shard_map/while/body/eval_jaxpr/rhd,khd->hrk/dot_general | solution.py:113
  130.5 2.8 %copy_dynamic-update-slice_fusion.2 = f32[2,512,16,128]{3,2,1,0:T(8,128)S(1)} fusion(f32[2,512,16,128]{3,2,1,0:T(8,128)S(1)} %bitcast.402, s32[]{:T(128)S(6)} %copy.96, f32[1,512,16,128]{3,1,2,0:T(8,128)S(1)} %multiply_bitcast_fusion.2), kind=kLoop, calls=%fused_computation.19.clone.1 | loop fusion | bytes 8388612 | tf_op jit(solution)/shard_map/while/body/jit(dynamic_update_index_in_dim)/dynamic_update_slice | solution.py:175
  133.3 3.2 %copy-done.1 = f32[2,512,16,128]{3,2,1,0:T(8,128)} copy-done((f32[2,512,16,128]{3,2,1,0:T(8,128)}, f32[2,512,16,128]{3,2,1,0:T(8,128)S(1)}, u32[]{:S(2)}) %copy-start.1) | copy-done | bytes 8388632 | tf_op jit(solution)/shard_map/while
  136.8 2.4 fusion.144
  139.4 2.5 fusion.146
  141.9 2.7 %multiply_convert_fusion.2 = bf16[16,512,128]{2,1,0:T(8,128)(2,1)S(1)} fusion(f32[16,512,128]{2,1,0:T(8,128)S(1)} %fusion.144, bf16[128,16,128]{2,0,1:T(8,128)(2,1)S(1)} %copy-done.5, f32[16,512]{1,0:T(8,128)S(1)} %bitcast.412, f32[16,512]{1,0:T(8,128)S(1)} %bitcast.414, pred[512,128]{1,0:T(8,128)(4,1)S(1)} %broadcast_compare_fusion.5, ...), kind=kOutput, calls=%fused_computation.21.clone.1 | convolution fusion | flops 274726912 | bytes 9043972 | tf_op jit(solution)/shard_map/while/body/eval_jaxpr/rhd,khd->hrk/dot_general | solution.py:113
  147.0 2.8 %copy_dynamic-update-slice_fusion.2 = f32[2,512,16,128]{3,2,1,0:T(8,128)S(1)} fusion(f32[2,512,16,128]{3,2,1,0:T(8,128)S(1)} %bitcast.402, s32[]{:T(128)S(6)} %copy.96, f32[1,512,16,128]{3,1,2,0:T(8,128)S(1)} %multiply_bitcast_fusion.2), kind=kLoop, calls=%fused_computation.19.clone.1 | loop fusion | bytes 8388612 | tf_op jit(solution)/shard_map/while/body/jit(dynamic_update_index_in_dim)/dynamic_update_slice | solution.py:175
  149.8 3.2 %copy-done.1 = f32[2,512,16,128]{3,2,1,0:T(8,128)} copy-done((f32[2,512,16,128]{3,2,1,0:T(8,128)}, f32[2,512,16,128]{3,2,1,0:T(8,128)S(1)}, u32[]{:S(2)}) %copy-start.1) | copy-done | bytes 8388632 | tf_op jit(solution)/shard_map/while
  153.0 10.7 %copy.69 = f32[128,8,16,128]{3,1,2,0:T(8,128)} copy(f32[128,8,16,128]{3,2,1,0:T(8,128)} %bitcast.403) | data formatting | bytes 16777216
  163.9 30.7 %all_to_all.5 = f32[4,256,512]{1,2,0:T(8,128)S(1)} all-to-all(f32[4,256,512]{1,2,0:T(8,128)S(1)} %maximum_bitcast_fusion), channel_id=1, replica_groups=mesh['rec'=4,'ctx_0'=4,'ctx_1'=4,'ctx_2'=2] {'rec'}, dimensions={0} | all-to-all | bytes 4194304 | tf_op jit(solution)/shard_map/all_to_all | solution.py:59
  196.4 59.3 %reduce-scatter.2.cloned.1.call-done = f32[32,2048]{1,0:T(8,128)} async-done(((f32[1024,2048]{1,0:T(8,128)}), f32[32,2048]{1,0:T(8,128)}) %reduce-scatter.2.cloned.1.call-update) | async-done | bytes 262160 | tf_op jit(solution)/shard_map/reduce_scatter | solution.py:181
  255.6 1.6 convert_bitcast_fusion
  (102 shorter events, 14.3 us)
Async XLA Ops:
  7.2 58.4 %all-gather.5.cloned.1.call-start = ((), (), s32[]{:S(2)}) async-start(), calls=%async_computation.2 | async-start | bytes 8650752 | tf_op jit(solution)/shard_map/all_gather | solution.py:19
  8.9 246.7 %reduce-scatter.2.cloned.1.call-start = ((), (), s32[]{:S(2)}) async-start(), calls=%async_computation.3 | async-start | bytes 8650752 | tf_op jit(solution)/shard_map/reduce_scatter | solution.py:181
  78.6 3.5 %copy-start.2 = (bf16[2,512,16,128]{3,1,2,0:T(8,128)(2,1)S(1)}, bf16[2,512,16,128]{3,1,2,0:T(8,128)(2,1)}, u32[]{:S(2)}) copy-start(bf16[2,512,16,128]{3,1,2,0:T(8,128)(2,1)} %get-tuple-element.480) | copy-start | bytes 12582916 | tf_op jit(solution)/shard_map/while
  78.7 3.5 %copy-start.4 = (bf16[128,16,128]{2,0,1:T(8,128)(2,1)S(1)}, bf16[128,16,128]{2,0,1:T(8,128)(2,1)}, u32[]{:S(2)}) copy-start(bf16[128,16,128]{2,0,1:T(8,128)(2,1)} %get-tuple-element.481) | copy-start | bytes 1572868 | tf_op jit(solution)/shard_map/while
  83.7 3.5 %copy-start.2 = (bf16[2,512,16,128]{3,1,2,0:T(8,128)(2,1)S(1)}, bf16[2,512,16,128]{3,1,2,0:T(8,128)(2,1)}, u32[]{:S(2)}) copy-start(bf16[2,512,16,128]{3,1,2,0:T(8,128)(2,1)} %get-tuple-element.480) | copy-start | bytes 12582916 | tf_op jit(solution)/shard_map/while
  83.7 3.5 %copy-start.4 = (bf16[128,16,128]{2,0,1:T(8,128)(2,1)S(1)}, bf16[128,16,128]{2,0,1:T(8,128)(2,1)}, u32[]{:S(2)}) copy-start(bf16[128,16,128]{2,0,1:T(8,128)(2,1)} %get-tuple-element.481) | copy-start | bytes 1572868 | tf_op jit(solution)/shard_map/while
  120.0 2.8 %copy-start.3 = (bf16[2,512,16,128]{3,1,2,0:T(8,128)(2,1)S(1)}, bf16[2,512,16,128]{3,1,2,0:T(8,128)(2,1)}, u32[]{:S(2)}) copy-start(bf16[2,512,16,128]{3,1,2,0:T(8,128)(2,1)} %get-tuple-element.520) | copy-start | bytes 12582916 | tf_op jit(solution)/shard_map/while
  122.8 2.5 copy-start.5
  125.3 2.8 %copy-start = (bf16[2,512,16,128]{3,1,2,0:T(8,128)(2,1)S(1)}, bf16[2,512,16,128]{3,1,2,0:T(8,128)(2,1)}, u32[]{:S(2)}) copy-start(bf16[2,512,16,128]{3,1,2,0:T(8,128)(2,1)} %get-tuple-element.516) | copy-start | bytes 12582916 | tf_op jit(solution)/shard_map/while
  125.4 4.6 %slice-start = ((s8[8388608]{0:T(1024)(128)(4,1)}), s8[4194304]{0:T(1024)(128)(4,1)S(1)}, s32[]{:S(2)}) async-start(s8[8388608]{0:T(1024)(128)(4,1)} %bitcast.401), calls=%async_computation.4 | async-start | bytes 8388608 | tf_op jit(solution)/shard_map/while
  128.1 2.4 slice-start.1
  133.3 3.2 %copy-start.1 = (f32[2,512,16,128]{3,2,1,0:T(8,128)}, f32[2,512,16,128]{3,2,1,0:T(8,128)S(1)}, u32[]{:S(2)}) copy-start(f32[2,512,16,128]{3,2,1,0:T(8,128)S(1)} %copy_dynamic-update-slice_fusion.2) | copy-start | bytes 25165828 | tf_op jit(solution)/shard_map/while
  136.5 2.8 %copy-start.3 = (bf16[2,512,16,128]{3,1,2,0:T(8,128)(2,1)S(1)}, bf16[2,512,16,128]{3,1,2,0:T(8,128)(2,1)}, u32[]{:S(2)}) copy-start(bf16[2,512,16,128]{3,1,2,0:T(8,128)(2,1)} %get-tuple-element.520) | copy-start | bytes 12582916 | tf_op jit(solution)/shard_map/while
  139.3 2.5 copy-start.5
  141.9 2.8 %copy-start = (bf16[2,512,16,128]{3,1,2,0:T(8,128)(2,1)S(1)}, bf16[2,512,16,128]{3,1,2,0:T(8,128)(2,1)}, u32[]{:S(2)}) copy-start(bf16[2,512,16,128]{3,1,2,0:T(8,128)(2,1)} %get-tuple-element.516) | copy-start | bytes 12582916 | tf_op jit(solution)/shard_map/while
  141.9 4.6 %slice-start = ((s8[8388608]{0:T(1024)(128)(4,1)}), s8[4194304]{0:T(1024)(128)(4,1)S(1)}, s32[]{:S(2)}) async-start(s8[8388608]{0:T(1024)(128)(4,1)} %bitcast.401), calls=%async_computation.4 | async-start | bytes 8388608 | tf_op jit(solution)/shard_map/while
  144.6 2.4 slice-start.1
  149.8 3.2 %copy-start.1 = (f32[2,512,16,128]{3,2,1,0:T(8,128)}, f32[2,512,16,128]{3,2,1,0:T(8,128)S(1)}, u32[]{:S(2)}) copy-start(f32[2,512,16,128]{3,2,1,0:T(8,128)S(1)} %copy_dynamic-update-slice_fusion.2) | copy-start | bytes 25165828 | tf_op jit(solution)/shard_map/while
Sparse Core Ops, SparseCore 0:
  10.2 55.3 all-gather.4
  163.9 91.6 reduce-scatter.1
where the time goes:
time: 265 us; the launch traced here: 264 us
  waiting for transfers between devices  109 us (41%)
  blocking collectives  61.1 us (23%)
  local copies, waits for them, and re-layouts  40.4 us (15%)
  matrix products  26.8 us (10%)
  between operations  14.3 us (5%)
  other arithmetic  11.8 us (4%)
    reduce_scatter x1, waiting for transfers between devices, body(): lax.psum_scatter(query_terms, CTX, scatter_dimension=0, tiled=True)  59.3 us
    all_gather x1, waiting for transfers between devices, sent_together(): out, at, outs = (lax.all_gather(both, axis, axis=dim, tiled=True), 0, [])  49.9 us
    all_to_all x1, blocking collectives, sent_and_summed(): lax.all_to_all(cut_along(shard, dim, count), axis, 0, 0, tiled=True)  30.7 us
    all_gather x3, blocking collectives, all_in_one(): both, at, found = (lax.all_gather(jnp.concatenate(lines), axis), 0, {})  30.4 us
    unnamed x12, local copies, waits for them, and re-layouts  25.6 us
    dot_general x4, matrix products, block_scores(): jnp.einsum('rhd,khd->hrk', query_block, keys_split, preferred_element_typ...  10.1 us
    dot_general x4, matrix products, weight_grads(): jnp.einsum('rhd,khd->hrk', grad_block, value_pieces, preferred_element_ty...  8.03 us
    while x32, local copies, waits for them, and re-layouts  7.69 us
  transfers between devices with their start and end apart: 2, of which 2 were waited for; matrix products, arithmetic and copies ran while one was open for 3% of the time, Pallas kernels for 0%

commit v1 on v0

v1 whole, which is shorter than its diff:
```python
import math

import jax
import jax.numpy as jnp
from jax import lax
from jax.experimental import pallas as pl
from jax.experimental.pallas import tpu as pltpu
from jax.sharding import Mesh
from jax.sharding import PartitionSpec as P

HEADS = 16
HEAD_DIM = 128
CAP = 32
TOK = 128
X, Z, C = "ctx_0", "ctx_1", "ctx_2"
CTX = (X, Z, C)
GROUPS = 4
CHUNK = 512
QG_ROWS = 72
FACTOR = 1.0 / math.sqrt(HEAD_DIM)
LOG2E = 1.4426950408889634
NEG_FILL = -1e30

NT = (((1,), (1,)), ((), ()))
TN = (((0,), (0,)), ((), ()))
NN = (((1,), (0,)), ((), ()))


def dot(a, b, dims):
    return lax.dot_general(a, b, dims, preferred_element_type=jnp.float32)


def folded(a, op):
    return op(a.reshape(-1, 8, a.shape[1]), axis=0)


def attention_kernel(qg, own, oth, dq, d_own, d_oth, s_buf, w_buf, a_own, a_oth):
    core = lax.axis_index(C)
    place = 2 * lax.axis_index(Z) + core
    sides = ((own, a_own, core), (oth, a_oth, 1 - core))
    rows = lax.broadcasted_iota(jnp.int32, (CHUNK, TOK), 0)
    spread = rows + rows // TOK * TOK
    for x in reversed(range(GROUPS)):
        q = jnp.concatenate([qg[4 * y + x, 0:CAP, :] for y in range(4)], axis=0)
        g = jnp.concatenate([qg[4 * y + x, CAP : 2 * CAP, :] for y in range(4)], axis=0)
        where = sum(qg[4 * y + x, 2 * CAP : 2 * CAP + 8, :].astype(jnp.float32) for y in range(4))
        slot_pos = where[0:1, :].astype(jnp.int32) + (8 * x + place) * TOK
        chunks = [(s, k) for k in range(x + 1) for s in range(2)]
        top = jnp.full((8, TOK), NEG_FILL, jnp.float32)
        for s, k in chunks:
            ref, _, part = sides[s]
            at = slice(k * CHUNK, (k + 1) * CHUNK)
            score = dot(ref[at, 0:HEAD_DIM], q, NT)
            if k == x:
                key_pos = spread + (2 * k * CHUNK + part * TOK)
                score = jnp.where(key_pos <= slot_pos, score, NEG_FILL)
            s_buf[s, at, :] = score
            top = jnp.maximum(top, folded(score, jnp.max))
        top = jnp.max(top, axis=0, keepdims=True)
        total = jnp.zeros((8, TOK), jnp.float32)
        weighted = jnp.zeros((8, TOK), jnp.float32)
        for s, k in chunks:
            ref = sides[s][0]
            at = slice(k * CHUNK, (k + 1) * CHUNK)
            e = jnp.exp2((s_buf[s, at, :] - top) * (FACTOR * LOG2E))
            dw = dot(ref[at, HEAD_DIM : 2 * HEAD_DIM], g, NT)
            s_buf[s, at, :] = e
            w_buf[s, at, :] = dw
            total = total + folded(e, jnp.sum)
            weighted = weighted + folded(e * dw, jnp.sum)
        scale = 1.0 / jnp.sum(total, axis=0, keepdims=True)
        delta = jnp.sum(weighted, axis=0, keepdims=True) * scale
        query_sum = jnp.zeros((TOK, HEAD_DIM), jnp.float32)
        for s, k in chunks:
            ref, acc, _ = sides[s]
            at = slice(k * CHUNK, (k + 1) * CHUNK)
            w = s_buf[s, at, :] * scale
            ds = (w * (w_buf[s, at, :] - delta)).astype(jnp.bfloat16)
            wb = w.astype(jnp.bfloat16)
            query_sum = query_sum + dot(ds, ref[at, 0:HEAD_DIM], TN)
            key_part = dot(ds, q, NN)
            value_part = dot(wb, g, NN)
            if x == GROUPS - 1:
                acc[at, 0:HEAD_DIM] = key_part
                acc[at, HEAD_DIM : 2 * HEAD_DIM] = value_part
            else:
                acc[at, 0:HEAD_DIM] += key_part
                acc[at, HEAD_DIM : 2 * HEAD_DIM] += value_part
        query_out = (query_sum * FACTOR).astype(jnp.bfloat16)
        for y in range(4):
            dq[4 * y + x, :, :] = query_out[CAP * y : CAP * (y + 1), :]
    d_own[:, 0:HEAD_DIM] = a_own[:, 0:HEAD_DIM] * FACTOR
    d_own[:, HEAD_DIM:] = a_own[:, HEAD_DIM:]
    d_oth[:, 0:HEAD_DIM] = (a_oth[:, 0:HEAD_DIM] * FACTOR).astype(jnp.bfloat16)
    d_oth[:, HEAD_DIM:] = a_oth[:, HEAD_DIM:].astype(jnp.bfloat16)


def attention(qg, own, oth):
    keys = own.shape[0]
    vmem = pl.BlockSpec(memory_space=pltpu.VMEM)
    return pl.pallas_call(
        attention_kernel,
        out_shape=(
            jax.ShapeDtypeStruct((16, CAP, HEAD_DIM), jnp.bfloat16),
            jax.ShapeDtypeStruct((keys, 2 * HEAD_DIM), jnp.float32),
            jax.ShapeDtypeStruct((keys, 2 * HEAD_DIM), jnp.bfloat16),
        ),
        in_specs=[vmem] * 3,
        out_specs=(vmem,) * 3,
        scratch_shapes=[
            pltpu.VMEM((2, keys, TOK), jnp.float32),
            pltpu.VMEM((2, keys, TOK), jnp.float32),
            pltpu.VMEM((keys, 2 * HEAD_DIM), jnp.float32),
            pltpu.VMEM((keys, 2 * HEAD_DIM), jnp.float32),
        ],
        compiler_params=pltpu.CompilerParams(vmem_limit_bytes=40 * 2**20),
        cost_estimate=pl.CostEstimate(
            flops=2 * 10 * 128 * 1024 * 128 * 5, bytes_accessed=6 * 2**20, transcendentals=10 * 128 * 1024
        ),
    )(qg, own, oth)


def swap_cores(a):
    return lax.ppermute(a, C, [(0, 1), (1, 0)])


def body(queries, grad_out, keys, values, surv_index, counts):
    depth, ctx = lax.axis_index("rec"), lax.axis_index(CTX)
    def own_heads(a):
        cols = lax.dynamic_slice_in_dim(a, depth * 4 * HEAD_DIM, 4 * HEAD_DIM, axis=1)
        return cols.reshape(TOK, 4, HEAD_DIM).transpose(1, 0, 2)

    kv = jnp.concatenate((own_heads(keys), own_heads(values)), axis=2)
    kv = jnp.broadcast_to(kv[:, None], (4, 4, TOK, 2 * HEAD_DIM)).reshape(16, TOK, 2 * HEAD_DIM)
    kv = lax.all_to_all(kv, (X, Z), 0, 0, tiled=True).reshape(16 * TOK, 2 * HEAD_DIM)
    kv_other = swap_cores(kv)
    live = jnp.arange(CAP) < lax.dynamic_index_in_dim(counts[0], ctx, keepdims=False)
    own_grad = jnp.where(live[:, None], grad_out[0], jnp.zeros_like(grad_out[0]))
    where = lax.dynamic_slice_in_dim(surv_index[0], ctx * CAP, CAP)
    where = jnp.where(jnp.arange(TOK) // CAP == depth, jnp.tile(where, 4), 0).astype(jnp.bfloat16)

    def by_head(a):
        return a.reshape(CAP, HEADS, HEAD_DIM).transpose(1, 0, 2)

    qg = jnp.concatenate(
        (by_head(queries[0]), by_head(own_grad), jnp.broadcast_to(where[None, None], (16, QG_ROWS - 2 * CAP, TOK))),
        axis=1,
    )
    qg = lax.all_to_all(qg, ("rec", X), 0, 0, tiled=True)
    dq, d_own, d_other = attention(qg, kv, kv_other)
    dq = lax.all_to_all(dq, ("rec", X), 0, 0, tiled=True)
    query_grad = dq.transpose(1, 0, 2).reshape(1, CAP, HEADS * HEAD_DIM)
    mine = swap_cores(d_other)
    sums = (d_own + mine.astype(jnp.float32)).astype(jnp.bfloat16)
    sums = lax.all_to_all(sums.reshape(16, TOK, 2 * HEAD_DIM), (X, Z), 0, 0, tiled=True)
    sums = jnp.sum(sums.reshape(4, 4, TOK, 2 * HEAD_DIM).astype(jnp.float32), axis=1).astype(jnp.bfloat16)
    key_grad = sums[:, :, :HEAD_DIM].transpose(1, 0, 2).reshape(TOK, 4 * HEAD_DIM)
    value_grad = sums[:, :, HEAD_DIM:].transpose(1, 0, 2).reshape(TOK, 4 * HEAD_DIM)
    return query_grad, key_grad, value_grad


def solution(mesh):
    split = Mesh(mesh.devices.reshape(mesh.shape["rec"], 4, 4, 2), ("rec", X, Z, C))
    return jax.shard_map(
        body,
        mesh=split,
        in_specs=(
            P("rec", CTX, None),
            P("rec", CTX, None),
            P(CTX, None),
            P(CTX, None),
            P("rec", None),
            P("rec", None),
        ),
        out_specs=(P("rec", CTX, None), P(CTX, "rec"), P(CTX, "rec")),
        check_vma=False,
    )
```

time: 265 us -> 89.2 us (0.34)
  waiting for transfers between devices: 109 us -> 41.4 us
  blocking collectives: 61.1 us -> 14.1 us
  local copies, waits for them, and re-layouts: 40.4 us -> 8.13 us
  matrix products: 26.8 us -> 0 us
  starting transfers between devices: 0.08 us -> 15.3 us
  between operations: 14.3 us -> 0.85 us
  other arithmetic: 11.8 us -> 2.19 us
  Pallas kernels: 0 us -> 6.74 us
    reduce_scatter x1 -> x0, waiting for transfers between devices: 59.3 us -> none  [body(): lax.psum_scatter(query_terms, CTX, scatter_dimension=0, tiled=True)]
    all_gather x1 -> x0, waiting for transfers between devices: 49.9 us -> none  [sent_together(): out, at, outs = (lax.all_gather(both, axis, axis=dim, tiled=True), 0, [])]
    all_to_all x0 -> x3, waiting for transfers between devices: none -> 41.4 us  [the longest x1 17.7 us: body(): lax.all_to_all(kv, (X, Z), 0, 0, tiled=True).reshape(16 * TOK, 2 * HEAD_DIM)]
    all_gather x3 -> x0, blocking collectives: 30.4 us -> none  [all_in_one(): both, at, found = (lax.all_gather(jnp.concatenate(lines), axis), 0, {})]
    dot_general x14 -> x0, matrix products: 26.8 us -> none  [the longest x4 10.1 us: block_scores(): jnp.einsum('rhd,khd->hrk', query_block, keys_split, preferred_element_typ...]
    unnamed x12 -> x17, local copies, waits for them, and re-layouts: 25.6 us -> 3.94 us
    all_to_all x1, blocking collectives: 30.7 us -> 14.1 us  [body(): qg = lax.all_to_all(qg, ('rec', X), 0, 0, tiled=True)]
    all_to_all x0 -> x3, starting transfers between devices: none -> 15.3 us  [the longest x1 7.99 us: body(): lax.all_to_all(kv, (X, Z), 0, 0, tiled=True).reshape(16 * TOK, 2 * HEAD_DIM)]
  transfers between devices with their start and end apart: 2 -> 5, of which waited for: 2 -> 3; matrix products, arithmetic and copies ran while one was open for 3% -> 4% of each run, Pallas kernels for 0% -> 0%
where the time goes in v1:
time: 89.2 us; the launch traced here: 88.8 us
  waiting for transfers between devices  41.4 us (46%)
  starting transfers between devices  15.3 us (17%)
  blocking collectives  14.1 us (16%)
  local copies, waits for them, and re-layouts  8.13 us (9%)
  Pallas kernels  6.74 us (8%)
  other arithmetic  2.19 us (2%)
    all_to_all x1, waiting for transfers between devices, body(): lax.all_to_all(kv, (X, Z), 0, 0, tiled=True).reshape(16 * TOK, 2 * HEAD_DIM)  17.7 us
    all_to_all x1, waiting for transfers between devices, body(): lax.all_to_all(sums.reshape(16, TOK, 2 * HEAD_DIM), (X, Z), 0, 0, tiled=T...  16.7 us
    all_to_all x1, blocking collectives, body(): qg = lax.all_to_all(qg, ('rec', X), 0, 0, tiled=True)  14.1 us
    all_to_all x1, starting transfers between devices, body(): lax.all_to_all(kv, (X, Z), 0, 0, tiled=True).reshape(16 * TOK, 2 * HEAD_DIM)  7.99 us
    all_to_all x1, waiting for transfers between devices, body(): dq = lax.all_to_all(dq, ('rec', X), 0, 0, tiled=True)  6.93 us
    pallas_call x1, Pallas kernels, attention(): pl.pallas_call(attention_kernel, out_shape=(jax.ShapeDtypeStruct((16, CAP...  6.74 us
    unnamed x17, local copies, waits for them, and re-layouts  3.94 us
    all_to_all x1, starting transfers between devices, body(): lax.all_to_all(sums.reshape(16, TOK, 2 * HEAD_DIM), (X, Z), 0, 0, tiled=T...  3.8 us
  transfers between devices with their start and end apart: 5, of which 3 were waited for; matrix products, arithmetic and copies ran while one was open for 4% of the time, Pallas kernels for 0%

profile of v1, /device:TPU:0, one launch (start us, length us, event | category | flops | bytes accessed | tf_op | source)
XLA Modules:
  0.0 88.8 jit_solution(5244214895840629171)
XLA Ops:
  0.6 0.0 copy-start
  0.7 1.0 %constant_dynamic-slice_fusion = (bf16[128,512]{1,0:T(8,128)(2,1)S(1)}, bf16[128,512]{1,0:T(8,128)(2,1)S(1)}) fusion(bf16[128,2048]{1,0:T(8,128)(2,1)} %param.9, s32[]{:T(128)S(6)} %select_n.38, bf16[128,2048]{1,0:T(8,128)(2,1)} %param.8), kind=kLoop, calls=%fused_computation.14 | loop fusion | bytes 524292 | tf_op jit(solution)/shard_map/dynamic_slice | solution.py:130
  1.6 0.1 copy.32
  1.8 0.1 copy.24
  1.9 0.0 copy-start.3
  1.9 0.0 copy-start.4
  2.0 0.1 copy.26
  2.1 0.0 copy-start.5
  2.1 1.1 %broadcast_in_dim.29 = bf16[4,4,128,256]{3,2,1,0:T(8,128)(2,1)} broadcast(bf16[4,128,256]{2,1,0:T(8,128)(2,1)S(1)} %copy.26), dimensions={0,2,3} | broadcast | bytes 1310720 | tf_op jit(solution)/shard_map/broadcast_in_dim | solution.py:134
  3.2 8.0 %all-to-all-start.1 = ((bf16[16,128,256]{2,1,0:T(8,128)(2,1)}), bf16[16,128,256]{2,1,0:T(8,128)(2,1)S(1)}, u32[]{:S(2)}, u32[]{:S(2)}) async-start(bf16[16,128,256]{2,1,0:T(8,128)(2,1)} %bitcast.8), calls=%async_computation.1 | async-start | bytes 2097152 | tf_op jit(solution)/shard_map/all_to_all | solution.py:135
  11.2 17.7 %all-to-all-done.1 = bf16[16,128,256]{2,1,0:T(8,128)(2,1)S(1)} async-done(((bf16[16,128,256]{2,1,0:T(8,128)(2,1)}), bf16[16,128,256]{2,1,0:T(8,128)(2,1)S(1)}, u32[]{:S(2)}, u32[]{:S(2)}) %all-to-all-start.1) | async-done | bytes 1048608 | tf_op jit(solution)/shard_map/all_to_all | solution.py:135
  29.0 0.1 fusion.1
  29.0 0.1 tile.13
  29.2 0.6 constant_dynamic-slice_fusion.3
  29.8 0.6 iota_compare_fusion
  30.5 0.1 fusion
  30.6 14.1 %all_to_all.20.qg = bf16[16,72,128]{2,1,0:T(8,128)(2,1)S(1)} all-to-all(bf16[16,72,128]{2,1,0:T(8,128)(2,1)S(1)} %pad_maximum_fusion), channel_id=1, replica_groups=mesh['rec'=4,'ctx_0'=4,'ctx_1'=4,'ctx_2'=2] {'rec','ctx_0'}, dimensions={0} | all-to-all | bytes 589824 | tf_op jit(solution)/shard_map/all_to_all | solution.py:149
  44.7 1.0 %copy-done.1 = bf16[2048,256]{1,0:T(8,128)(2,1)} copy-done((bf16[2048,256]{1,0:T(8,128)(2,1)}, bf16[2048,256]{1,0:T(8,128)(2,1)S(1)}, u32[]{:S(2)}) %copy-start.1) | copy-done | bytes 1048600
  45.7 1.2 %copy-done.2 = bf16[2048,256]{1,0:T(8,128)(2,1)S(1)} copy-done((bf16[2048,256]{1,0:T(8,128)(2,1)S(1)}, bf16[2048,256]{1,0:T(8,128)(2,1)}, u32[]{:S(2)}) %copy-start.2) | copy-done | bytes 1048600
  46.9 6.7 %shard_map.85 = (bf16[16,32,128]{2,1,0:T(8,128)(2,1)}, f32[2048,256]{1,0:T(8,128)S(1)}, bf16[2048,256]{1,0:T(8,128)(2,1)}) custom-call(bf16[16,72,128]{2,1,0:T(8,128)(2,1)S(1)} %all_to_all.20.qg, bf16[2048,256]{1,0:T(8,128)(2,1)S(1)} %bitcast.32, bf16[2048,256]{1,0:T(8,128)(2,1)S(1)} %copy-done.2), custom_call_target="tpu_custom_call" | custom-call | flops 1677721600 | bytes 6291456 | tf_op jit(solution)/shard_map/pallas_call | solution.py:101
  53.7 3.5 %all-to-all-start.2 = ((bf16[16,32,128]{2,1,0:T(8,128)(2,1)}), bf16[16,32,128]{2,1,0:T(8,128)(2,1)S(1)}, u32[]{:S(2)}, u32[]{:S(2)}) async-start(bf16[16,32,128]{2,1,0:T(8,128)(2,1)} %get-tuple-element.6), calls=%async_computation.2 | async-start | bytes 262144 | tf_op jit(solution)/shard_map/all_to_all | solution.py:151
  57.2 1.3 %add_convert_fusion = bf16[2048,256]{1,0:T(8,128)(2,1)} fusion(f32[2048,256]{1,0:T(8,128)S(1)} %get-tuple-element.7, bf16[2048,256]{1,0:T(8,128)(2,1)S(1)} %collective-permute-done.1), kind=kLoop, calls=%fused_computation | loop fusion | flops 1572864 | bytes 4194304 | tf_op jit(solution)/shard_map/convert_element_type | solution.py:154
  58.5 6.9 %all-to-all-done.2 = bf16[16,32,128]{2,1,0:T(8,128)(2,1)S(1)} async-done(((bf16[16,32,128]{2,1,0:T(8,128)(2,1)}), bf16[16,32,128]{2,1,0:T(8,128)(2,1)S(1)}, u32[]{:S(2)}, u32[]{:S(2)}) %all-to-all-start.2) | async-done | bytes 131104 | tf_op jit(solution)/shard_map/all_to_all | solution.py:151
  65.4 3.8 %all-to-all-start.3 = ((bf16[16,128,256]{2,1,0:T(8,128)(2,1)}), bf16[16,128,256]{2,1,0:T(8,128)(2,1)S(1)}, u32[]{:S(2)}, u32[]{:S(2)}) async-start(bf16[16,128,256]{2,1,0:T(8,128)(2,1)} %bitcast.11), calls=%async_computation.3 | async-start | bytes 2097152 | tf_op jit(solution)/shard_map/all_to_all | solution.py:155
  69.2 0.1 copy.27
  69.3 0.7 reshape.73
  70.0 16.7 %all-to-all-done.3 = bf16[16,128,256]{2,1,0:T(8,128)(2,1)S(1)} async-done(((bf16[16,128,256]{2,1,0:T(8,128)(2,1)}), bf16[16,128,256]{2,1,0:T(8,128)(2,1)S(1)}, u32[]{:S(2)}, u32[]{:S(2)}) %all-to-all-start.3) | async-done | bytes 1048608 | tf_op jit(solution)/shard_map/all_to_all | solution.py:155
  86.7 0.1 bitcast_reduce_fusion
  86.9 0.1 copy.29
  87.1 0.8 copy.31
  87.9 0.1 copy.28
  88.0 0.8 copy.30
  (18 shorter events, 0.2 us)
Async XLA Ops:
  0.6 28.3 %copy-start = (s32[1,1024]{1,0:T(1,128)S(1)}, s32[1,1024]{1,0:T(1,128)}, u32[]{:S(2)}) copy-start(s32[1,1024]{1,0:T(1,128)} %param.10) | copy-start | bytes 12292
  1.9 27.2 %copy-start.3 = (bf16[1,32,2048]{2,1,0:T(8,128)(2,1)S(1)}, bf16[1,32,2048]{2,1,0:T(8,128)(2,1)}, u32[]{:S(2)}) copy-start(bf16[1,32,2048]{2,1,0:T(8,128)(2,1)} %param.6) | copy-start | bytes 393220
  1.9 27.2 %copy-start.4 = (bf16[1,32,2048]{2,1,0:T(8,128)(2,1)S(1)}, bf16[1,32,2048]{2,1,0:T(8,128)(2,1)}, u32[]{:S(2)}) copy-start(bf16[1,32,2048]{2,1,0:T(8,128)(2,1)} %param.7) | copy-start | bytes 393220
  2.1 27.1 %copy-start.5 = (s32[1,32]{1,0:T(1,128)S(1)}, s32[1,32]{1,0:T(1,128)}, u32[]{:S(2)}) copy-start(s32[1,32]{1,0:T(1,128)} %param.11) | copy-start | bytes 388
  3.2 25.7 %all-to-all-start.1 = ((bf16[16,128,256]{2,1,0:T(8,128)(2,1)}), bf16[16,128,256]{2,1,0:T(8,128)(2,1)S(1)}, u32[]{:S(2)}, u32[]{:S(2)}) async-start(bf16[16,128,256]{2,1,0:T(8,128)(2,1)} %bitcast.8), calls=%async_computation.1 | async-start | bytes 2097152 | tf_op jit(solution)/shard_map/all_to_all | solution.py:135
  29.0 15.8 %collective-permute-start = (bf16[2048,256]{1,0:T(8,128)(2,1)S(1)}, bf16[2048,256]{1,0:T(8,128)(2,1)S(1)}, u32[]{:S(2)}, u32[]{:S(2)}) collective-permute-start(bf16[2048,256]{1,0:T(8,128)(2,1)S(1)} %bitcast.31), channel_id=1, source_target_pairs={{0,1},{1,0},{2,3},{3,2},{4,5},{5,4},{6,7},{7,6},{8,9},{9,8},{10,11... | collective-permute-start | bytes 3145736 | tf_op jit(solution)/shard_map/ppermute | solution.py:124
  44.7 1.0 %copy-start.1 = (bf16[2048,256]{1,0:T(8,128)(2,1)}, bf16[2048,256]{1,0:T(8,128)(2,1)S(1)}, u32[]{:S(2)}) copy-start(bf16[2048,256]{1,0:T(8,128)(2,1)S(1)} %collective-permute-done.oth) | copy-start | bytes 3145732
  45.7 1.2 %copy-start.2 = (bf16[2048,256]{1,0:T(8,128)(2,1)S(1)}, bf16[2048,256]{1,0:T(8,128)(2,1)}, u32[]{:S(2)}) copy-start(bf16[2048,256]{1,0:T(8,128)(2,1)} %copy-done.1) | copy-start | bytes 3145732
  53.7 3.5 %collective-permute-start.1 = (bf16[2048,256]{1,0:T(8,128)(2,1)}, bf16[2048,256]{1,0:T(8,128)(2,1)S(1)}, u32[]{:S(2)}, u32[]{:S(2)}) collective-permute-start(bf16[2048,256]{1,0:T(8,128)(2,1)} %get-tuple-element.8), channel_id=1, source_target_pairs={{0,1},{1,0},{2,3},{3,2},{4,5},{5,4},{6,7},{7,6},{8,9},{9,8},{10,11... | collective-permute-start | bytes 3145736 | tf_op jit(solution)/shard_map/ppermute | solution.py:124
  53.7 11.7 %all-to-all-start.2 = ((bf16[16,32,128]{2,1,0:T(8,128)(2,1)}), bf16[16,32,128]{2,1,0:T(8,128)(2,1)S(1)}, u32[]{:S(2)}, u32[]{:S(2)}) async-start(bf16[16,32,128]{2,1,0:T(8,128)(2,1)} %get-tuple-element.6), calls=%async_computation.2 | async-start | bytes 262144 | tf_op jit(solution)/shard_map/all_to_all | solution.py:151
  65.4 21.3 %all-to-all-start.3 = ((bf16[16,128,256]{2,1,0:T(8,128)(2,1)}), bf16[16,128,256]{2,1,0:T(8,128)(2,1)S(1)}, u32[]{:S(2)}, u32[]{:S(2)}) async-start(bf16[16,128,256]{2,1,0:T(8,128)(2,1)} %bitcast.11), calls=%async_computation.3 | async-start | bytes 2097152 | tf_op jit(solution)/shard_map/all_to_all | solution.py:155

commit v2 on v1

--- a/solution.py
+++ b/solution.py
@@ -34,16 +34,23 @@
     return op(a.reshape(-1, 8, a.shape[1]), axis=0)
 
 
-def attention_kernel(qg, own, oth, dq, d_own, d_oth, s_buf, w_buf, a_own, a_oth):
+def attention_kernel(*refs):
+    q_in, (own, oth) = refs[0:4], refs[4:6]
+    q_out, (d_own, d_oth) = refs[6:10], refs[10:12]
+    qg, dq, s_buf, w_buf, a_own, a_oth = refs[12:]
     core = lax.axis_index(C)
+    here = lax.axis_index(X)
     place = 2 * lax.axis_index(Z) + core
     sides = ((own, a_own, core), (oth, a_oth, 1 - core))
+    for p in range(4):
+        qg[p] = q_in[p][...]
     rows = lax.broadcasted_iota(jnp.int32, (CHUNK, TOK), 0)
     spread = rows + rows // TOK * TOK
     for x in reversed(range(GROUPS)):
-        q = jnp.concatenate([qg[4 * y + x, 0:CAP, :] for y in range(4)], axis=0)
-        g = jnp.concatenate([qg[4 * y + x, CAP : 2 * CAP, :] for y in range(4)], axis=0)
-        where = sum(qg[4 * y + x, 2 * CAP : 2 * CAP + 8, :].astype(jnp.float32) for y in range(4))
+        from_x = lax.rem(here - x + 4, 4)
+        q = jnp.concatenate([qg[from_x, o, 0:CAP, :] for o in range(4)], axis=0)
+        g = jnp.concatenate([qg[from_x, o, CAP : 2 * CAP, :] for o in range(4)], axis=0)
+        where = sum(qg[from_x, o, 2 * CAP : 2 * CAP + 8, :].astype(jnp.float32) for o in range(4))
         slot_pos = where[0:1, :].astype(jnp.int32) + (8 * x + place) * TOK
         chunks = [(s, k) for k in range(x + 1) for s in range(2)]
         top = jnp.full((8, TOK), NEG_FILL, jnp.float32)
@@ -86,9 +93,9 @@
             else:
                 acc[at, 0:HEAD_DIM] += key_part
                 acc[at, HEAD_DIM : 2 * HEAD_DIM] += value_part
-        query_out = (query_sum * FACTOR).astype(jnp.bfloat16)
-        for y in range(4):
-            dq[4 * y + x, :, :] = query_out[CAP * y : CAP * (y + 1), :]
+        dq[from_x] = (query_sum * FACTOR).astype(jnp.bfloat16).reshape(4, CAP, HEAD_DIM)
+    for p in range(4):
+        q_out[p][...] = dq[p]
     d_own[:, 0:HEAD_DIM] = a_own[:, 0:HEAD_DIM] * FACTOR
     d_own[:, HEAD_DIM:] = a_own[:, HEAD_DIM:]
     d_oth[:, 0:HEAD_DIM] = (a_oth[:, 0:HEAD_DIM] * FACTOR).astype(jnp.bfloat16)
@@ -98,16 +105,18 @@
 def attention(qg, own, oth):
     keys = own.shape[0]
     vmem = pl.BlockSpec(memory_space=pltpu.VMEM)
-    return pl.pallas_call(
+    out = pl.pallas_call(
         attention_kernel,
-        out_shape=(
-            jax.ShapeDtypeStruct((16, CAP, HEAD_DIM), jnp.bfloat16),
+        out_shape=(jax.ShapeDtypeStruct((4, CAP, HEAD_DIM), jnp.bfloat16),) * 4
+        + (
             jax.ShapeDtypeStruct((keys, 2 * HEAD_DIM), jnp.float32),
             jax.ShapeDtypeStruct((keys, 2 * HEAD_DIM), jnp.bfloat16),
         ),
-        in_specs=[vmem] * 3,
-        out_specs=(vmem,) * 3,
+        in_specs=[vmem] * 6,
+        out_specs=(vmem,) * 6,
         scratch_shapes=[
+            pltpu.VMEM((4, 4, QG_ROWS, HEAD_DIM), jnp.bfloat16),
+            pltpu.VMEM((4, 4, CAP, HEAD_DIM), jnp.bfloat16),
             pltpu.VMEM((2, keys, TOK), jnp.float32),
             pltpu.VMEM((2, keys, TOK), jnp.float32),
             pltpu.VMEM((keys, 2 * HEAD_DIM), jnp.float32),
@@ -117,52 +126,143 @@
         cost_estimate=pl.CostEstimate(
             flops=2 * 10 * 128 * 1024 * 128 * 5, bytes_accessed=6 * 2**20, transcendentals=10 * 128 * 1024
         ),
-    )(qg, own, oth)
+    )(*qg, own, oth)
+    return out[0:4], out[4], out[5]
+
+
+def pack_kernel(keys, values, queries, grad_out, surv_index, counts, kv, *rest):
+    qg, (k_buf, v_buf, q_buf, g_buf, s_buf, c_buf, sems) = rest[0:4], rest[4:]
+    depth = lax.axis_index("rec")
+    ctx = lax.axis_index(X) * 8 + lax.axis_index(Z) * 2 + lax.axis_index(C)
+    mine = pl.ds(pl.multiple_of(depth * 4 * HEAD_DIM, 4 * HEAD_DIM), 4 * HEAD_DIM)
+    copies = [
+        pltpu.make_async_copy(src, dst, sems.at[n])
+        for n, (src, dst) in enumerate(
+            (
+                (keys.at[:, mine], k_buf),
+                (values.at[:, mine], v_buf),
+                (queries.at[0], q_buf),
+                (grad_out.at[0], g_buf),
+                (surv_index, s_buf),
+                (counts, c_buf),
+            )
+        )
+    ]
+    for copy in copies:
+        copy.start()
+    copies[0].wait()
+    copies[1].wait()
+    for x in range(4):
+        cols = slice(x * HEAD_DIM, (x + 1) * HEAD_DIM)
+        for z in range(4):
+            kv[4 * x + z, :, 0:HEAD_DIM] = k_buf[:, cols]
+            kv[4 * x + z, :, HEAD_DIM:] = v_buf[:, cols]
+    for copy in copies[2:]:
+        copy.wait()
+    live = lax.broadcasted_iota(jnp.int32, (CAP, HEAD_DIM), 0) < c_buf[0, ctx]
+    quarter = lax.rem(ctx, 4)
+    near = s_buf[0:1, pl.ds(pl.multiple_of(ctx // 4 * TOK, TOK), TOK)]
+    lane_group = lax.broadcasted_iota(jnp.int32, (8, TOK), 1) // CAP
+    for o in range(4):
+        where = pltpu.roll(jnp.broadcast_to(near, (8, TOK)), lax.rem(o - quarter + 4, 4) * CAP, 1)
+        where = jnp.where(lane_group == o, where, 0).astype(jnp.float32).astype(jnp.bfloat16)
+        for x in range(4):
+            head = lax.rem(depth + o, 4) * 4 + x
+            cols = pl.ds(pl.multiple_of(head * HEAD_DIM, HEAD_DIM), HEAD_DIM)
+            qg[o][x, 0:CAP, :] = q_buf[:, cols]
+            grad = jnp.where(live, g_buf[:, cols].astype(jnp.float32), 0.0)
+            qg[o][x, CAP : 2 * CAP, :] = grad.astype(jnp.bfloat16)
+            qg[o][x, 2 * CAP :, :] = where
+
+
+def pack(keys, values, queries, grad_out, surv_index, counts):
+    vmem = pl.BlockSpec(memory_space=pltpu.VMEM)
+    hbm = pl.BlockSpec(memory_space=pltpu.HBM)
+    out = pl.pallas_call(
+        pack_kernel,
+        out_shape=(jax.ShapeDtypeStruct((16, TOK, 2 * HEAD_DIM), jnp.bfloat16),)
+        + (jax.ShapeDtypeStruct((4, QG_ROWS, HEAD_DIM), jnp.bfloat16),) * 4,
+        in_specs=[hbm] * 6,
+        out_specs=(vmem,) * 5,
+        scratch_shapes=[
+            pltpu.VMEM((TOK, 4 * HEAD_DIM), jnp.bfloat16),
+            pltpu.VMEM((TOK, 4 * HEAD_DIM), jnp.bfloat16),
+            pltpu.VMEM((CAP, HEADS * HEAD_DIM), jnp.bfloat16),
+            pltpu.VMEM((CAP, HEADS * HEAD_DIM), jnp.bfloat16),
+            pltpu.VMEM(surv_index.shape, jnp.int32),
+            pltpu.SMEM(counts.shape, jnp.int32),
+            pltpu.SemaphoreType.DMA((6,)),
+        ],
+        compiler_params=pltpu.CompilerParams(vmem_limit_bytes=8 * 2**20),
+    )(*(pltpu.with_memory_space_constraint(a, pltpu.HBM) for a in (keys, values, queries, grad_out, surv_index, counts)))
+    return out[0], out[1:]
+
+
+def unpack_kernel(parts, key_grad, value_grad, k_buf, v_buf, sems):
+    sides = ((k_buf, key_grad, 0), (v_buf, value_grad, HEAD_DIM))
+    copies = []
+    for n, (buf, out, at) in enumerate(sides):
+        for x in range(4):
+            total = sum(parts[4 * x + z, :, at : at + HEAD_DIM].astype(jnp.float32) for z in range(4))
+            buf[:, x * HEAD_DIM : (x + 1) * HEAD_DIM] = total.astype(jnp.bfloat16)
+        copies.append(pltpu.make_async_copy(buf, out, sems.at[n]))
+        copies[n].start()
+    for copy in copies:
+        copy.wait()
+
+
+def unpack(parts):
+    out = jax.ShapeDtypeStruct((TOK, 4 * HEAD_DIM), jnp.bfloat16)
+    return pl.pallas_call(
+        unpack_kernel,
+        out_shape=(out, out),
+        in_specs=[pl.BlockSpec(memory_space=pltpu.VMEM)],
+        out_specs=(pl.BlockSpec(memory_space=pl.ANY),) * 2,
+        scratch_shapes=[
+            pltpu.VMEM((TOK, 4 * HEAD_DIM), jnp.bfloat16),
+            pltpu.VMEM((TOK, 4 * HEAD_DIM), jnp.bfloat16),
+            pltpu.SemaphoreType.DMA((2,)),
+        ],
+        compiler_params=pltpu.CompilerParams(vmem_limit_bytes=8 * 2**20),
+    )(parts)
+
+
+def moved(a, axis, by):
+    return a if by % 4 == 0 else lax.ppermute(a, axis, [(i, (i + by) % 4) for i in range(4)])
 
 
 def swap_cores(a):
     return lax.ppermute(a, C, [(0, 1), (1, 0)])
 
 
-def body(queries, grad_out, keys, values, surv_index, counts):
-    depth, ctx = lax.axis_index("rec"), lax.axis_index(CTX)
-    def own_heads(a):
-        cols = lax.dynamic_slice_in_dim(a, depth * 4 * HEAD_DIM, 4 * HEAD_DIM, axis=1)
-        return cols.reshape(TOK, 4, HEAD_DIM).transpose(1, 0, 2)
-
-    kv = jnp.concatenate((own_heads(keys), own_heads(values)), axis=2)
-    kv = jnp.broadcast_to(kv[:, None], (4, 4, TOK, 2 * HEAD_DIM)).reshape(16, TOK, 2 * HEAD_DIM)
+def gradients(queries, grad_out, keys, values, surv_index, counts):
+    depth, here = lax.axis_index("rec"), lax.axis_index(X)
+    kv, by_depth = pack(keys, values, queries, grad_out, surv_index, counts)
     kv = lax.all_to_all(kv, (X, Z), 0, 0, tiled=True).reshape(16 * TOK, 2 * HEAD_DIM)
     kv_other = swap_cores(kv)
-    live = jnp.arange(CAP) < lax.dynamic_index_in_dim(counts[0], ctx, keepdims=False)
-    own_grad = jnp.where(live[:, None], grad_out[0], jnp.zeros_like(grad_out[0]))
-    where = lax.dynamic_slice_in_dim(surv_index[0], ctx * CAP, CAP)
-    where = jnp.where(jnp.arange(TOK) // CAP == depth, jnp.tile(where, 4), 0).astype(jnp.bfloat16)
-
-    def by_head(a):
-        return a.reshape(CAP, HEADS, HEAD_DIM).transpose(1, 0, 2)
-
-    qg = jnp.concatenate(
-        (by_head(queries[0]), by_head(own_grad), jnp.broadcast_to(where[None, None], (16, QG_ROWS - 2 * CAP, TOK))),
-        axis=1,
-    )
-    qg = lax.all_to_all(qg, ("rec", X), 0, 0, tiled=True)
+    by_depth = [moved(by_depth[o], "rec", o) for o in range(4)]
+
+    def for_x(p):
+        at = lax.rem(here + p, 4)
+        return jnp.concatenate([lax.dynamic_slice_in_dim(a, at, 1, axis=0) for a in by_depth], axis=0)
+
+    qg = [moved(for_x(p), X, p) for p in range(4)]
     dq, d_own, d_other = attention(qg, kv, kv_other)
-    dq = lax.all_to_all(dq, ("rec", X), 0, 0, tiled=True)
-    query_grad = dq.transpose(1, 0, 2).reshape(1, CAP, HEADS * HEAD_DIM)
     mine = swap_cores(d_other)
     sums = (d_own + mine.astype(jnp.float32)).astype(jnp.bfloat16)
     sums = lax.all_to_all(sums.reshape(16, TOK, 2 * HEAD_DIM), (X, Z), 0, 0, tiled=True)
-    sums = jnp.sum(sums.reshape(4, 4, TOK, 2 * HEAD_DIM).astype(jnp.float32), axis=1).astype(jnp.bfloat16)
-    key_grad = sums[:, :, :HEAD_DIM].transpose(1, 0, 2).reshape(TOK, 4 * HEAD_DIM)
-    value_grad = sums[:, :, HEAD_DIM:].transpose(1, 0, 2).reshape(TOK, 4 * HEAD_DIM)
+    dq = [moved(dq[p], X, -p) for p in range(4)]
+    dq = [moved(jnp.stack([dq[p][o] for p in range(4)]), "rec", -o) for o in range(4)]
+    dq = jnp.roll(jnp.stack(dq), (depth, here), (0, 1))
+    query_grad = dq.reshape(HEADS, CAP, HEAD_DIM).transpose(1, 0, 2).reshape(1, CAP, HEADS * HEAD_DIM)
+    key_grad, value_grad = unpack(sums)
     return query_grad, key_grad, value_grad
 
 
 def solution(mesh):
     split = Mesh(mesh.devices.reshape(mesh.shape["rec"], 4, 4, 2), ("rec", X, Z, C))
     return jax.shard_map(
-        body,
+        gradients,
         mesh=split,
         in_specs=(
             P("rec", CTX, None),

time: 89.2 us -> 84.8 us (0.951)
  waiting for transfers between devices: 41.4 us -> 27.7 us
  blocking collectives: 14.1 us -> 24.6 us
  local copies, waits for them, and re-layouts: 8.13 us -> 0.88 us
  starting transfers between devices: 15.3 us -> 21.3 us
  Pallas kernels: 6.74 us -> 7.89 us
    all_to_all x3 -> x1, waiting for transfers between devices: 41.4 us -> 12.1 us  [gradients(): lax.all_to_all(sums.reshape(16, TOK, 2 * HEAD_DIM), (X, Z), 0, 0, tiled=T...]
    ppermute x0 -> x12, starting transfers between devices: none -> 17.5 us  [moved(): lax.ppermute(a, axis, [(i, (i + by) % 4) for i in range(4)])]
    ppermute x0 -> x12, waiting for transfers between devices: none -> 15.6 us  [moved(): lax.ppermute(a, axis, [(i, (i + by) % 4) for i in range(4)])]
    all_to_all x3 -> x1, starting transfers between devices: 15.3 us -> 3.88 us  [gradients(): lax.all_to_all(sums.reshape(16, TOK, 2 * HEAD_DIM), (X, Z), 0, 0, tiled=T...]
    all_to_all x1, blocking collectives: 14.1 us -> 24.6 us  [gradients(): lax.all_to_all(kv, (X, Z), 0, 0, tiled=True).reshape(16 * TOK, 2 * HEAD_DIM)]
    unnamed x17 -> x5, local copies, waits for them, and re-layouts: 3.94 us -> 0.05 us
    dynamic_slice x3 -> x5, local copies, waits for them, and re-layouts: 1.71 us -> 0.04 us  [the longest x4 0.03 us: for_x(): lax.dynamic_slice_in_dim(a, at, 1, axis=0)]
    pallas_call x1 -> x3, Pallas kernels: 6.74 us -> 7.89 us  [the longest x1 5.8 us: attention(): pl.pallas_call(attention_kernel, out_shape=(jax.ShapeDtypeStruct((4, CAP,...]
  transfers between devices with their start and end apart: 5 -> 15, of which waited for: 3 -> 12; matrix products, arithmetic and copies ran while one was open for 4% -> 1% of each run, Pallas kernels for 0% -> 0%
where the time goes in v2:
time: 84.8 us; the launch traced here: 84.6 us
  waiting for transfers between devices  27.7 us (33%)
  blocking collectives  24.6 us (29%)
  starting transfers between devices  21.3 us (25%)
  Pallas kernels  7.89 us (9%)
  other arithmetic  1.42 us (2%)
  local copies, waits for them, and re-layouts  0.88 us (1%)
    all_to_all x1, blocking collectives, gradients(): lax.all_to_all(kv, (X, Z), 0, 0, tiled=True).reshape(16 * TOK, 2 * HEAD_DIM)  24.6 us
    ppermute x12, starting transfers between devices, moved(): lax.ppermute(a, axis, [(i, (i + by) % 4) for i in range(4)])  17.5 us
    ppermute x12, waiting for transfers between devices, moved(): lax.ppermute(a, axis, [(i, (i + by) % 4) for i in range(4)])  15.6 us
    all_to_all x1, waiting for transfers between devices, gradients(): lax.all_to_all(sums.reshape(16, TOK, 2 * HEAD_DIM), (X, Z), 0, 0, tiled=T...  12.1 us
    pallas_call x1, Pallas kernels, attention(): pl.pallas_call(attention_kernel, out_shape=(jax.ShapeDtypeStruct((4, CAP,...  5.8 us
    all_to_all x1, starting transfers between devices, gradients(): lax.all_to_all(sums.reshape(16, TOK, 2 * HEAD_DIM), (X, Z), 0, 0, tiled=T...  3.88 us
  transfers between devices with their start and end apart: 15, of which 12 were waited for; matrix products, arithmetic and copies ran while one was open for 1% of the time, Pallas kernels for 0%

profile of v2, /device:TPU:0, one launch (start us, length us, event | category | flops | bytes accessed | tf_op | source)
XLA Modules:
  0.0 84.6 jit_solution(9955569483970303896)
XLA Ops:
  0.6 1.3 %shard_map.85 = (bf16[16,128,256]{2,1,0:T(8,128)(2,1)S(1)}, bf16[4,72,128]{2,1,0:T(8,128)(2,1)S(1)}, bf16[4,72,128]{2,1,0:T(8,128)(2,1)S(1)}, bf16[4,72,128]{2,1,0:T(8,128)(2,1)S(1)}, bf16[4,72,128]{2,1,0:T(8,128)(2,1)S(1)}) custom-call(bf16[128,2048]{1,0:T(8,128)(2,1)} %keys.1, bf16[128,2048]{1,0:T(8,128)(2,1)} %values.1, bf16[1,32,2048]{2,1,0:T(8,128)(2,1)} %queries.1, ...), custom_call_target="tpu_custom_call" | custom-call | tf_op jit(solution)/shard_map/pallas_call | solution.py:181
  1.9 24.6 %all_to_all.10 = bf16[16,128,256]{2,1,0:T(8,128)(2,1)S(1)} all-to-all(bf16[16,128,256]{2,1,0:T(8,128)(2,1)S(1)} %get-tuple-element.20), channel_id=1, replica_groups=mesh['rec'=4,'ctx_0'=4,'ctx_1'=4,'ctx_2'=2] {'ctx_0','ctx_1'}, dimensions={0} | all-to-all | bytes 2097152 | tf_op jit(solution)/shard_map/all_to_all | solution.py:241
  26.6 1.6 %collective-permute-start = (bf16[4,72,128]{2,1,0:T(8,128)(2,1)S(1)}, bf16[4,72,128]{2,1,0:T(8,128)(2,1)S(1)}, u32[]{:S(2)}, u32[]{:S(2)}) collective-permute-start(bf16[4,72,128]{2,1,0:T(8,128)(2,1)S(1)} %get-tuple-element.17), channel_id=1, source_target_pairs={{0,32},{32,64},{64,96},{96,0},{1,33},{33,65},{65,97},{97,1},{2,34}... | collective-permute-start | bytes 221192 | tf_op jit(solution)/shard_map/ppermute | solution.py:231
  28.1 2.9 %collective-permute-start.1 = (bf16[4,72,128]{2,1,0:T(8,128)(2,1)S(1)}, bf16[4,72,128]{2,1,0:T(8,128)(2,1)S(1)}, u32[]{:S(2)}, u32[]{:S(2)}) collective-permute-start(bf16[4,72,128]{2,1,0:T(8,128)(2,1)S(1)} %get-tuple-element.18), channel_id=1, source_target_pairs={{0,64},{32,96},{64,0},{96,32},{1,65},{33,97},{65,1},{97,33},{2,66}... | collective-permute-start | bytes 221192 | tf_op jit(solution)/shard_map/ppermute | solution.py:231
  31.0 1.3 %collective-permute-start.2 = (bf16[4,72,128]{2,1,0:T(8,128)(2,1)S(1)}, bf16[4,72,128]{2,1,0:T(8,128)(2,1)S(1)}, u32[]{:S(2)}, u32[]{:S(2)}) collective-permute-start(bf16[4,72,128]{2,1,0:T(8,128)(2,1)S(1)} %get-tuple-element.19), channel_id=1, source_target_pairs={{0,96},{32,0},{64,32},{96,64},{1,97},{33,1},{65,33},{97,65},{2,98}... | collective-permute-start | bytes 221192 | tf_op jit(solution)/shard_map/ppermute | solution.py:231
  32.4 0.1 collective-permute-done
  32.5 2.8 %collective-permute-done.1 = bf16[4,72,128]{2,1,0:T(8,128)(2,1)S(1)} collective-permute-done((bf16[4,72,128]{2,1,0:T(8,128)(2,1)S(1)}, bf16[4,72,128]{2,1,0:T(8,128)(2,1)S(1)}, u32[]{:S(2)}, u32[]{:S(2)}) %collective-permute-start.1) | collective-permute-done | bytes 73760 | tf_op jit(solution)/shard_map/ppermute | solution.py:231
  35.3 0.1 collective-permute-done.2
  35.4 0.2 collective-permute-start.3
  35.6 2.9 %collective-permute-start.4 = (bf16[4,72,128]{2,1,0:T(8,128)(2,1)S(1)}, bf16[4,72,128]{2,1,0:T(8,128)(2,1)S(1)}, u32[]{:S(2)}, u32[]{:S(2)}) collective-permute-start(bf16[4,72,128]{2,1,0:T(8,128)(2,1)S(1)} %pad_maximum_fusion.2), channel_id=1, source_target_pairs={{0,16},{8,24},{16,0},{24,8},{1,17},{9,25},{17,1},{25,9},{2,18},{10... | collective-permute-start | bytes 221192 | tf_op jit(solution)/shard_map/ppermute | solution.py:231
  38.5 1.1 %collective-permute-start.5 = (bf16[4,72,128]{2,1,0:T(8,128)(2,1)S(1)}, bf16[4,72,128]{2,1,0:T(8,128)(2,1)S(1)}, u32[]{:S(2)}, u32[]{:S(2)}) collective-permute-start(bf16[4,72,128]{2,1,0:T(8,128)(2,1)S(1)} %pad_maximum_fusion.3), channel_id=1, source_target_pairs={{0,24},{8,0},{16,8},{24,16},{1,25},{9,1},{17,9},{25,17},{2,26},{10... | collective-permute-start | bytes 221192 | tf_op jit(solution)/shard_map/ppermute | solution.py:231
  39.6 2.4 %collective-permute-done.3.refs_1_ = bf16[4,72,128]{2,1,0:T(8,128)(2,1)S(1)} collective-permute-done((bf16[4,72,128]{2,1,0:T(8,128)(2,1)S(1)}, bf16[4,72,128]{2,1,0:T(8,128)(2,1)S(1)}, u32[]{:S(2)}, u32[]{:S(2)}) %collective-permute-start.3) | collective-permute-done | bytes 73760 | tf_op jit(solution)/shard_map/ppermute | solution.py:231
  42.0 0.9 %collective-permute-done.5.refs_3_ = bf16[4,72,128]{2,1,0:T(8,128)(2,1)S(1)} collective-permute-done((bf16[4,72,128]{2,1,0:T(8,128)(2,1)S(1)}, bf16[4,72,128]{2,1,0:T(8,128)(2,1)S(1)}, u32[]{:S(2)}, u32[]{:S(2)}) %collective-permute-start.5) | collective-permute-done | bytes 73760 | tf_op jit(solution)/shard_map/ppermute | solution.py:231
  42.9 5.8 %shard_map.86 = (bf16[4,32,128]{2,1,0:T(8,128)(2,1)S(1)}, bf16[4,32,128]{2,1,0:T(8,128)(2,1)S(1)}, bf16[4,32,128]{2,1,0:T(8,128)(2,1)S(1)}, bf16[4,32,128]{2,1,0...) custom-call(bf16[4,72,128]{2,1,0:T(8,128)(2,1)S(1)} %pad_maximum_fusion.refs_0_, ...), custom_call_target="tpu_custom_call" | custom-call | flops 1677721600 | bytes 6291456 | tf_op jit(solution)/shard_map/pallas_call | solution.py:108
  48.8 2.6 %collective-permute-start.7 = (bf16[4,32,128]{2,1,0:T(8,128)(2,1)S(1)}, bf16[4,32,128]{2,1,0:T(8,128)(2,1)S(1)}, u32[]{:S(2)}, u32[]{:S(2)}) collective-permute-start(bf16[4,32,128]{2,1,0:T(8,128)(2,1)S(1)} %get-tuple-element.22), channel_id=1, source_target_pairs={{0,24},{8,0},{16,8},{24,16},{1,25},{9,1},{17,9},{25,17},{2,26},{10... | collective-permute-start | bytes 98312 | tf_op jit(solution)/shard_map/ppermute | solution.py:231
  51.3 0.7 collective-permute-start.8
  52.1 0.2 collective-permute-start.9
  52.3 0.6 collective-permute-done.7
  52.9 3.8 %collective-permute-done.8 = bf16[4,32,128]{2,1,0:T(8,128)(2,1)S(1)} collective-permute-done((bf16[4,32,128]{2,1,0:T(8,128)(2,1)S(1)}, bf16[4,32,128]{2,1,0:T(8,128)(2,1)S(1)}, u32[]{:S(2)}, u32[]{:S(2)}) %collective-permute-start.8) | collective-permute-done | bytes 32800 | tf_op jit(solution)/shard_map/ppermute | solution.py:231
  56.8 0.4 collective-permute-done.9
  57.2 2.6 %collective-permute-start.10 = (bf16[4,32,128]{2,1,0:T(8,128)(2,1)S(1)}, bf16[4,32,128]{2,1,0:T(8,128)(2,1)S(1)}, u32[]{:S(2)}, u32[]{:S(2)}) collective-permute-start(bf16[4,32,128]{2,1,0:T(8,128)(2,1)S(1)} %pad_maximum_fusion.4), channel_id=1, source_target_pairs={{0,96},{32,0},{64,32},{96,64},{1,97},{33,1},{65,33},{97,65},{2,98}... | collective-permute-start | bytes 98312 | tf_op jit(solution)/shard_map/ppermute | solution.py:231
  59.8 0.5 collective-permute-start.11
  60.4 0.7 collective-permute-start.12
  61.1 0.3 collective-permute-done.10
  61.4 3.8 %collective-permute-done.11 = bf16[4,32,128]{2,1,0:T(8,128)(2,1)S(1)} collective-permute-done((bf16[4,32,128]{2,1,0:T(8,128)(2,1)S(1)}, bf16[4,32,128]{2,1,0:T(8,128)(2,1)S(1)}, u32[]{:S(2)}, u32[]{:S(2)}) %collective-permute-start.11) | collective-permute-done | bytes 32800 | tf_op jit(solution)/shard_map/ppermute | solution.py:231
  65.3 0.3 collective-permute-done.12
  65.6 1.3 %add_convert_fusion = bf16[2048,256]{1,0:T(8,128)(2,1)} fusion(f32[2048,256]{1,0:T(8,128)S(1)} %get-tuple-element.25, bf16[2048,256]{1,0:T(8,128)(2,1)S(1)} %collective-permute-done.13), kind=kLoop, calls=%fused_computation | loop fusion | flops 1572864 | bytes 4194304 | tf_op jit(solution)/shard_map/convert_element_type | solution.py:252
  66.9 3.9 %all-to-all-start.1 = ((bf16[16,128,256]{2,1,0:T(8,128)(2,1)}), bf16[16,128,256]{2,1,0:T(8,128)(2,1)S(1)}, u32[]{:S(2)}, u32[]{:S(2)}) async-start(bf16[16,128,256]{2,1,0:T(8,128)(2,1)} %bitcast.7), calls=%async_computation.1 | async-start | bytes 2097152 | tf_op jit(solution)/shard_map/all_to_all | solution.py:253
  70.8 0.1 fusion
  71.0 0.7 reshape.20
  71.7 12.1 %all-to-all-done.1.parts = bf16[16,128,256]{2,1,0:T(8,128)(2,1)S(1)} async-done(((bf16[16,128,256]{2,1,0:T(8,128)(2,1)}), bf16[16,128,256]{2,1,0:T(8,128)(2,1)S(1)}, u32[]{:S(2)}, u32[]{:S(2)}) %all-to-all-start.1) | async-done | bytes 1048608 | tf_op jit(solution)/shard_map/all_to_all | solution.py:253
  83.8 0.8 shard_map.87
  (30 shorter events, 0.3 us)
Async XLA Ops:
  26.6 16.4 %collective-permute-start.6 = (bf16[2048,256]{1,0:T(8,128)(2,1)S(1)}, bf16[2048,256]{1,0:T(8,128)(2,1)S(1)}, u32[]{:S(2)}, u32[]{:S(2)}) collective-permute-start(bf16[2048,256]{1,0:T(8,128)(2,1)S(1)} %bitcast.20), channel_id=1, source_target_pairs={{0,1},{1,0},{2,3},{3,2},{4,5},{5,4},{6,7},{7,6},{8,9},{9,8},{10,11... | collective-permute-start | bytes 3145736 | tf_op jit(solution)/shard_map/ppermute | solution.py:235
  26.6 6.0 %collective-permute-start = (bf16[4,72,128]{2,1,0:T(8,128)(2,1)S(1)}, bf16[4,72,128]{2,1,0:T(8,128)(2,1)S(1)}, u32[]{:S(2)}, u32[]{:S(2)}) collective-permute-start(bf16[4,72,128]{2,1,0:T(8,128)(2,1)S(1)} %get-tuple-element.17), channel_id=1, source_target_pairs={{0,32},{32,64},{64,96},{96,0},{1,33},{33,65},{65,97},{97,1},{2,34}... | collective-permute-start | bytes 221192 | tf_op jit(solution)/shard_map/ppermute | solution.py:231
  28.1 7.1 %collective-permute-start.1 = (bf16[4,72,128]{2,1,0:T(8,128)(2,1)S(1)}, bf16[4,72,128]{2,1,0:T(8,128)(2,1)S(1)}, u32[]{:S(2)}, u32[]{:S(2)}) collective-permute-start(bf16[4,72,128]{2,1,0:T(8,128)(2,1)S(1)} %get-tuple-element.18), channel_id=1, source_target_pairs={{0,64},{32,96},{64,0},{96,32},{1,65},{33,97},{65,1},{97,33},{2,66}... | collective-permute-start | bytes 221192 | tf_op jit(solution)/shard_map/ppermute | solution.py:231
  31.0 4.4 %collective-permute-start.2 = (bf16[4,72,128]{2,1,0:T(8,128)(2,1)S(1)}, bf16[4,72,128]{2,1,0:T(8,128)(2,1)S(1)}, u32[]{:S(2)}, u32[]{:S(2)}) collective-permute-start(bf16[4,72,128]{2,1,0:T(8,128)(2,1)S(1)} %get-tuple-element.19), channel_id=1, source_target_pairs={{0,96},{32,0},{64,32},{96,64},{1,97},{33,1},{65,33},{97,65},{2,98}... | collective-permute-start | bytes 221192 | tf_op jit(solution)/shard_map/ppermute | solution.py:231
  35.4 6.6 %collective-permute-start.3 = (bf16[4,72,128]{2,1,0:T(8,128)(2,1)S(1)}, bf16[4,72,128]{2,1,0:T(8,128)(2,1)S(1)}, u32[]{:S(2)}, u32[]{:S(2)}) collective-permute-start(bf16[4,72,128]{2,1,0:T(8,128)(2,1)S(1)} %pad_maximum_fusion.1), channel_id=1, source_target_pairs={{0,8},{8,16},{16,24},{24,0},{1,9},{9,17},{17,25},{25,1},{2,10},{10... | collective-permute-start | bytes 221192 | tf_op jit(solution)/shard_map/ppermute | solution.py:231
  35.6 6.4 %collective-permute-start.4 = (bf16[4,72,128]{2,1,0:T(8,128)(2,1)S(1)}, bf16[4,72,128]{2,1,0:T(8,128)(2,1)S(1)}, u32[]{:S(2)}, u32[]{:S(2)}) collective-permute-start(bf16[4,72,128]{2,1,0:T(8,128)(2,1)S(1)} %pad_maximum_fusion.2), channel_id=1, source_target_pairs={{0,16},{8,24},{16,0},{24,8},{1,17},{9,25},{17,1},{25,9},{2,18},{10... | collective-permute-start | bytes 221192 | tf_op jit(solution)/shard_map/ppermute | solution.py:231
  38.5 4.4 %collective-permute-start.5 = (bf16[4,72,128]{2,1,0:T(8,128)(2,1)S(1)}, bf16[4,72,128]{2,1,0:T(8,128)(2,1)S(1)}, u32[]{:S(2)}, u32[]{:S(2)}) collective-permute-start(bf16[4,72,128]{2,1,0:T(8,128)(2,1)S(1)} %pad_maximum_fusion.3), channel_id=1, source_target_pairs={{0,24},{8,0},{16,8},{24,16},{1,25},{9,1},{17,9},{25,17},{2,26},{10... | collective-permute-start | bytes 221192 | tf_op jit(solution)/shard_map/ppermute | solution.py:231
  48.8 4.2 %collective-permute-start.7 = (bf16[4,32,128]{2,1,0:T(8,128)(2,1)S(1)}, bf16[4,32,128]{2,1,0:T(8,128)(2,1)S(1)}, u32[]{:S(2)}, u32[]{:S(2)}) collective-permute-start(bf16[4,32,128]{2,1,0:T(8,128)(2,1)S(1)} %get-tuple-element.22), channel_id=1, source_target_pairs={{0,24},{8,0},{16,8},{24,16},{1,25},{9,1},{17,9},{25,17},{2,26},{10... | collective-permute-start | bytes 98312 | tf_op jit(solution)/shard_map/ppermute | solution.py:231
  51.3 5.4 %collective-permute-start.8 = (bf16[4,32,128]{2,1,0:T(8,128)(2,1)S(1)}, bf16[4,32,128]{2,1,0:T(8,128)(2,1)S(1)}, u32[]{:S(2)}, u32[]{:S(2)}) collective-permute-start(bf16[4,32,128]{2,1,0:T(8,128)(2,1)S(1)} %get-tuple-element.23), channel_id=1, source_target_pairs={{0,16},{8,24},{16,0},{24,8},{1,17},{9,25},{17,1},{25,9},{2,18},{10... | collective-permute-start | bytes 98312 | tf_op jit(solution)/shard_map/ppermute | solution.py:231
  52.1 5.1 %collective-permute-start.9 = (bf16[4,32,128]{2,1,0:T(8,128)(2,1)S(1)}, bf16[4,32,128]{2,1,0:T(8,128)(2,1)S(1)}, u32[]{:S(2)}, u32[]{:S(2)}) collective-permute-start(bf16[4,32,128]{2,1,0:T(8,128)(2,1)S(1)} %get-tuple-element.24), channel_id=1, source_target_pairs={{0,8},{8,16},{16,24},{24,0},{1,9},{9,17},{17,25},{25,1},{2,10},{10... | collective-permute-start | bytes 98312 | tf_op jit(solution)/shard_map/ppermute | solution.py:231
  52.3 13.3 %collective-permute-start.13 = (bf16[2048,256]{1,0:T(8,128)(2,1)S(1)}, bf16[2048,256]{1,0:T(8,128)(2,1)S(1)}, u32[]{:S(2)}, u32[]{:S(2)}) collective-permute-start(bf16[2048,256]{1,0:T(8,128)(2,1)S(1)} %get-tuple-element.26), channel_id=1, source_target_pairs={{0,1},{1,0},{2,3},{3,2},{4,5},{5,4},{6,7},{7,6},{8,9},{9,8},{10,11... | collective-permute-start | bytes 3145736 | tf_op jit(solution)/shard_map/ppermute | solution.py:235
  57.2 4.2 %collective-permute-start.10 = (bf16[4,32,128]{2,1,0:T(8,128)(2,1)S(1)}, bf16[4,32,128]{2,1,0:T(8,128)(2,1)S(1)}, u32[]{:S(2)}, u32[]{:S(2)}) collective-permute-start(bf16[4,32,128]{2,1,0:T(8,128)(2,1)S(1)} %pad_maximum_fusion.4), channel_id=1, source_target_pairs={{0,96},{32,0},{64,32},{96,64},{1,97},{33,1},{65,33},{97,65},{2,98}... | collective-permute-start | bytes 98312 | tf_op jit(solution)/shard_map/ppermute | solution.py:231
  59.8 5.4 %collective-permute-start.11 = (bf16[4,32,128]{2,1,0:T(8,128)(2,1)S(1)}, bf16[4,32,128]{2,1,0:T(8,128)(2,1)S(1)}, u32[]{:S(2)}, u32[]{:S(2)}) collective-permute-start(bf16[4,32,128]{2,1,0:T(8,128)(2,1)S(1)} %pad_maximum_fusion.5), channel_id=1, source_target_pairs={{0,64},{32,96},{64,0},{96,32},{1,65},{33,97},{65,1},{97,33},{2,66}... | collective-permute-start | bytes 98312 | tf_op jit(solution)/shard_map/ppermute | solution.py:231
  60.4 5.2 %collective-permute-start.12 = (bf16[4,32,128]{2,1,0:T(8,128)(2,1)S(1)}, bf16[4,32,128]{2,1,0:T(8,128)(2,1)S(1)}, u32[]{:S(2)}, u32[]{:S(2)}) collective-permute-start(bf16[4,32,128]{2,1,0:T(8,128)(2,1)S(1)} %pad_maximum_fusion.6), channel_id=1, source_target_pairs={{0,32},{32,64},{64,96},{96,0},{1,33},{33,65},{65,97},{97,1},{2,34}... | collective-permute-start | bytes 98312 | tf_op jit(solution)/shard_map/ppermute | solution.py:231
  66.9 16.9 %all-to-all-start.1 = ((bf16[16,128,256]{2,1,0:T(8,128)(2,1)}), bf16[16,128,256]{2,1,0:T(8,128)(2,1)S(1)}, u32[]{:S(2)}, u32[]{:S(2)}) async-start(bf16[16,128,256]{2,1,0:T(8,128)(2,1)} %bitcast.7), calls=%async_computation.1 | async-start | bytes 2097152 | tf_op jit(solution)/shard_map/all_to_all | solution.py:253

commit v3 on v2

v3 whole, which is shorter than its diff:
```python
import math

import jax
import jax.numpy as jnp
from jax import lax
from jax.experimental import pallas as pl
from jax.experimental.pallas import tpu as pltpu
from jax.sharding import Mesh
from jax.sharding import PartitionSpec as P

HEADS = 16
HEAD_DIM = 128
CAP = 32
TOK = 128
X, Z, C = "ctx_0", "ctx_1", "ctx_2"
CTX = (X, Z, C)
GROUPS = 4
CHUNK = 512
QG_ROWS = 72
FACTOR = 1.0 / math.sqrt(HEAD_DIM)
LOG2E = 1.4426950408889634
NEG_FILL = -1e30

NT = (((1,), (1,)), ((), ()))
TN = (((0,), (0,)), ((), ()))
NN = (((1,), (0,)), ((), ()))


def dot(a, b, dims):
    return lax.dot_general(a, b, dims, preferred_element_type=jnp.float32)


def folded(a, op):
    return op(a.reshape(-1, 8, a.shape[1]), axis=0)


def group_operands(qg, x):
    src = lax.rem(lax.axis_index(X) - x + 4, 4)
    q = jnp.concatenate([qg[src, o, 0:CAP, :] for o in range(4)], axis=0)
    g = jnp.concatenate([qg[src, o, CAP : 2 * CAP, :] for o in range(4)], axis=0)
    where = sum(qg[src, o, 2 * CAP : 2 * CAP + 8, :].astype(jnp.float32) for o in range(4))
    place = 8 * x + 2 * lax.axis_index(Z) + lax.axis_index(C)
    return q, g, where[0:1, :].astype(jnp.int32) + place * TOK


def exponentials(kv, part, x, q, g, slot_pos, e_buf, w_buf):
    rows = lax.broadcasted_iota(jnp.int32, (CHUNK, TOK), 0)
    spread = rows + rows // TOK * TOK
    top = jnp.full((8, TOK), NEG_FILL, jnp.float32)
    for k in range(x + 1):
        at = slice(k * CHUNK, (k + 1) * CHUNK)
        score = dot(kv[at, 0:HEAD_DIM], q, NT)
        if k == x:
            score = jnp.where(spread + (2 * k * CHUNK + part * TOK) <= slot_pos, score, NEG_FILL)
        e_buf[at, :] = score
        top = jnp.maximum(top, folded(score, jnp.max))
    top = jnp.max(top, axis=0, keepdims=True)
    total = jnp.zeros((8, TOK), jnp.float32)
    weighted = jnp.zeros((8, TOK), jnp.float32)
    for k in range(x + 1):
        at = slice(k * CHUNK, (k + 1) * CHUNK)
        score = e_buf[at, :]
        e = jnp.exp2((score - top) * (FACTOR * LOG2E))
        if k == x:
            e = jnp.where(score > 0.5 * NEG_FILL, e, 0.0)
        dw = dot(kv[at, HEAD_DIM : 2 * HEAD_DIM], g, NT)
        e_buf[at, :] = e
        w_buf[at, :] = dw
        total = total + folded(e, jnp.sum)
        weighted = weighted + folded(e * dw, jnp.sum)
    return top, jnp.sum(total, axis=0, keepdims=True), jnp.sum(weighted, axis=0, keepdims=True)


def first_kernel(q0, q1, q2, q3, own, e_own, w_own, stats, qg):
    for p, ref in enumerate((q0, q1, q2, q3)):
        qg[p] = ref[...]
    for x in reversed(range(GROUPS)):
        q, g, slot_pos = group_operands(qg, x)
        at = pl.ds(x * (x + 1) // 2 * CHUNK, (x + 1) * CHUNK)
        part = lax.axis_index(C)
        found = exponentials(own, part, x, q, g, slot_pos, e_own.at[at], w_own.at[at])
        for n in range(3):
            stats[8 * x + n : 8 * x + n + 1, :] = found[n]


def second_kernel(*refs):
    q_in, (own, oth, e_own, w_own, stats) = refs[0:4], refs[4:9]
    q_out, (d_own, d_oth) = refs[9:13], refs[13:15]
    qg, dq, e_buf, w_buf, a_own, a_oth = refs[15:]
    for p in range(4):
        qg[p] = q_in[p][...]
    for x in reversed(range(GROUPS)):
        q, g, slot_pos = group_operands(qg, x)
        at = pl.ds(x * (x + 1) // 2 * CHUNK, (x + 1) * CHUNK)
        top, total, weighted = exponentials(oth, 1 - lax.axis_index(C), x, q, g, slot_pos, e_buf, w_buf)
        own_top, own_total, own_weighted = (stats[8 * x + n : 8 * x + n + 1, :] for n in range(3))
        joint = jnp.maximum(top, own_top)
        oth_scale = jnp.exp2((top - joint) * (FACTOR * LOG2E))
        own_scale = jnp.exp2((own_top - joint) * (FACTOR * LOG2E))
        scale = 1.0 / (total * oth_scale + own_total * own_scale)
        delta = (weighted * oth_scale + own_weighted * own_scale) * scale
        query_sum = jnp.zeros((TOK, HEAD_DIM), jnp.float32)
        for ref, acc, e_ref, w_ref, factor in (
            (oth, a_oth, e_buf, w_buf, oth_scale * scale),
            (own, a_own, e_own.at[at], w_own.at[at], own_scale * scale),
        ):
            for k in range(x + 1):
                rows = slice(k * CHUNK, (k + 1) * CHUNK)
                w = e_ref[rows, :] * factor
                ds = (w * (w_ref[rows, :] - delta)).astype(jnp.bfloat16)
                query_sum = query_sum + dot(ds, ref[rows, 0:HEAD_DIM], TN)
                key_part = dot(ds, q, NN)
                value_part = dot(w.astype(jnp.bfloat16), g, NN)
                if x == GROUPS - 1:
                    acc[rows, 0:HEAD_DIM] = key_part
                    acc[rows, HEAD_DIM : 2 * HEAD_DIM] = value_part
                else:
                    acc[rows, 0:HEAD_DIM] += key_part
                    acc[rows, HEAD_DIM : 2 * HEAD_DIM] += value_part
        src = lax.rem(lax.axis_index(X) - x + 4, 4)
        dq[src] = (query_sum * FACTOR).astype(jnp.bfloat16).reshape(4, CAP, HEAD_DIM)
    for p in range(4):
        q_out[p][...] = dq[p]
    d_own[:, 0:HEAD_DIM] = a_own[:, 0:HEAD_DIM] * FACTOR
    d_own[:, HEAD_DIM:] = a_own[:, HEAD_DIM:]
    d_oth[:, 0:HEAD_DIM] = (a_oth[:, 0:HEAD_DIM] * FACTOR).astype(jnp.bfloat16)
    d_oth[:, HEAD_DIM:] = a_oth[:, HEAD_DIM:].astype(jnp.bfloat16)


VMEM = pl.BlockSpec(memory_space=pltpu.VMEM)
HBM = pl.BlockSpec(memory_space=pltpu.HBM)
PAIRS = GROUPS * (GROUPS + 1) // 2 * CHUNK


def kernel_params(mib):
    return pltpu.CompilerParams(vmem_limit_bytes=mib * 2**20)


def attention_first(qg, own):
    return pl.pallas_call(
        first_kernel,
        out_shape=(
            jax.ShapeDtypeStruct((PAIRS, TOK), jnp.float32),
            jax.ShapeDtypeStruct((PAIRS, TOK), jnp.float32),
            jax.ShapeDtypeStruct((8 * GROUPS, TOK), jnp.float32),
        ),
        in_specs=[VMEM] * 5,
        out_specs=(VMEM,) * 3,
        scratch_shapes=[pltpu.VMEM((4, 4, QG_ROWS, HEAD_DIM), jnp.bfloat16)],
        compiler_params=kernel_params(16),
        cost_estimate=pl.CostEstimate(
            flops=2 * 2 * PAIRS * TOK * HEAD_DIM, bytes_accessed=4 * 2**20, transcendentals=PAIRS * TOK
        ),
    )(*qg, own)


def attention_second(qg, own, oth, found):
    keys = own.shape[0]
    out = pl.pallas_call(
        second_kernel,
        out_shape=(jax.ShapeDtypeStruct((4, CAP, HEAD_DIM), jnp.bfloat16),) * 4
        + (
            jax.ShapeDtypeStruct((keys, 2 * HEAD_DIM), jnp.float32),
            jax.ShapeDtypeStruct((keys, 2 * HEAD_DIM), jnp.bfloat16),
        ),
        in_specs=[VMEM] * 9,
        out_specs=(VMEM,) * 6,
        scratch_shapes=[
            pltpu.VMEM((4, 4, QG_ROWS, HEAD_DIM), jnp.bfloat16),
            pltpu.VMEM((4, 4, CAP, HEAD_DIM), jnp.bfloat16),
            pltpu.VMEM((keys, TOK), jnp.float32),
            pltpu.VMEM((keys, TOK), jnp.float32),
            pltpu.VMEM((keys, 2 * HEAD_DIM), jnp.float32),
            pltpu.VMEM((keys, 2 * HEAD_DIM), jnp.float32),
        ],
        compiler_params=kernel_params(24),
        cost_estimate=pl.CostEstimate(
            flops=2 * 8 * PAIRS * TOK * HEAD_DIM, bytes_accessed=10 * 2**20, transcendentals=PAIRS * TOK
        ),
    )(*qg, own, oth, *found)
    return out[0:4], out[4], out[5]


def pack_kernel(keys, values, queries, grad_out, surv_index, counts, kv, *rest):
    qg, (k_buf, v_buf, kv_buf, q_buf, g_buf, s_buf, c_buf, sems) = rest[0:4], rest[4:]
    depth = lax.axis_index("rec")
    ctx = lax.axis_index(X) * 8 + lax.axis_index(Z) * 2 + lax.axis_index(C)
    mine = pl.ds(pl.multiple_of(depth * 4 * HEAD_DIM, 4 * HEAD_DIM), 4 * HEAD_DIM)
    copies = [
        pltpu.make_async_copy(src, dst, sems.at[n])
        for n, (src, dst) in enumerate(
            (
                (keys.at[:, mine], k_buf),
                (values.at[:, mine], v_buf),
                (queries.at[0], q_buf),
                (grad_out.at[0], g_buf),
                (surv_index, s_buf),
                (counts, c_buf),
            )
        )
    ]
    for copy in copies:
        copy.start()
    copies[0].wait()
    copies[1].wait()
    for x in range(4):
        cols = slice(x * HEAD_DIM, (x + 1) * HEAD_DIM)
        kv_buf[x, :, 0:HEAD_DIM] = k_buf[:, cols]
        kv_buf[x, :, HEAD_DIM:] = v_buf[:, cols]
    out = [pltpu.make_async_copy(kv_buf, kv.at[:, z], sems.at[6 + z]) for z in range(4)]
    for copy in out:
        copy.start()
    for copy in copies[2:]:
        copy.wait()
    live = lax.broadcasted_iota(jnp.int32, (CAP, HEAD_DIM), 0) < c_buf[0, ctx]
    quarter = lax.rem(ctx, 4)
    near = s_buf[0:1, pl.ds(pl.multiple_of(ctx // 4 * TOK, TOK), TOK)]
    lane_group = lax.broadcasted_iota(jnp.int32, (8, TOK), 1) // CAP
    for o in range(4):
        where = pltpu.roll(jnp.broadcast_to(near, (8, TOK)), lax.rem(o - quarter + 4, 4) * CAP, 1)
        where = jnp.where(lane_group == o, where, 0).astype(jnp.float32).astype(jnp.bfloat16)
        for x in range(4):
            head = lax.rem(depth + o, 4) * 4 + x
            cols = pl.ds(pl.multiple_of(head * HEAD_DIM, HEAD_DIM), HEAD_DIM)
            qg[o][x, 0:CAP, :] = q_buf[:, cols]
            grad = jnp.where(live, g_buf[:, cols].astype(jnp.float32), 0.0)
            qg[o][x, CAP : 2 * CAP, :] = grad.astype(jnp.bfloat16)
            qg[o][x, 2 * CAP :, :] = where
    for copy in out:
        copy.wait()


def pack(keys, values, queries, grad_out, surv_index, counts):
    vmem = pl.BlockSpec(memory_space=pltpu.VMEM)
    hbm = pl.BlockSpec(memory_space=pltpu.HBM)
    out = pl.pallas_call(
        pack_kernel,
        out_shape=(jax.ShapeDtypeStruct((4, 4, TOK, 2 * HEAD_DIM), jnp.bfloat16),)
        + (jax.ShapeDtypeStruct((4, QG_ROWS, HEAD_DIM), jnp.bfloat16),) * 4,
        in_specs=[hbm] * 6,
        out_specs=(hbm,) + (vmem,) * 4,
        scratch_shapes=[
            pltpu.VMEM((TOK, 4 * HEAD_DIM), jnp.bfloat16),
            pltpu.VMEM((TOK, 4 * HEAD_DIM), jnp.bfloat16),
            pltpu.VMEM((4, TOK, 2 * HEAD_DIM), jnp.bfloat16),
            pltpu.VMEM((CAP, HEADS * HEAD_DIM), jnp.bfloat16),
            pltpu.VMEM((CAP, HEADS * HEAD_DIM), jnp.bfloat16),
            pltpu.VMEM(surv_index.shape, jnp.int32),
            pltpu.SMEM(counts.shape, jnp.int32),
            pltpu.SemaphoreType.DMA((10,)),
        ],
        compiler_params=pltpu.CompilerParams(vmem_limit_bytes=8 * 2**20),
    )(*(pltpu.with_memory_space_constraint(a, pltpu.HBM) for a in (keys, values, queries, grad_out, surv_index, counts)))
    return out[0].reshape(16, TOK, 2 * HEAD_DIM), out[1:]


def unpack_kernel(parts, key_grad, value_grad, k_buf, v_buf, sems):
    sides = ((k_buf, key_grad, 0), (v_buf, value_grad, HEAD_DIM))
    copies = []
    for n, (buf, out, at) in enumerate(sides):
        for x in range(4):
            total = sum(parts[4 * x + z, :, at : at + HEAD_DIM].astype(jnp.float32) for z in range(4))
            buf[:, x * HEAD_DIM : (x + 1) * HEAD_DIM] = total.astype(jnp.bfloat16)
        copies.append(pltpu.make_async_copy(buf, out, sems.at[n]))
        copies[n].start()
    for copy in copies:
        copy.wait()


def unpack(parts):
    out = jax.ShapeDtypeStruct((TOK, 4 * HEAD_DIM), jnp.bfloat16)
    return pl.pallas_call(
        unpack_kernel,
        out_shape=(out, out),
        in_specs=[pl.BlockSpec(memory_space=pltpu.VMEM)],
        out_specs=(pl.BlockSpec(memory_space=pl.ANY),) * 2,
        scratch_shapes=[
            pltpu.VMEM((TOK, 4 * HEAD_DIM), jnp.bfloat16),
            pltpu.VMEM((TOK, 4 * HEAD_DIM), jnp.bfloat16),
            pltpu.SemaphoreType.DMA((2,)),
        ],
        compiler_params=pltpu.CompilerParams(vmem_limit_bytes=8 * 2**20),
    )(parts)


def add_kernel(own, mine, out, buf, sems):
    copies = []
    for k in range(GROUPS):
        rows = slice(k * CHUNK, (k + 1) * CHUNK)
        buf[rows, :] = (own[rows, :] + mine[rows, :].astype(jnp.float32)).astype(jnp.bfloat16)
        copies.append(pltpu.make_async_copy(buf.at[rows], out.at[rows], sems.at[k]))
        copies[k].start()
    for copy in copies:
        copy.wait()


def added(own, mine):
    return pl.pallas_call(
        add_kernel,
        out_shape=jax.ShapeDtypeStruct(mine.shape, jnp.bfloat16),
        in_specs=[VMEM] * 2,
        out_specs=HBM,
        scratch_shapes=[pltpu.VMEM(mine.shape, jnp.bfloat16), pltpu.SemaphoreType.DMA((GROUPS,))],
        compiler_params=pltpu.CompilerParams(vmem_limit_bytes=8 * 2**20),
    )(own, mine)


def moved(a, axis, by):
    return a if by % 4 == 0 else lax.ppermute(a, axis, [(i, (i + by) % 4) for i in range(4)])


def swap_cores(a):
    return lax.ppermute(a, C, [(0, 1), (1, 0)])


def gradients(queries, grad_out, keys, values, surv_index, counts):
    depth, here = lax.axis_index("rec"), lax.axis_index(X)
    kv, by_depth = pack(keys, values, queries, grad_out, surv_index, counts)
    kv = lax.all_to_all(kv, (X, Z), 0, 0, tiled=True).reshape(16 * TOK, 2 * HEAD_DIM)
    kv_other = swap_cores(kv)
    by_depth = [moved(by_depth[o], "rec", o) for o in range(4)]

    def for_x(p):
        at = lax.rem(here + p, 4)
        return jnp.concatenate([lax.dynamic_slice_in_dim(a, at, 1, axis=0) for a in by_depth], axis=0)

    qg = [moved(for_x(p), X, p) for p in range(4)]
    found = attention_first(qg, kv)
    dq, d_own, d_other = attention_second(qg, kv, kv_other, found)
    mine = swap_cores(d_other)
    sums = added(d_own, mine)
    sums = lax.all_to_all(sums.reshape(16, TOK, 2 * HEAD_DIM), (X, Z), 0, 0, tiled=True)
    back = []
    for p in range(4):
        back.append(moved(dq[p], X, -p))
    dq = back
    dq = [moved(jnp.stack([dq[p][o] for p in range(4)]), "rec", -o) for o in range(4)]
    dq = jnp.roll(jnp.stack(dq), (depth, here), (0, 1))
    query_grad = dq.reshape(HEADS, CAP, HEAD_DIM).transpose(1, 0, 2).reshape(1, CAP, HEADS * HEAD_DIM)
    key_grad, value_grad = unpack(sums)
    return query_grad, key_grad, value_grad


def solution(mesh):
    split = Mesh(mesh.devices.reshape(mesh.shape["rec"], 4, 4, 2), ("rec", X, Z, C))
    return jax.shard_map(
        gradients,
        mesh=split,
        in_specs=(
            P("rec", CTX, None),
            P("rec", CTX, None),
            P(CTX, None),
            P(CTX, None),
            P("rec", None),
            P("rec", None),
        ),
        out_specs=(P("rec", CTX, None), P(CTX, "rec"), P(CTX, "rec")),
        check_vma=False,
    )
```

time: 84.8 us -> 84.5 us (level)
  other arithmetic: 1.42 us -> 0.16 us
  Pallas kernels: 7.89 us -> 8.8 us
    convert_element_type x1 -> x0, other arithmetic: 1.26 us -> none  [gradients(): sums = (d_own + mine.astype(jnp.float32)).astype(jnp.bfloat16)]
    pallas_call x2 -> x4, Pallas kernels: 7.08 us -> 7.99 us  [the longest x1 4.38 us: attention_second(): pl.pallas_call(second_kernel, out_shape=(jax.ShapeDtypeStruct((4, CAP, HE...]
  transfers between devices with their start and end apart: 15 -> 15, of which waited for: 12 -> 12; matrix products, arithmetic and copies ran while one was open for 1% -> 1% of each run, Pallas kernels for 0% -> 1%
where the time goes in v3:
time: 84.5 us; the launch traced here: 84.3 us
  waiting for transfers between devices  27.7 us (33%)
  blocking collectives  24.6 us (29%)
  starting transfers between devices  21.4 us (25%)
  Pallas kernels  8.8 us (10%)
  local copies, waits for them, and re-layouts  0.88 us (1%)
    all_to_all x1, blocking collectives, gradients(): lax.all_to_all(kv, (X, Z), 0, 0, tiled=True).reshape(16 * TOK, 2 * HEAD_DIM)  24.6 us
    ppermute x12, starting transfers between devices, moved(): lax.ppermute(a, axis, [(i, (i + by) % 4) for i in range(4)])  17.5 us
    ppermute x12, waiting for transfers between devices, moved(): lax.ppermute(a, axis, [(i, (i + by) % 4) for i in range(4)])  15.6 us
    all_to_all x1, waiting for transfers between devices, gradients(): lax.all_to_all(sums.reshape(16, TOK, 2 * HEAD_DIM), (X, Z), 0, 0, tiled=T...  12.1 us
    pallas_call x1, Pallas kernels, attention_second(): pl.pallas_call(second_kernel, out_shape=(jax.ShapeDtypeStruct((4, CAP, HE...  4.38 us
    all_to_all x1, starting transfers between devices, gradients(): lax.all_to_all(sums.reshape(16, TOK, 2 * HEAD_DIM), (X, Z), 0, 0, tiled=T...  3.89 us
  transfers between devices with their start and end apart: 15, of which 12 were waited for; matrix products, arithmetic and copies ran while one was open for 1% of the time, Pallas kernels for 1%

profile of v3, /device:TPU:0, one launch (start us, length us, event | category | flops | bytes accessed | tf_op | source)
XLA Modules:
  0.0 84.3 jit_solution(13568940875228588925)
XLA Ops:
  0.6 1.3 %shard_map.85 = (bf16[4,4,128,256]{3,2,1,0:T(8,128)(2,1)S(1)}, bf16[4,72,128]{2,1,0:T(8,128)(2,1)S(1)}, bf16[4,72,128]{2,1,0:T(8,128)(2,1)S(1)}, bf16[4,72,128]{2,1,0:T(8,128)(2,1)S(1)}, bf16[4,72,128]{2,1,0:T(8,128)(2,1)S(1)}) custom-call(bf16[128,2048]{1,0:T(8,128)(2,1)} %keys.1, bf16[128,2048]{1,0:T(8,128)(2,1)} %values.1, bf16[1,32,2048]{2,1,0:T(8,128)(2,1)} %queries.1, ...), custom_call_target="tpu_custom_call" | custom-call | tf_op jit(solution)/shard_map/pallas_call | solution.py:236
  1.9 24.6 %all_to_all.10 = bf16[16,128,256]{2,1,0:T(8,128)(2,1)S(1)} all-to-all(bf16[16,128,256]{2,1,0:T(8,128)(2,1)S(1)} %bitcast.24), channel_id=1, replica_groups=mesh['rec'=4,'ctx_0'=4,'ctx_1'=4,'ctx_2'=2] {'ctx_0','ctx_1'}, dimensions={0} | all-to-all | bytes 2097152 | tf_op jit(solution)/shard_map/all_to_all | solution.py:319
  26.6 1.6 %collective-permute-start = (bf16[4,72,128]{2,1,0:T(8,128)(2,1)S(1)}, bf16[4,72,128]{2,1,0:T(8,128)(2,1)S(1)}, u32[]{:S(2)}, u32[]{:S(2)}) collective-permute-start(bf16[4,72,128]{2,1,0:T(8,128)(2,1)S(1)} %get-tuple-element.20), channel_id=1, source_target_pairs={{0,32},{32,64},{64,96},{96,0},{1,33},{33,65},{65,97},{97,1},{2,34}... | collective-permute-start | bytes 221192 | tf_op jit(solution)/shard_map/ppermute | solution.py:309
  28.2 2.9 %collective-permute-start.1 = (bf16[4,72,128]{2,1,0:T(8,128)(2,1)S(1)}, bf16[4,72,128]{2,1,0:T(8,128)(2,1)S(1)}, u32[]{:S(2)}, u32[]{:S(2)}) collective-permute-start(bf16[4,72,128]{2,1,0:T(8,128)(2,1)S(1)} %get-tuple-element.21), channel_id=1, source_target_pairs={{0,64},{32,96},{64,0},{96,32},{1,65},{33,97},{65,1},{97,33},{2,66}... | collective-permute-start | bytes 221192 | tf_op jit(solution)/shard_map/ppermute | solution.py:309
  31.1 1.3 %collective-permute-start.2 = (bf16[4,72,128]{2,1,0:T(8,128)(2,1)S(1)}, bf16[4,72,128]{2,1,0:T(8,128)(2,1)S(1)}, u32[]{:S(2)}, u32[]{:S(2)}) collective-permute-start(bf16[4,72,128]{2,1,0:T(8,128)(2,1)S(1)} %get-tuple-element.22), channel_id=1, source_target_pairs={{0,96},{32,0},{64,32},{96,64},{1,97},{33,1},{65,33},{97,65},{2,98}... | collective-permute-start | bytes 221192 | tf_op jit(solution)/shard_map/ppermute | solution.py:309
  32.4 0.1 collective-permute-done
  32.5 2.8 %collective-permute-done.1 = bf16[4,72,128]{2,1,0:T(8,128)(2,1)S(1)} collective-permute-done((bf16[4,72,128]{2,1,0:T(8,128)(2,1)S(1)}, bf16[4,72,128]{2,1,0:T(8,128)(2,1)S(1)}, u32[]{:S(2)}, u32[]{:S(2)}) %collective-permute-start.1) | collective-permute-done | bytes 73760 | tf_op jit(solution)/shard_map/ppermute | solution.py:309
  35.3 0.1 collective-permute-done.2
  35.4 0.2 collective-permute-start.3
  35.7 2.9 %collective-permute-start.4 = (bf16[4,72,128]{2,1,0:T(8,128)(2,1)S(1)}, bf16[4,72,128]{2,1,0:T(8,128)(2,1)S(1)}, u32[]{:S(2)}, u32[]{:S(2)}) collective-permute-start(bf16[4,72,128]{2,1,0:T(8,128)(2,1)S(1)} %pad_maximum_fusion.2), channel_id=1, source_target_pairs={{0,16},{8,24},{16,0},{24,8},{1,17},{9,25},{17,1},{25,9},{2,18},{10... | collective-permute-start | bytes 221192 | tf_op jit(solution)/shard_map/ppermute | solution.py:309
  38.5 1.1 %collective-permute-start.5 = (bf16[4,72,128]{2,1,0:T(8,128)(2,1)S(1)}, bf16[4,72,128]{2,1,0:T(8,128)(2,1)S(1)}, u32[]{:S(2)}, u32[]{:S(2)}) collective-permute-start(bf16[4,72,128]{2,1,0:T(8,128)(2,1)S(1)} %pad_maximum_fusion.3), channel_id=1, source_target_pairs={{0,24},{8,0},{16,8},{24,16},{1,25},{9,1},{17,9},{25,17},{2,26},{10... | collective-permute-start | bytes 221192 | tf_op jit(solution)/shard_map/ppermute | solution.py:309
  39.7 2.4 %collective-permute-done.3.q1.refs_1_ = bf16[4,72,128]{2,1,0:T(8,128)(2,1)S(1)} collective-permute-done((bf16[4,72,128]{2,1,0:T(8,128)(2,1)S(1)}, bf16[4,72,128]{2,1,0:T(8,128)(2,1)S(1)}, u32[]{:S(2)}, u32[]{:S(2)}) %collective-permute-start.3) | collective-permute-done | bytes 73760 | tf_op jit(solution)/shard_map/ppermute | solution.py:309
  42.0 0.9 %collective-permute-done.5.q3.refs_3_ = bf16[4,72,128]{2,1,0:T(8,128)(2,1)S(1)} collective-permute-done((bf16[4,72,128]{2,1,0:T(8,128)(2,1)S(1)}, bf16[4,72,128]{2,1,0:T(8,128)(2,1)S(1)}, u32[]{:S(2)}, u32[]{:S(2)}) %collective-permute-start.5) | collective-permute-done | bytes 73760 | tf_op jit(solution)/shard_map/ppermute | solution.py:309
  43.0 1.2 %shard_map.86 = (f32[5120,128]{1,0:T(8,128)S(1)}, f32[5120,128]{1,0:T(8,128)S(1)}, f32[32,128]{1,0:T(8,128)S(1)}) custom-call(bf16[4,72,128]{2,1,0:T(8,128)(2,1)S(1)} %pad_maximum_fusion.q0.refs_0_, bf16[4,72,128]{2,1,0:T(8,128)(2,1)S(1)} %collective-permute-done.3.q1.refs_1_, bf16[4,72,128]{2,1,0:T(8,128)(2,1)S(1)} %collective-permute-done.4.q2.refs_2_, ...), custom_call_target="tpu_custom_call" | custom-call | flops 335544320 | bytes 4194304 | tf_op jit(solution)/shard_map/pallas_call | solution.py:140
  44.2 4.4 %shard_map.87 = (bf16[4,32,128]{2,1,0:T(8,128)(2,1)S(1)}, bf16[4,32,128]{2,1,0:T(8,128)(2,1)S(1)}, bf16[4,32,128]{2,1,0:T(8,128)(2,1)S(1)}, bf16[4,32,128]{2,1,0...) custom-call(bf16[4,72,128]{2,1,0:T(8,128)(2,1)S(1)} %pad_maximum_fusion.q0.refs_0_, ...), custom_call_target="tpu_custom_call" | custom-call | flops 1342177280 | bytes 10485760 | tf_op jit(solution)/shard_map/pallas_call | solution.py:159
  48.6 2.6 %collective-permute-start.7 = (bf16[4,32,128]{2,1,0:T(8,128)(2,1)S(1)}, bf16[4,32,128]{2,1,0:T(8,128)(2,1)S(1)}, u32[]{:S(2)}, u32[]{:S(2)}) collective-permute-start(bf16[4,32,128]{2,1,0:T(8,128)(2,1)S(1)} %get-tuple-element.28), channel_id=1, source_target_pairs={{0,24},{8,0},{16,8},{24,16},{1,25},{9,1},{17,9},{25,17},{2,26},{10... | collective-permute-start | bytes 98312 | tf_op jit(solution)/shard_map/ppermute | solution.py:309
  51.2 0.7 collective-permute-start.8
  51.9 0.3 collective-permute-start.9
  52.1 0.6 collective-permute-done.7
  52.8 3.8 %collective-permute-done.8 = bf16[4,32,128]{2,1,0:T(8,128)(2,1)S(1)} collective-permute-done((bf16[4,32,128]{2,1,0:T(8,128)(2,1)S(1)}, bf16[4,32,128]{2,1,0:T(8,128)(2,1)S(1)}, u32[]{:S(2)}, u32[]{:S(2)}) %collective-permute-start.8) | collective-permute-done | bytes 32800 | tf_op jit(solution)/shard_map/ppermute | solution.py:309
  56.6 0.4 collective-permute-done.9
  57.0 2.6 %collective-permute-start.10 = (bf16[4,32,128]{2,1,0:T(8,128)(2,1)S(1)}, bf16[4,32,128]{2,1,0:T(8,128)(2,1)S(1)}, u32[]{:S(2)}, u32[]{:S(2)}) collective-permute-start(bf16[4,32,128]{2,1,0:T(8,128)(2,1)S(1)} %pad_maximum_fusion.4), channel_id=1, source_target_pairs={{0,96},{32,0},{64,32},{96,64},{1,97},{33,1},{65,33},{97,65},{2,98}... | collective-permute-start | bytes 98312 | tf_op jit(solution)/shard_map/ppermute | solution.py:309
  59.7 0.5 collective-permute-start.11
  60.2 0.7 collective-permute-start.12
  61.0 0.3 collective-permute-done.10
  61.3 3.8 %collective-permute-done.11 = bf16[4,32,128]{2,1,0:T(8,128)(2,1)S(1)} collective-permute-done((bf16[4,32,128]{2,1,0:T(8,128)(2,1)S(1)}, bf16[4,32,128]{2,1,0:T(8,128)(2,1)S(1)}, u32[]{:S(2)}, u32[]{:S(2)}) %collective-permute-start.11) | collective-permute-done | bytes 32800 | tf_op jit(solution)/shard_map/ppermute | solution.py:309
  65.1 0.3 collective-permute-done.12
  65.5 1.1 %shard_map.88 = bf16[2048,256]{1,0:T(8,128)(2,1)} custom-call(f32[2048,256]{1,0:T(8,128)S(1)} %get-tuple-element.31.own, bf16[2048,256]{1,0:T(8,128)(2,1)S(1)} %collective-permute-done.13.mine), custom_call_target="tpu_custom_call" | custom-call | tf_op jit(solution)/shard_map/pallas_call | solution.py:298
  66.6 3.9 %all-to-all-start.1 = ((bf16[16,128,256]{2,1,0:T(8,128)(2,1)}), bf16[16,128,256]{2,1,0:T(8,128)(2,1)S(1)}, u32[]{:S(2)}, u32[]{:S(2)}) async-start(bf16[16,128,256]{2,1,0:T(8,128)(2,1)} %bitcast.8), calls=%async_computation.1 | async-start | bytes 2097152 | tf_op jit(solution)/shard_map/all_to_all | solution.py:332
  70.7 0.7 reshape.24
  71.4 12.1 %all-to-all-done.1.parts = bf16[16,128,256]{2,1,0:T(8,128)(2,1)S(1)} async-done(((bf16[16,128,256]{2,1,0:T(8,128)(2,1)}), bf16[16,128,256]{2,1,0:T(8,128)(2,1)S(1)}, u32[]{:S(2)}, u32[]{:S(2)}) %all-to-all-start.1) | async-done | bytes 1048608 | tf_op jit(solution)/shard_map/all_to_all | solution.py:332
  83.5 0.8 shard_map.89
  (31 shorter events, 0.3 us)
Async XLA Ops:
  26.6 17.6 %collective-permute-start.6 = (bf16[2048,256]{1,0:T(8,128)(2,1)S(1)}, bf16[2048,256]{1,0:T(8,128)(2,1)S(1)}, u32[]{:S(2)}, u32[]{:S(2)}) collective-permute-start(bf16[2048,256]{1,0:T(8,128)(2,1)S(1)} %bitcast.21), channel_id=1, source_target_pairs={{0,1},{1,0},{2,3},{3,2},{4,5},{5,4},{6,7},{7,6},{8,9},{9,8},{10,11... | collective-permute-start | bytes 3145736 | tf_op jit(solution)/shard_map/ppermute | solution.py:313
  26.6 6.0 %collective-permute-start = (bf16[4,72,128]{2,1,0:T(8,128)(2,1)S(1)}, bf16[4,72,128]{2,1,0:T(8,128)(2,1)S(1)}, u32[]{:S(2)}, u32[]{:S(2)}) collective-permute-start(bf16[4,72,128]{2,1,0:T(8,128)(2,1)S(1)} %get-tuple-element.20), channel_id=1, source_target_pairs={{0,32},{32,64},{64,96},{96,0},{1,33},{33,65},{65,97},{97,1},{2,34}... | collective-permute-start | bytes 221192 | tf_op jit(solution)/shard_map/ppermute | solution.py:309
  28.2 7.1 %collective-permute-start.1 = (bf16[4,72,128]{2,1,0:T(8,128)(2,1)S(1)}, bf16[4,72,128]{2,1,0:T(8,128)(2,1)S(1)}, u32[]{:S(2)}, u32[]{:S(2)}) collective-permute-start(bf16[4,72,128]{2,1,0:T(8,128)(2,1)S(1)} %get-tuple-element.21), channel_id=1, source_target_pairs={{0,64},{32,96},{64,0},{96,32},{1,65},{33,97},{65,1},{97,33},{2,66}... | collective-permute-start | bytes 221192 | tf_op jit(solution)/shard_map/ppermute | solution.py:309
  31.1 4.4 %collective-permute-start.2 = (bf16[4,72,128]{2,1,0:T(8,128)(2,1)S(1)}, bf16[4,72,128]{2,1,0:T(8,128)(2,1)S(1)}, u32[]{:S(2)}, u32[]{:S(2)}) collective-permute-start(bf16[4,72,128]{2,1,0:T(8,128)(2,1)S(1)} %get-tuple-element.22), channel_id=1, source_target_pairs={{0,96},{32,0},{64,32},{96,64},{1,97},{33,1},{65,33},{97,65},{2,98}... | collective-permute-start | bytes 221192 | tf_op jit(solution)/shard_map/ppermute | solution.py:309
  35.4 6.6 %collective-permute-start.3 = (bf16[4,72,128]{2,1,0:T(8,128)(2,1)S(1)}, bf16[4,72,128]{2,1,0:T(8,128)(2,1)S(1)}, u32[]{:S(2)}, u32[]{:S(2)}) collective-permute-start(bf16[4,72,128]{2,1,0:T(8,128)(2,1)S(1)} %pad_maximum_fusion.1), channel_id=1, source_target_pairs={{0,8},{8,16},{16,24},{24,0},{1,9},{9,17},{17,25},{25,1},{2,10},{10... | collective-permute-start | bytes 221192 | tf_op jit(solution)/shard_map/ppermute | solution.py:309
  35.7 6.4 %collective-permute-start.4 = (bf16[4,72,128]{2,1,0:T(8,128)(2,1)S(1)}, bf16[4,72,128]{2,1,0:T(8,128)(2,1)S(1)}, u32[]{:S(2)}, u32[]{:S(2)}) collective-permute-start(bf16[4,72,128]{2,1,0:T(8,128)(2,1)S(1)} %pad_maximum_fusion.2), channel_id=1, source_target_pairs={{0,16},{8,24},{16,0},{24,8},{1,17},{9,25},{17,1},{25,9},{2,18},{10... | collective-permute-start | bytes 221192 | tf_op jit(solution)/shard_map/ppermute | solution.py:309
  38.5 4.4 %collective-permute-start.5 = (bf16[4,72,128]{2,1,0:T(8,128)(2,1)S(1)}, bf16[4,72,128]{2,1,0:T(8,128)(2,1)S(1)}, u32[]{:S(2)}, u32[]{:S(2)}) collective-permute-start(bf16[4,72,128]{2,1,0:T(8,128)(2,1)S(1)} %pad_maximum_fusion.3), channel_id=1, source_target_pairs={{0,24},{8,0},{16,8},{24,16},{1,25},{9,1},{17,9},{25,17},{2,26},{10... | collective-permute-start | bytes 221192 | tf_op jit(solution)/shard_map/ppermute | solution.py:309
  48.6 4.2 %collective-permute-start.7 = (bf16[4,32,128]{2,1,0:T(8,128)(2,1)S(1)}, bf16[4,32,128]{2,1,0:T(8,128)(2,1)S(1)}, u32[]{:S(2)}, u32[]{:S(2)}) collective-permute-start(bf16[4,32,128]{2,1,0:T(8,128)(2,1)S(1)} %get-tuple-element.28), channel_id=1, source_target_pairs={{0,24},{8,0},{16,8},{24,16},{1,25},{9,1},{17,9},{25,17},{2,26},{10... | collective-permute-start | bytes 98312 | tf_op jit(solution)/shard_map/ppermute | solution.py:309
  51.2 5.4 %collective-permute-start.8 = (bf16[4,32,128]{2,1,0:T(8,128)(2,1)S(1)}, bf16[4,32,128]{2,1,0:T(8,128)(2,1)S(1)}, u32[]{:S(2)}, u32[]{:S(2)}) collective-permute-start(bf16[4,32,128]{2,1,0:T(8,128)(2,1)S(1)} %get-tuple-element.29), channel_id=1, source_target_pairs={{0,16},{8,24},{16,0},{24,8},{1,17},{9,25},{17,1},{25,9},{2,18},{10... | collective-permute-start | bytes 98312 | tf_op jit(solution)/shard_map/ppermute | solution.py:309
  51.9 5.1 %collective-permute-start.9 = (bf16[4,32,128]{2,1,0:T(8,128)(2,1)S(1)}, bf16[4,32,128]{2,1,0:T(8,128)(2,1)S(1)}, u32[]{:S(2)}, u32[]{:S(2)}) collective-permute-start(bf16[4,32,128]{2,1,0:T(8,128)(2,1)S(1)} %get-tuple-element.30), channel_id=1, source_target_pairs={{0,8},{8,16},{16,24},{24,0},{1,9},{9,17},{17,25},{25,1},{2,10},{10... | collective-permute-start | bytes 98312 | tf_op jit(solution)/shard_map/ppermute | solution.py:309
  52.1 13.3 %collective-permute-start.13 = (bf16[2048,256]{1,0:T(8,128)(2,1)S(1)}, bf16[2048,256]{1,0:T(8,128)(2,1)S(1)}, u32[]{:S(2)}, u32[]{:S(2)}) collective-permute-start(bf16[2048,256]{1,0:T(8,128)(2,1)S(1)} %get-tuple-element.32), channel_id=1, source_target_pairs={{0,1},{1,0},{2,3},{3,2},{4,5},{5,4},{6,7},{7,6},{8,9},{9,8},{10,11... | collective-permute-start | bytes 3145736 | tf_op jit(solution)/shard_map/ppermute | solution.py:313
  57.0 4.2 %collective-permute-start.10 = (bf16[4,32,128]{2,1,0:T(8,128)(2,1)S(1)}, bf16[4,32,128]{2,1,0:T(8,128)(2,1)S(1)}, u32[]{:S(2)}, u32[]{:S(2)}) collective-permute-start(bf16[4,32,128]{2,1,0:T(8,128)(2,1)S(1)} %pad_maximum_fusion.4), channel_id=1, source_target_pairs={{0,96},{32,0},{64,32},{96,64},{1,97},{33,1},{65,33},{97,65},{2,98}... | collective-permute-start | bytes 98312 | tf_op jit(solution)/shard_map/ppermute | solution.py:309
  59.7 5.4 %collective-permute-start.11 = (bf16[4,32,128]{2,1,0:T(8,128)(2,1)S(1)}, bf16[4,32,128]{2,1,0:T(8,128)(2,1)S(1)}, u32[]{:S(2)}, u32[]{:S(2)}) collective-permute-start(bf16[4,32,128]{2,1,0:T(8,128)(2,1)S(1)} %pad_maximum_fusion.5), channel_id=1, source_target_pairs={{0,64},{32,96},{64,0},{96,32},{1,65},{33,97},{65,1},{97,33},{2,66}... | collective-permute-start | bytes 98312 | tf_op jit(solution)/shard_map/ppermute | solution.py:309
  60.2 5.2 %collective-permute-start.12 = (bf16[4,32,128]{2,1,0:T(8,128)(2,1)S(1)}, bf16[4,32,128]{2,1,0:T(8,128)(2,1)S(1)}, u32[]{:S(2)}, u32[]{:S(2)}) collective-permute-start(bf16[4,32,128]{2,1,0:T(8,128)(2,1)S(1)} %pad_maximum_fusion.6), channel_id=1, source_target_pairs={{0,32},{32,64},{64,96},{96,0},{1,33},{33,65},{65,97},{97,1},{2,34}... | collective-permute-start | bytes 98312 | tf_op jit(solution)/shard_map/ppermute | solution.py:309
  66.6 16.9 %all-to-all-start.1 = ((bf16[16,128,256]{2,1,0:T(8,128)(2,1)}), bf16[16,128,256]{2,1,0:T(8,128)(2,1)S(1)}, u32[]{:S(2)}, u32[]{:S(2)}) async-start(bf16[16,128,256]{2,1,0:T(8,128)(2,1)} %bitcast.8), calls=%async_computation.1 | async-start | bytes 2097152 | tf_op jit(solution)/shard_map/all_to_all | solution.py:332

commit v4 on v3

--- a/solution.py
+++ b/solution.py
@@ -118,9 +118,11 @@
                     acc[rows, 0:HEAD_DIM] += key_part
                     acc[rows, HEAD_DIM : 2 * HEAD_DIM] += value_part
         src = lax.rem(lax.axis_index(X) - x + 4, 4)
-        dq[src] = (query_sum * FACTOR).astype(jnp.bfloat16).reshape(4, CAP, HEAD_DIM)
-    for p in range(4):
-        q_out[p][...] = dq[p]
+        query_out = (query_sum * FACTOR).astype(jnp.bfloat16)
+        for o in range(4):
+            dq[o, src] = query_out[CAP * o : CAP * (o + 1), :]
+    for o in range(4):
+        q_out[o][...] = dq[o]
     d_own[:, 0:HEAD_DIM] = a_own[:, 0:HEAD_DIM] * FACTOR
     d_own[:, HEAD_DIM:] = a_own[:, HEAD_DIM:]
     d_oth[:, 0:HEAD_DIM] = (a_oth[:, 0:HEAD_DIM] * FACTOR).astype(jnp.bfloat16)
@@ -254,33 +256,40 @@
     return out[0].reshape(16, TOK, 2 * HEAD_DIM), out[1:]
 
 
-def unpack_kernel(parts, key_grad, value_grad, k_buf, v_buf, sems):
-    sides = ((k_buf, key_grad, 0), (v_buf, value_grad, HEAD_DIM))
+def finish_kernel(parts, q0, q1, q2, q3, key_grad, value_grad, query_grad, k_buf, v_buf, q_buf, sems):
     copies = []
-    for n, (buf, out, at) in enumerate(sides):
+    for n, (buf, out, at) in enumerate(((k_buf, key_grad, 0), (v_buf, value_grad, HEAD_DIM))):
         for x in range(4):
             total = sum(parts[4 * x + z, :, at : at + HEAD_DIM].astype(jnp.float32) for z in range(4))
             buf[:, x * HEAD_DIM : (x + 1) * HEAD_DIM] = total.astype(jnp.bfloat16)
         copies.append(pltpu.make_async_copy(buf, out, sems.at[n]))
         copies[n].start()
+    depth, here = lax.axis_index("rec"), lax.axis_index(X)
+    for p, ref in enumerate((q0, q1, q2, q3)):
+        for o in range(4):
+            head = lax.rem(depth + o, 4) * 4 + lax.rem(here + p, 4)
+            q_buf[:, pl.ds(pl.multiple_of(head * HEAD_DIM, HEAD_DIM), HEAD_DIM)] = ref[o]
+    copies.append(pltpu.make_async_copy(q_buf, query_grad.at[0], sems.at[2]))
+    copies[2].start()
     for copy in copies:
         copy.wait()
 
 
-def unpack(parts):
+def finish(parts, dq):
     out = jax.ShapeDtypeStruct((TOK, 4 * HEAD_DIM), jnp.bfloat16)
     return pl.pallas_call(
-        unpack_kernel,
-        out_shape=(out, out),
-        in_specs=[pl.BlockSpec(memory_space=pltpu.VMEM)],
-        out_specs=(pl.BlockSpec(memory_space=pl.ANY),) * 2,
+        finish_kernel,
+        out_shape=(out, out, jax.ShapeDtypeStruct((1, CAP, HEADS * HEAD_DIM), jnp.bfloat16)),
+        in_specs=[VMEM] * 5,
+        out_specs=(pl.BlockSpec(memory_space=pl.ANY),) * 3,
         scratch_shapes=[
             pltpu.VMEM((TOK, 4 * HEAD_DIM), jnp.bfloat16),
             pltpu.VMEM((TOK, 4 * HEAD_DIM), jnp.bfloat16),
-            pltpu.SemaphoreType.DMA((2,)),
+            pltpu.VMEM((CAP, HEADS * HEAD_DIM), jnp.bfloat16),
+            pltpu.SemaphoreType.DMA((3,)),
         ],
         compiler_params=pltpu.CompilerParams(vmem_limit_bytes=8 * 2**20),
-    )(parts)
+    )(parts, *dq)
 
 
 def add_kernel(own, mine, out, buf, sems):
@@ -314,7 +323,7 @@
 
 
 def gradients(queries, grad_out, keys, values, surv_index, counts):
-    depth, here = lax.axis_index("rec"), lax.axis_index(X)
+    here = lax.axis_index(X)
     kv, by_depth = pack(keys, values, queries, grad_out, surv_index, counts)
     kv = lax.all_to_all(kv, (X, Z), 0, 0, tiled=True).reshape(16 * TOK, 2 * HEAD_DIM)
     kv_other = swap_cores(kv)
@@ -330,14 +339,9 @@
     mine = swap_cores(d_other)
     sums = added(d_own, mine)
     sums = lax.all_to_all(sums.reshape(16, TOK, 2 * HEAD_DIM), (X, Z), 0, 0, tiled=True)
-    back = []
-    for p in range(4):
-        back.append(moved(dq[p], X, -p))
-    dq = back
-    dq = [moved(jnp.stack([dq[p][o] for p in range(4)]), "rec", -o) for o in range(4)]
-    dq = jnp.roll(jnp.stack(dq), (depth, here), (0, 1))
-    query_grad = dq.reshape(HEADS, CAP, HEAD_DIM).transpose(1, 0, 2).reshape(1, CAP, HEADS * HEAD_DIM)
-    key_grad, value_grad = unpack(sums)
+    dq = [moved(dq[o], "rec", -o) for o in range(4)]
+    dq = [moved(jnp.stack([dq[o][p] for o in range(4)]), X, -p) for p in range(4)]
+    key_grad, value_grad, query_grad = finish(sums, dq)
     return query_grad, key_grad, value_grad
 
 

time: 84.5 us -> 78 us (0.923)
  waiting for transfers between devices: 27.7 us -> 19.1 us
  starting transfers between devices: 21.4 us -> 23.7 us
    all_to_all x1, waiting for transfers between devices: 12.1 us -> 1.96 us  [gradients(): lax.all_to_all(sums.reshape(16, TOK, 2 * HEAD_DIM), (X, Z), 0, 0, tiled=T...]
    ppermute x12, waiting for transfers between devices: 15.6 us -> 17.1 us  [moved(): lax.ppermute(a, axis, [(i, (i + by) % 4) for i in range(4)])]
    ppermute x12, starting transfers between devices: 17.5 us -> 18.8 us  [moved(): lax.ppermute(a, axis, [(i, (i + by) % 4) for i in range(4)])]
    all_to_all x1, starting transfers between devices: 3.89 us -> 4.81 us  [gradients(): lax.all_to_all(sums.reshape(16, TOK, 2 * HEAD_DIM), (X, Z), 0, 0, tiled=T...]
  transfers between devices with their start and end apart: 15 -> 15, of which waited for: 12 -> 9; matrix products, arithmetic and copies ran while one was open for 1% -> 0% of each run, Pallas kernels for 1% -> 3%
where the time goes in v4:
time: 78 us; the launch traced here: 77.2 us
  blocking collectives  24.6 us (32%)
  starting transfers between devices  23.7 us (30%)
  waiting for transfers between devices  19.1 us (24%)
  Pallas kernels  8.86 us (11%)
    all_to_all x1, blocking collectives, gradients(): lax.all_to_all(kv, (X, Z), 0, 0, tiled=True).reshape(16 * TOK, 2 * HEAD_DIM)  24.6 us
    ppermute x12, starting transfers between devices, moved(): lax.ppermute(a, axis, [(i, (i + by) % 4) for i in range(4)])  18.8 us
    ppermute x12, waiting for transfers between devices, moved(): lax.ppermute(a, axis, [(i, (i + by) % 4) for i in range(4)])  17.1 us
    all_to_all x1, starting transfers between devices, gradients(): lax.all_to_all(sums.reshape(16, TOK, 2 * HEAD_DIM), (X, Z), 0, 0, tiled=T...  4.81 us
    pallas_call x1, Pallas kernels, attention_second(): pl.pallas_call(second_kernel, out_shape=(jax.ShapeDtypeStruct((4, CAP, HE...  4.38 us
    all_to_all x1, waiting for transfers between devices, gradients(): lax.all_to_all(sums.reshape(16, TOK, 2 * HEAD_DIM), (X, Z), 0, 0, tiled=T...  1.96 us
  transfers between devices with their start and end apart: 15, of which 9 were waited for; matrix products, arithmetic and copies ran while one was open for 0% of the time, Pallas kernels for 3%

profile of v4, /device:TPU:0, one launch (start us, length us, event | category | flops | bytes accessed | tf_op | source)
XLA Modules:
  0.0 77.2 jit_solution(3317166081552526327)
XLA Ops:
  0.6 1.3 %shard_map.85 = (bf16[4,4,128,256]{3,2,1,0:T(8,128)(2,1)S(1)}, bf16[4,72,128]{2,1,0:T(8,128)(2,1)S(1)}, bf16[4,72,128]{2,1,0:T(8,128)(2,1)S(1)}, bf16[4,72,128]{2,1,0:T(8,128)(2,1)S(1)}, bf16[4,72,128]{2,1,0:T(8,128)(2,1)S(1)}) custom-call(bf16[128,2048]{1,0:T(8,128)(2,1)} %keys.1, bf16[128,2048]{1,0:T(8,128)(2,1)} %values.1, bf16[1,32,2048]{2,1,0:T(8,128)(2,1)} %queries.1, ...), custom_call_target="tpu_custom_call" | custom-call | tf_op jit(solution)/shard_map/pallas_call | solution.py:238
  1.9 24.6 %all_to_all.10 = bf16[16,128,256]{2,1,0:T(8,128)(2,1)S(1)} all-to-all(bf16[16,128,256]{2,1,0:T(8,128)(2,1)S(1)} %bitcast.6), channel_id=1, replica_groups=mesh['rec'=4,'ctx_0'=4,'ctx_1'=4,'ctx_2'=2] {'ctx_0','ctx_1'}, dimensions={0} | all-to-all | bytes 2097152 | tf_op jit(solution)/shard_map/all_to_all | solution.py:328
  26.6 0.0 collective-permute-start.6
  26.6 1.6 %collective-permute-start = (bf16[4,72,128]{2,1,0:T(8,128)(2,1)S(1)}, bf16[4,72,128]{2,1,0:T(8,128)(2,1)S(1)}, u32[]{:S(2)}, u32[]{:S(2)}) collective-permute-start(bf16[4,72,128]{2,1,0:T(8,128)(2,1)S(1)} %get-tuple-element.21), channel_id=1, source_target_pairs={{0,32},{32,64},{64,96},{96,0},{1,33},{33,65},{65,97},{97,1},{2,34}... | collective-permute-start | bytes 221192 | tf_op jit(solution)/shard_map/ppermute | solution.py:318
  28.2 2.9 %collective-permute-start.1 = (bf16[4,72,128]{2,1,0:T(8,128)(2,1)S(1)}, bf16[4,72,128]{2,1,0:T(8,128)(2,1)S(1)}, u32[]{:S(2)}, u32[]{:S(2)}) collective-permute-start(bf16[4,72,128]{2,1,0:T(8,128)(2,1)S(1)} %get-tuple-element.22), channel_id=1, source_target_pairs={{0,64},{32,96},{64,0},{96,32},{1,65},{33,97},{65,1},{97,33},{2,66}... | collective-permute-start | bytes 221192 | tf_op jit(solution)/shard_map/ppermute | solution.py:318
  31.1 1.3 %collective-permute-start.2 = (bf16[4,72,128]{2,1,0:T(8,128)(2,1)S(1)}, bf16[4,72,128]{2,1,0:T(8,128)(2,1)S(1)}, u32[]{:S(2)}, u32[]{:S(2)}) collective-permute-start(bf16[4,72,128]{2,1,0:T(8,128)(2,1)S(1)} %get-tuple-element.23), channel_id=1, source_target_pairs={{0,96},{32,0},{64,32},{96,64},{1,97},{33,1},{65,33},{97,65},{2,98}... | collective-permute-start | bytes 221192 | tf_op jit(solution)/shard_map/ppermute | solution.py:318
  32.4 0.1 collective-permute-done
  32.5 2.8 %collective-permute-done.1 = bf16[4,72,128]{2,1,0:T(8,128)(2,1)S(1)} collective-permute-done((bf16[4,72,128]{2,1,0:T(8,128)(2,1)S(1)}, bf16[4,72,128]{2,1,0:T(8,128)(2,1)S(1)}, u32[]{:S(2)}, u32[]{:S(2)}) %collective-permute-start.1) | collective-permute-done | bytes 73760 | tf_op jit(solution)/shard_map/ppermute | solution.py:318
  35.3 0.1 collective-permute-done.2
  35.4 0.2 collective-permute-start.3
  35.7 2.9 %collective-permute-start.4 = (bf16[4,72,128]{2,1,0:T(8,128)(2,1)S(1)}, bf16[4,72,128]{2,1,0:T(8,128)(2,1)S(1)}, u32[]{:S(2)}, u32[]{:S(2)}) collective-permute-start(bf16[4,72,128]{2,1,0:T(8,128)(2,1)S(1)} %pad_maximum_fusion.2), channel_id=1, source_target_pairs={{0,16},{8,24},{16,0},{24,8},{1,17},{9,25},{17,1},{25,9},{2,18},{10... | collective-permute-start | bytes 221192 | tf_op jit(solution)/shard_map/ppermute | solution.py:318
  38.5 1.1 %collective-permute-start.5 = (bf16[4,72,128]{2,1,0:T(8,128)(2,1)S(1)}, bf16[4,72,128]{2,1,0:T(8,128)(2,1)S(1)}, u32[]{:S(2)}, u32[]{:S(2)}) collective-permute-start(bf16[4,72,128]{2,1,0:T(8,128)(2,1)S(1)} %pad_maximum_fusion.3), channel_id=1, source_target_pairs={{0,24},{8,0},{16,8},{24,16},{1,25},{9,1},{17,9},{25,17},{2,26},{10... | collective-permute-start | bytes 221192 | tf_op jit(solution)/shard_map/ppermute | solution.py:318
  39.7 2.4 %collective-permute-done.3.q1.refs_1_ = bf16[4,72,128]{2,1,0:T(8,128)(2,1)S(1)} collective-permute-done((bf16[4,72,128]{2,1,0:T(8,128)(2,1)S(1)}, bf16[4,72,128]{2,1,0:T(8,128)(2,1)S(1)}, u32[]{:S(2)}, u32[]{:S(2)}) %collective-permute-start.3) | collective-permute-done | bytes 73760 | tf_op jit(solution)/shard_map/ppermute | solution.py:318
  42.0 0.0 collective-permute-done.4.q2.refs_2_
  42.0 0.9 %collective-permute-done.5.q3.refs_3_ = bf16[4,72,128]{2,1,0:T(8,128)(2,1)S(1)} collective-permute-done((bf16[4,72,128]{2,1,0:T(8,128)(2,1)S(1)}, bf16[4,72,128]{2,1,0:T(8,128)(2,1)S(1)}, u32[]{:S(2)}, u32[]{:S(2)}) %collective-permute-start.5) | collective-permute-done | bytes 73760 | tf_op jit(solution)/shard_map/ppermute | solution.py:318
  43.0 1.2 %shard_map.86 = (f32[5120,128]{1,0:T(8,128)S(1)}, f32[5120,128]{1,0:T(8,128)S(1)}, f32[32,128]{1,0:T(8,128)S(1)}) custom-call(bf16[4,72,128]{2,1,0:T(8,128)(2,1)S(1)} %pad_maximum_fusion.q0.refs_0_, bf16[4,72,128]{2,1,0:T(8,128)(2,1)S(1)} %collective-permute-done.3.q1.refs_1_, bf16[4,72,128]{2,1,0:T(8,128)(2,1)S(1)} %collective-permute-done.4.q2.refs_2_, ...), custom_call_target="tpu_custom_call" | custom-call | flops 335544320 | bytes 4194304 | tf_op jit(solution)/shard_map/pallas_call | solution.py:142
  44.2 0.0 collective-permute-done.6.refs_5_
  44.2 4.4 %shard_map.87 = (bf16[4,32,128]{2,1,0:T(8,128)(2,1)S(1)}, bf16[4,32,128]{2,1,0:T(8,128)(2,1)S(1)}, bf16[4,32,128]{2,1,0:T(8,128)(2,1)S(1)}, bf16[4,32,128]{2,1,0...) custom-call(bf16[4,72,128]{2,1,0:T(8,128)(2,1)S(1)} %pad_maximum_fusion.q0.refs_0_, ...), custom_call_target="tpu_custom_call" | custom-call | flops 1342177280 | bytes 10485760 | tf_op jit(solution)/shard_map/pallas_call | solution.py:161
  48.6 0.1 collective-permute-start.7
  48.7 2.6 %collective-permute-start.8 = (bf16[4,32,128]{2,1,0:T(8,128)(2,1)S(1)}, bf16[4,32,128]{2,1,0:T(8,128)(2,1)S(1)}, u32[]{:S(2)}, u32[]{:S(2)}) collective-permute-start(bf16[4,32,128]{2,1,0:T(8,128)(2,1)S(1)} %get-tuple-element.31), channel_id=1, source_target_pairs={{0,96},{32,0},{64,32},{96,64},{1,97},{33,1},{65,33},{97,65},{2,98}... | collective-permute-start | bytes 98312 | tf_op jit(solution)/shard_map/ppermute | solution.py:318
  51.3 0.5 collective-permute-start.9
  51.8 0.7 collective-permute-start.10
  52.6 1.1 %shard_map.88 = bf16[2048,256]{1,0:T(8,128)(2,1)} custom-call(f32[2048,256]{1,0:T(8,128)S(1)} %get-tuple-element.28.own, bf16[2048,256]{1,0:T(8,128)(2,1)S(1)} %collective-permute-done.7.mine), custom_call_target="tpu_custom_call" | custom-call | tf_op jit(solution)/shard_map/pallas_call | solution.py:307
  53.7 4.8 %all-to-all-start.1 = ((bf16[16,128,256]{2,1,0:T(8,128)(2,1)}), bf16[16,128,256]{2,1,0:T(8,128)(2,1)S(1)}, u32[]{:S(2)}, u32[]{:S(2)}) async-start(bf16[16,128,256]{2,1,0:T(8,128)(2,1)} %bitcast.2), calls=%async_computation.1 | async-start | bytes 2097152 | tf_op jit(solution)/shard_map/all_to_all | solution.py:341
  58.6 3.2 %collective-permute-start.11 = (bf16[4,32,128]{2,1,0:T(8,128)(2,1)S(1)}, bf16[4,32,128]{2,1,0:T(8,128)(2,1)S(1)}, u32[]{:S(2)}, u32[]{:S(2)}) collective-permute-start(bf16[4,32,128]{2,1,0:T(8,128)(2,1)S(1)} %pad_maximum_fusion.5), channel_id=1, source_target_pairs={{0,24},{8,0},{16,8},{24,16},{1,25},{9,1},{17,9},{25,17},{2,26},{10... | collective-permute-start | bytes 98312 | tf_op jit(solution)/shard_map/ppermute | solution.py:318
  61.8 0.9 %collective-permute-start.12 = (bf16[4,32,128]{2,1,0:T(8,128)(2,1)S(1)}, bf16[4,32,128]{2,1,0:T(8,128)(2,1)S(1)}, u32[]{:S(2)}, u32[]{:S(2)}) collective-permute-start(bf16[4,32,128]{2,1,0:T(8,128)(2,1)S(1)} %pad_maximum_fusion.6), channel_id=1, source_target_pairs={{0,16},{8,24},{16,0},{24,8},{1,17},{9,25},{17,1},{25,9},{2,18},{10... | collective-permute-start | bytes 98312 | tf_op jit(solution)/shard_map/ppermute | solution.py:318
  62.7 0.9 %collective-permute-start.13 = (bf16[4,32,128]{2,1,0:T(8,128)(2,1)S(1)}, bf16[4,32,128]{2,1,0:T(8,128)(2,1)S(1)}, u32[]{:S(2)}, u32[]{:S(2)}) collective-permute-start(bf16[4,32,128]{2,1,0:T(8,128)(2,1)S(1)} %pad_maximum_fusion.7), channel_id=1, source_target_pairs={{0,8},{8,16},{16,24},{24,0},{1,9},{9,17},{17,25},{25,1},{2,10},{10... | collective-permute-start | bytes 98312 | tf_op jit(solution)/shard_map/ppermute | solution.py:318
  63.5 9.3 %collective-permute-done.11.q1 = bf16[4,32,128]{2,1,0:T(8,128)(2,1)S(1)} collective-permute-done((bf16[4,32,128]{2,1,0:T(8,128)(2,1)S(1)}, bf16[4,32,128]{2,1,0:T(8,128)(2,1)S(1)}, u32[]{:S(2)}, u32[]{:S(2)}) %collective-permute-start.11) | collective-permute-done | bytes 32800 | tf_op jit(solution)/shard_map/ppermute | solution.py:318
  72.8 1.5 %collective-permute-done.12.q2 = bf16[4,32,128]{2,1,0:T(8,128)(2,1)S(1)} collective-permute-done((bf16[4,32,128]{2,1,0:T(8,128)(2,1)S(1)}, bf16[4,32,128]{2,1,0:T(8,128)(2,1)S(1)}, u32[]{:S(2)}, u32[]{:S(2)}) %collective-permute-start.12) | collective-permute-done | bytes 32800 | tf_op jit(solution)/shard_map/ppermute | solution.py:318
  74.3 0.1 collective-permute-done.13.q3
  74.4 2.0 %all-to-all-done.1.parts = bf16[16,128,256]{2,1,0:T(8,128)(2,1)S(1)} async-done(((bf16[16,128,256]{2,1,0:T(8,128)(2,1)}), bf16[16,128,256]{2,1,0:T(8,128)(2,1)S(1)}, u32[]{:S(2)}, u32[]{:S(2)}) %all-to-all-start.1) | async-done | bytes 1048608 | tf_op jit(solution)/shard_map/all_to_all | solution.py:341
  76.3 0.9 %shard_map.89 = (bf16[128,512]{1,0:T(8,128)(2,1)}, bf16[128,512]{1,0:T(8,128)(2,1)}, bf16[1,32,2048]{2,1,0:T(8,128)(2,1)}) custom-call(bf16[16,128,256]{2,1,0:T(8,128)(2,1)S(1)} %all-to-all-done.1.parts, bf16[4,32,128]{2,1,0:T(8,128)(2,1)S(1)} %pad_maximum_fusion.4.q0, bf16[4,32,128]{2,1,0:T(8,128)(2,1)S(1)} %collective-permute-done.11.q1, ...), custom_call_target="tpu_custom_call" | custom-call | tf_op jit(solution)/shard_map/pallas_call | solution.py:280
  (20 shorter events, 0.1 us)
Async XLA Ops:
  26.6 17.6 %collective-permute-start.6 = (bf16[2048,256]{1,0:T(8,128)(2,1)S(1)}, bf16[2048,256]{1,0:T(8,128)(2,1)S(1)}, u32[]{:S(2)}, u32[]{:S(2)}) collective-permute-start(bf16[2048,256]{1,0:T(8,128)(2,1)S(1)} %bitcast.3), channel_id=1, source_target_pairs={{0,1},{1,0},{2,3},{3,2},{4,5},{5,4},{6,7},{7,6},{8,9},{9,8},{10,11... | collective-permute-start | bytes 3145736 | tf_op jit(solution)/shard_map/ppermute | solution.py:322
  26.6 6.0 %collective-permute-start = (bf16[4,72,128]{2,1,0:T(8,128)(2,1)S(1)}, bf16[4,72,128]{2,1,0:T(8,128)(2,1)S(1)}, u32[]{:S(2)}, u32[]{:S(2)}) collective-permute-start(bf16[4,72,128]{2,1,0:T(8,128)(2,1)S(1)} %get-tuple-element.21), channel_id=1, source_target_pairs={{0,32},{32,64},{64,96},{96,0},{1,33},{33,65},{65,97},{97,1},{2,34}... | collective-permute-start | bytes 221192 | tf_op jit(solution)/shard_map/ppermute | solution.py:318
  28.2 7.1 %collective-permute-start.1 = (bf16[4,72,128]{2,1,0:T(8,128)(2,1)S(1)}, bf16[4,72,128]{2,1,0:T(8,128)(2,1)S(1)}, u32[]{:S(2)}, u32[]{:S(2)}) collective-permute-start(bf16[4,72,128]{2,1,0:T(8,128)(2,1)S(1)} %get-tuple-element.22), channel_id=1, source_target_pairs={{0,64},{32,96},{64,0},{96,32},{1,65},{33,97},{65,1},{97,33},{2,66}... | collective-permute-start | bytes 221192 | tf_op jit(solution)/shard_map/ppermute | solution.py:318
  31.1 4.4 %collective-permute-start.2 = (bf16[4,72,128]{2,1,0:T(8,128)(2,1)S(1)}, bf16[4,72,128]{2,1,0:T(8,128)(2,1)S(1)}, u32[]{:S(2)}, u32[]{:S(2)}) collective-permute-start(bf16[4,72,128]{2,1,0:T(8,128)(2,1)S(1)} %get-tuple-element.23), channel_id=1, source_target_pairs={{0,96},{32,0},{64,32},{96,64},{1,97},{33,1},{65,33},{97,65},{2,98}... | collective-permute-start | bytes 221192 | tf_op jit(solution)/shard_map/ppermute | solution.py:318
  35.4 6.6 %collective-permute-start.3 = (bf16[4,72,128]{2,1,0:T(8,128)(2,1)S(1)}, bf16[4,72,128]{2,1,0:T(8,128)(2,1)S(1)}, u32[]{:S(2)}, u32[]{:S(2)}) collective-permute-start(bf16[4,72,128]{2,1,0:T(8,128)(2,1)S(1)} %pad_maximum_fusion.1), channel_id=1, source_target_pairs={{0,8},{8,16},{16,24},{24,0},{1,9},{9,17},{17,25},{25,1},{2,10},{10... | collective-permute-start | bytes 221192 | tf_op jit(solution)/shard_map/ppermute | solution.py:318
  35.7 6.4 %collective-permute-start.4 = (bf16[4,72,128]{2,1,0:T(8,128)(2,1)S(1)}, bf16[4,72,128]{2,1,0:T(8,128)(2,1)S(1)}, u32[]{:S(2)}, u32[]{:S(2)}) collective-permute-start(bf16[4,72,128]{2,1,0:T(8,128)(2,1)S(1)} %pad_maximum_fusion.2), channel_id=1, source_target_pairs={{0,16},{8,24},{16,0},{24,8},{1,17},{9,25},{17,1},{25,9},{2,18},{10... | collective-permute-start | bytes 221192 | tf_op jit(solution)/shard_map/ppermute | solution.py:318
  38.5 4.4 %collective-permute-start.5 = (bf16[4,72,128]{2,1,0:T(8,128)(2,1)S(1)}, bf16[4,72,128]{2,1,0:T(8,128)(2,1)S(1)}, u32[]{:S(2)}, u32[]{:S(2)}) collective-permute-start(bf16[4,72,128]{2,1,0:T(8,128)(2,1)S(1)} %pad_maximum_fusion.3), channel_id=1, source_target_pairs={{0,24},{8,0},{16,8},{24,16},{1,25},{9,1},{17,9},{25,17},{2,26},{10... | collective-permute-start | bytes 221192 | tf_op jit(solution)/shard_map/ppermute | solution.py:318
  48.6 4.0 %collective-permute-start.7 = (bf16[2048,256]{1,0:T(8,128)(2,1)S(1)}, bf16[2048,256]{1,0:T(8,128)(2,1)S(1)}, u32[]{:S(2)}, u32[]{:S(2)}) collective-permute-start(bf16[2048,256]{1,0:T(8,128)(2,1)S(1)} %get-tuple-element.29), channel_id=1, source_target_pairs={{0,1},{1,0},{2,3},{3,2},{4,5},{5,4},{6,7},{7,6},{8,9},{9,8},{10,11... | collective-permute-start | bytes 3145736 | tf_op jit(solution)/shard_map/ppermute | solution.py:322
  48.7 9.8 %collective-permute-start.8 = (bf16[4,32,128]{2,1,0:T(8,128)(2,1)S(1)}, bf16[4,32,128]{2,1,0:T(8,128)(2,1)S(1)}, u32[]{:S(2)}, u32[]{:S(2)}) collective-permute-start(bf16[4,32,128]{2,1,0:T(8,128)(2,1)S(1)} %get-tuple-element.31), channel_id=1, source_target_pairs={{0,96},{32,0},{64,32},{96,64},{1,97},{33,1},{65,33},{97,65},{2,98}... | collective-permute-start | bytes 98312 | tf_op jit(solution)/shard_map/ppermute | solution.py:318
  51.3 7.2 %collective-permute-start.9 = (bf16[4,32,128]{2,1,0:T(8,128)(2,1)S(1)}, bf16[4,32,128]{2,1,0:T(8,128)(2,1)S(1)}, u32[]{:S(2)}, u32[]{:S(2)}) collective-permute-start(bf16[4,32,128]{2,1,0:T(8,128)(2,1)S(1)} %get-tuple-element.32), channel_id=1, source_target_pairs={{0,64},{32,96},{64,0},{96,32},{1,65},{33,97},{65,1},{97,33},{2,66}... | collective-permute-start | bytes 98312 | tf_op jit(solution)/shard_map/ppermute | solution.py:318
  51.8 6.7 %collective-permute-start.10 = (bf16[4,32,128]{2,1,0:T(8,128)(2,1)S(1)}, bf16[4,32,128]{2,1,0:T(8,128)(2,1)S(1)}, u32[]{:S(2)}, u32[]{:S(2)}) collective-permute-start(bf16[4,32,128]{2,1,0:T(8,128)(2,1)S(1)} %get-tuple-element.33), channel_id=1, source_target_pairs={{0,32},{32,64},{64,96},{96,0},{1,33},{33,65},{65,97},{97,1},{2,34}... | collective-permute-start | bytes 98312 | tf_op jit(solution)/shard_map/ppermute | solution.py:318
  53.7 22.6 %all-to-all-start.1 = ((bf16[16,128,256]{2,1,0:T(8,128)(2,1)}), bf16[16,128,256]{2,1,0:T(8,128)(2,1)S(1)}, u32[]{:S(2)}, u32[]{:S(2)}) async-start(bf16[16,128,256]{2,1,0:T(8,128)(2,1)} %bitcast.2), calls=%async_computation.1 | async-start | bytes 2097152 | tf_op jit(solution)/shard_map/all_to_all | solution.py:341
  58.6 14.3 %collective-permute-start.11 = (bf16[4,32,128]{2,1,0:T(8,128)(2,1)S(1)}, bf16[4,32,128]{2,1,0:T(8,128)(2,1)S(1)}, u32[]{:S(2)}, u32[]{:S(2)}) collective-permute-start(bf16[4,32,128]{2,1,0:T(8,128)(2,1)S(1)} %pad_maximum_fusion.5), channel_id=1, source_target_pairs={{0,24},{8,0},{16,8},{24,16},{1,25},{9,1},{17,9},{25,17},{2,26},{10... | collective-permute-start | bytes 98312 | tf_op jit(solution)/shard_map/ppermute | solution.py:318
  61.8 12.5 %collective-permute-start.12 = (bf16[4,32,128]{2,1,0:T(8,128)(2,1)S(1)}, bf16[4,32,128]{2,1,0:T(8,128)(2,1)S(1)}, u32[]{:S(2)}, u32[]{:S(2)}) collective-permute-start(bf16[4,32,128]{2,1,0:T(8,128)(2,1)S(1)} %pad_maximum_fusion.6), channel_id=1, source_target_pairs={{0,16},{8,24},{16,0},{24,8},{1,17},{9,25},{17,1},{25,9},{2,18},{10... | collective-permute-start | bytes 98312 | tf_op jit(solution)/shard_map/ppermute | solution.py:318
  62.7 11.7 %collective-permute-start.13 = (bf16[4,32,128]{2,1,0:T(8,128)(2,1)S(1)}, bf16[4,32,128]{2,1,0:T(8,128)(2,1)S(1)}, u32[]{:S(2)}, u32[]{:S(2)}) collective-permute-start(bf16[4,32,128]{2,1,0:T(8,128)(2,1)S(1)} %pad_maximum_fusion.7), channel_id=1, source_target_pairs={{0,8},{8,16},{16,24},{24,0},{1,9},{9,17},{17,25},{25,1},{2,10},{10... | collective-permute-start | bytes 98312 | tf_op jit(solution)/shard_map/ppermute | solution.py:318

commit v5 on v4

--- a/solution.py
+++ b/solution.py
@@ -84,14 +84,14 @@
 
 
 def second_kernel(*refs):
-    q_in, (own, oth, e_own, w_own, stats) = refs[0:4], refs[4:9]
-    q_out, (d_own, d_oth) = refs[9:13], refs[13:15]
-    qg, dq, e_buf, w_buf, a_own, a_oth = refs[15:]
+    q_in, (oth, own, e_own, w_own, stats) = refs[0:4], refs[4:9]
+    q_out, (d_oth, ds_own, wb_own) = refs[9:13], refs[13:16]
+    qg, dq, e_buf, w_buf, acc = refs[16:]
     for p in range(4):
         qg[p] = q_in[p][...]
     for x in reversed(range(GROUPS)):
         q, g, slot_pos = group_operands(qg, x)
-        at = pl.ds(x * (x + 1) // 2 * CHUNK, (x + 1) * CHUNK)
+        first = x * (x + 1) // 2 * CHUNK
         top, total, weighted = exponentials(oth, 1 - lax.axis_index(C), x, q, g, slot_pos, e_buf, w_buf)
         own_top, own_total, own_weighted = (stats[8 * x + n : 8 * x + n + 1, :] for n in range(3))
         joint = jnp.maximum(top, own_top)
@@ -100,33 +100,52 @@
         scale = 1.0 / (total * oth_scale + own_total * own_scale)
         delta = (weighted * oth_scale + own_weighted * own_scale) * scale
         query_sum = jnp.zeros((TOK, HEAD_DIM), jnp.float32)
-        for ref, acc, e_ref, w_ref, factor in (
-            (oth, a_oth, e_buf, w_buf, oth_scale * scale),
-            (own, a_own, e_own.at[at], w_own.at[at], own_scale * scale),
-        ):
-            for k in range(x + 1):
-                rows = slice(k * CHUNK, (k + 1) * CHUNK)
-                w = e_ref[rows, :] * factor
-                ds = (w * (w_ref[rows, :] - delta)).astype(jnp.bfloat16)
-                query_sum = query_sum + dot(ds, ref[rows, 0:HEAD_DIM], TN)
-                key_part = dot(ds, q, NN)
-                value_part = dot(w.astype(jnp.bfloat16), g, NN)
-                if x == GROUPS - 1:
-                    acc[rows, 0:HEAD_DIM] = key_part
-                    acc[rows, HEAD_DIM : 2 * HEAD_DIM] = value_part
-                else:
-                    acc[rows, 0:HEAD_DIM] += key_part
-                    acc[rows, HEAD_DIM : 2 * HEAD_DIM] += value_part
+        for k in range(x + 1):
+            rows = slice(k * CHUNK, (k + 1) * CHUNK)
+            w = e_buf[rows, :] * (oth_scale * scale)
+            ds = (w * (w_buf[rows, :] - delta)).astype(jnp.bfloat16)
+            query_sum = query_sum + dot(ds, oth[rows, 0:HEAD_DIM], TN)
+            key_part = dot(ds, q, NN)
+            value_part = dot(w.astype(jnp.bfloat16), g, NN)
+            if x == GROUPS - 1:
+                acc[rows, 0:HEAD_DIM] = key_part
+                acc[rows, HEAD_DIM : 2 * HEAD_DIM] = value_part
+            else:
+                acc[rows, 0:HEAD_DIM] += key_part
+                acc[rows, HEAD_DIM : 2 * HEAD_DIM] += value_part
+        for k in range(x + 1):
+            at = slice(first + k * CHUNK, first + (k + 1) * CHUNK)
+            w = e_own[at, :] * (own_scale * scale)
+            ds = (w * (w_own[at, :] - delta)).astype(jnp.bfloat16)
+            query_sum = query_sum + dot(ds, own[k * CHUNK : (k + 1) * CHUNK, 0:HEAD_DIM], TN)
+            ds_own[at, :] = ds
+            wb_own[at, :] = w.astype(jnp.bfloat16)
         src = lax.rem(lax.axis_index(X) - x + 4, 4)
         query_out = (query_sum * FACTOR).astype(jnp.bfloat16)
         for o in range(4):
             dq[o, src] = query_out[CAP * o : CAP * (o + 1), :]
     for o in range(4):
         q_out[o][...] = dq[o]
-    d_own[:, 0:HEAD_DIM] = a_own[:, 0:HEAD_DIM] * FACTOR
-    d_own[:, HEAD_DIM:] = a_own[:, HEAD_DIM:]
-    d_oth[:, 0:HEAD_DIM] = (a_oth[:, 0:HEAD_DIM] * FACTOR).astype(jnp.bfloat16)
-    d_oth[:, HEAD_DIM:] = a_oth[:, HEAD_DIM:].astype(jnp.bfloat16)
+    d_oth[:, 0:HEAD_DIM] = (acc[:, 0:HEAD_DIM] * FACTOR).astype(jnp.bfloat16)
+    d_oth[:, HEAD_DIM:] = acc[:, HEAD_DIM:].astype(jnp.bfloat16)
+
+
+def third_kernel(q0, q1, q2, q3, ds_own, wb_own, d_own, qg):
+    for p, ref in enumerate((q0, q1, q2, q3)):
+        qg[p] = ref[...]
+    for x in reversed(range(GROUPS)):
+        q, g, _ = group_operands(qg, x)
+        for k in range(x + 1):
+            rows = slice(k * CHUNK, (k + 1) * CHUNK)
+            at = slice(x * (x + 1) // 2 * CHUNK + k * CHUNK, x * (x + 1) // 2 * CHUNK + (k + 1) * CHUNK)
+            key_part = dot(ds_own[at, :], q, NN)
+            value_part = dot(wb_own[at, :], g, NN)
+            if x == GROUPS - 1:
+                d_own[rows, 0:HEAD_DIM] = key_part
+                d_own[rows, HEAD_DIM : 2 * HEAD_DIM] = value_part
+            else:
+                d_own[rows, 0:HEAD_DIM] += key_part
+                d_own[rows, HEAD_DIM : 2 * HEAD_DIM] += value_part
 
 
 VMEM = pl.BlockSpec(memory_space=pltpu.VMEM)
@@ -162,25 +181,39 @@
         second_kernel,
         out_shape=(jax.ShapeDtypeStruct((4, CAP, HEAD_DIM), jnp.bfloat16),) * 4
         + (
-            jax.ShapeDtypeStruct((keys, 2 * HEAD_DIM), jnp.float32),
             jax.ShapeDtypeStruct((keys, 2 * HEAD_DIM), jnp.bfloat16),
+            jax.ShapeDtypeStruct((PAIRS, TOK), jnp.bfloat16),
+            jax.ShapeDtypeStruct((PAIRS, TOK), jnp.bfloat16),
         ),
         in_specs=[VMEM] * 9,
-        out_specs=(VMEM,) * 6,
+        out_specs=(VMEM,) * 7,
         scratch_shapes=[
             pltpu.VMEM((4, 4, QG_ROWS, HEAD_DIM), jnp.bfloat16),
             pltpu.VMEM((4, 4, CAP, HEAD_DIM), jnp.bfloat16),
             pltpu.VMEM((keys, TOK), jnp.float32),
             pltpu.VMEM((keys, TOK), jnp.float32),
             pltpu.VMEM((keys, 2 * HEAD_DIM), jnp.float32),
-            pltpu.VMEM((keys, 2 * HEAD_DIM), jnp.float32),
         ],
-        compiler_params=kernel_params(24),
+        compiler_params=kernel_params(20),
         cost_estimate=pl.CostEstimate(
-            flops=2 * 8 * PAIRS * TOK * HEAD_DIM, bytes_accessed=10 * 2**20, transcendentals=PAIRS * TOK
-        ),
-    )(*qg, own, oth, *found)
-    return out[0:4], out[4], out[5]
+            flops=2 * 6 * PAIRS * TOK * HEAD_DIM, bytes_accessed=10 * 2**20, transcendentals=PAIRS * TOK
+        ),
+    )(*qg, oth, own, *found)
+    return out[0:4], out[4], out[5:7]
+
+
+def attention_third(qg, products):
+    return pl.pallas_call(
+        third_kernel,
+        out_shape=jax.ShapeDtypeStruct((GROUPS * CHUNK, 2 * HEAD_DIM), jnp.float32),
+        in_specs=[VMEM] * 6,
+        out_specs=VMEM,
+        scratch_shapes=[pltpu.VMEM((4, 4, QG_ROWS, HEAD_DIM), jnp.bfloat16)],
+        compiler_params=kernel_params(12),
+        cost_estimate=pl.CostEstimate(
+            flops=2 * 2 * PAIRS * TOK * HEAD_DIM, bytes_accessed=5 * 2**20, transcendentals=0
+        ),
+    )(*qg, *products)
 
 
 def pack_kernel(keys, values, queries, grad_out, surv_index, counts, kv, *rest):
@@ -296,7 +329,9 @@
     copies = []
     for k in range(GROUPS):
         rows = slice(k * CHUNK, (k + 1) * CHUNK)
-        buf[rows, :] = (own[rows, :] + mine[rows, :].astype(jnp.float32)).astype(jnp.bfloat16)
+        other = mine[rows, :].astype(jnp.float32)
+        buf[rows, 0:HEAD_DIM] = (own[rows, 0:HEAD_DIM] * FACTOR + other[:, 0:HEAD_DIM]).astype(jnp.bfloat16)
+        buf[rows, HEAD_DIM:] = (own[rows, HEAD_DIM:] + other[:, HEAD_DIM:]).astype(jnp.bfloat16)
         copies.append(pltpu.make_async_copy(buf.at[rows], out.at[rows], sems.at[k]))
         copies[k].start()
     for copy in copies:
@@ -335,8 +370,9 @@
 
     qg = [moved(for_x(p), X, p) for p in range(4)]
     found = attention_first(qg, kv)
-    dq, d_own, d_other = attention_second(qg, kv, kv_other, found)
+    dq, d_other, products = attention_second(qg, kv, kv_other, found)
     mine = swap_cores(d_other)
+    d_own = attention_third(qg, products)
     sums = added(d_own, mine)
     sums = lax.all_to_all(sums.reshape(16, TOK, 2 * HEAD_DIM), (X, Z), 0, 0, tiled=True)
     dq = [moved(dq[o], "rec", -o) for o in range(4)]

time: 78 us -> 78.2 us (level)
    pallas_call x0 -> x1, Pallas kernels: none -> 0.85 us  [attention_third(): pl.pallas_call(third_kernel, out_shape=jax.ShapeDtypeStruct((GROUPS * CHU...]
  transfers between devices with their start and end apart: 15 -> 15, of which waited for: 9 -> 9; matrix products, arithmetic and copies ran while one was open for 0% -> 0% of each run, Pallas kernels for 3% -> 4%
where the time goes in v5:
time: 78.2 us; the launch traced here: 77.4 us
  blocking collectives  24.6 us (31%)
  starting transfers between devices  23.7 us (30%)
  waiting for transfers between devices  19.1 us (24%)
  Pallas kernels  9.08 us (12%)
    all_to_all x1, blocking collectives, gradients(): lax.all_to_all(kv, (X, Z), 0, 0, tiled=True).reshape(16 * TOK, 2 * HEAD_DIM)  24.6 us
    ppermute x12, starting transfers between devices, moved(): lax.ppermute(a, axis, [(i, (i + by) % 4) for i in range(4)])  18.8 us
    ppermute x12, waiting for transfers between devices, moved(): lax.ppermute(a, axis, [(i, (i + by) % 4) for i in range(4)])  17.1 us
    all_to_all x1, starting transfers between devices, gradients(): lax.all_to_all(sums.reshape(16, TOK, 2 * HEAD_DIM), (X, Z), 0, 0, tiled=T...  4.81 us
    pallas_call x1, Pallas kernels, attention_second(): pl.pallas_call(second_kernel, out_shape=(jax.ShapeDtypeStruct((4, CAP, HE...  3.72 us
    all_to_all x1, waiting for transfers between devices, gradients(): lax.all_to_all(sums.reshape(16, TOK, 2 * HEAD_DIM), (X, Z), 0, 0, tiled=T...  1.96 us
  transfers between devices with their start and end apart: 15, of which 9 were waited for; matrix products, arithmetic and copies ran while one was open for 0% of the time, Pallas kernels for 4%

profile of v5, /device:TPU:0, one launch (start us, length us, event | category | flops | bytes accessed | tf_op | source)
XLA Modules:
  0.0 77.4 jit_solution(13072861052636781070)
XLA Ops:
  0.6 1.3 %shard_map.85 = (bf16[4,4,128,256]{3,2,1,0:T(8,128)(2,1)S(1)}, bf16[4,72,128]{2,1,0:T(8,128)(2,1)S(1)}, bf16[4,72,128]{2,1,0:T(8,128)(2,1)S(1)}, bf16[4,72,128]{2,1,0:T(8,128)(2,1)S(1)}, bf16[4,72,128]{2,1,0:T(8,128)(2,1)S(1)}) custom-call(bf16[128,2048]{1,0:T(8,128)(2,1)} %keys.1, bf16[128,2048]{1,0:T(8,128)(2,1)} %values.1, bf16[1,32,2048]{2,1,0:T(8,128)(2,1)} %queries.1, ...), custom_call_target="tpu_custom_call" | custom-call | tf_op jit(solution)/shard_map/pallas_call | solution.py:271
  1.9 24.6 %all_to_all.10 = bf16[16,128,256]{2,1,0:T(8,128)(2,1)S(1)} all-to-all(bf16[16,128,256]{2,1,0:T(8,128)(2,1)S(1)} %bitcast.6), channel_id=1, replica_groups=mesh['rec'=4,'ctx_0'=4,'ctx_1'=4,'ctx_2'=2] {'ctx_0','ctx_1'}, dimensions={0} | all-to-all | bytes 2097152 | tf_op jit(solution)/shard_map/all_to_all | solution.py:363
  26.6 0.0 collective-permute-start.6
  26.6 1.6 %collective-permute-start = (bf16[4,72,128]{2,1,0:T(8,128)(2,1)S(1)}, bf16[4,72,128]{2,1,0:T(8,128)(2,1)S(1)}, u32[]{:S(2)}, u32[]{:S(2)}) collective-permute-start(bf16[4,72,128]{2,1,0:T(8,128)(2,1)S(1)} %get-tuple-element.22), channel_id=1, source_target_pairs={{0,32},{32,64},{64,96},{96,0},{1,33},{33,65},{65,97},{97,1},{2,34}... | collective-permute-start | bytes 221192 | tf_op jit(solution)/shard_map/ppermute | solution.py:353
  28.2 2.9 %collective-permute-start.1 = (bf16[4,72,128]{2,1,0:T(8,128)(2,1)S(1)}, bf16[4,72,128]{2,1,0:T(8,128)(2,1)S(1)}, u32[]{:S(2)}, u32[]{:S(2)}) collective-permute-start(bf16[4,72,128]{2,1,0:T(8,128)(2,1)S(1)} %get-tuple-element.23), channel_id=1, source_target_pairs={{0,64},{32,96},{64,0},{96,32},{1,65},{33,97},{65,1},{97,33},{2,66}... | collective-permute-start | bytes 221192 | tf_op jit(solution)/shard_map/ppermute | solution.py:353
  31.1 1.3 %collective-permute-start.2 = (bf16[4,72,128]{2,1,0:T(8,128)(2,1)S(1)}, bf16[4,72,128]{2,1,0:T(8,128)(2,1)S(1)}, u32[]{:S(2)}, u32[]{:S(2)}) collective-permute-start(bf16[4,72,128]{2,1,0:T(8,128)(2,1)S(1)} %get-tuple-element.24), channel_id=1, source_target_pairs={{0,96},{32,0},{64,32},{96,64},{1,97},{33,1},{65,33},{97,65},{2,98}... | collective-permute-start | bytes 221192 | tf_op jit(solution)/shard_map/ppermute | solution.py:353
  32.4 0.1 collective-permute-done
  32.5 2.8 %collective-permute-done.1 = bf16[4,72,128]{2,1,0:T(8,128)(2,1)S(1)} collective-permute-done((bf16[4,72,128]{2,1,0:T(8,128)(2,1)S(1)}, bf16[4,72,128]{2,1,0:T(8,128)(2,1)S(1)}, u32[]{:S(2)}, u32[]{:S(2)}) %collective-permute-start.1) | collective-permute-done | bytes 73760 | tf_op jit(solution)/shard_map/ppermute | solution.py:353
  35.3 0.1 collective-permute-done.2
  35.4 0.2 collective-permute-start.3
  35.7 2.9 %collective-permute-start.4 = (bf16[4,72,128]{2,1,0:T(8,128)(2,1)S(1)}, bf16[4,72,128]{2,1,0:T(8,128)(2,1)S(1)}, u32[]{:S(2)}, u32[]{:S(2)}) collective-permute-start(bf16[4,72,128]{2,1,0:T(8,128)(2,1)S(1)} %pad_maximum_fusion.2), channel_id=1, source_target_pairs={{0,16},{8,24},{16,0},{24,8},{1,17},{9,25},{17,1},{25,9},{2,18},{10... | collective-permute-start | bytes 221192 | tf_op jit(solution)/shard_map/ppermute | solution.py:353
  38.5 1.1 %collective-permute-start.5 = (bf16[4,72,128]{2,1,0:T(8,128)(2,1)S(1)}, bf16[4,72,128]{2,1,0:T(8,128)(2,1)S(1)}, u32[]{:S(2)}, u32[]{:S(2)}) collective-permute-start(bf16[4,72,128]{2,1,0:T(8,128)(2,1)S(1)} %pad_maximum_fusion.3), channel_id=1, source_target_pairs={{0,24},{8,0},{16,8},{24,16},{1,25},{9,1},{17,9},{25,17},{2,26},{10... | collective-permute-start | bytes 221192 | tf_op jit(solution)/shard_map/ppermute | solution.py:353
  39.7 2.4 %collective-permute-done.3.q1.refs_1_ = bf16[4,72,128]{2,1,0:T(8,128)(2,1)S(1)} collective-permute-done((bf16[4,72,128]{2,1,0:T(8,128)(2,1)S(1)}, bf16[4,72,128]{2,1,0:T(8,128)(2,1)S(1)}, u32[]{:S(2)}, u32[]{:S(2)}) %collective-permute-start.3) | collective-permute-done | bytes 73760 | tf_op jit(solution)/shard_map/ppermute | solution.py:353
  42.0 0.0 collective-permute-done.4.q2.refs_2_
  42.0 0.9 %collective-permute-done.5.q3.refs_3_ = bf16[4,72,128]{2,1,0:T(8,128)(2,1)S(1)} collective-permute-done((bf16[4,72,128]{2,1,0:T(8,128)(2,1)S(1)}, bf16[4,72,128]{2,1,0:T(8,128)(2,1)S(1)}, u32[]{:S(2)}, u32[]{:S(2)}) %collective-permute-start.5) | collective-permute-done | bytes 73760 | tf_op jit(solution)/shard_map/ppermute | solution.py:353
  43.0 1.2 %shard_map.86 = (f32[5120,128]{1,0:T(8,128)S(1)}, f32[5120,128]{1,0:T(8,128)S(1)}, f32[32,128]{1,0:T(8,128)S(1)}) custom-call(bf16[4,72,128]{2,1,0:T(8,128)(2,1)S(1)} %pad_maximum_fusion.q0.refs_0_, bf16[4,72,128]{2,1,0:T(8,128)(2,1)S(1)} %collective-permute-done.3.q1.refs_1_, bf16[4,72,128]{2,1,0:T(8,128)(2,1)S(1)} %collective-permute-done.4.q2.refs_2_, ...), custom_call_target="tpu_custom_call" | custom-call | flops 335544320 | bytes 4194304 | tf_op jit(solution)/shard_map/pallas_call | solution.py:161
  44.2 3.7 %shard_map.87 = (bf16[4,32,128]{2,1,0:T(8,128)(2,1)S(1)}, bf16[4,32,128]{2,1,0:T(8,128)(2,1)S(1)}, bf16[4,32,128]{2,1,0:T(8,128)(2,1)S(1)}, bf16[4,32,128]{2,1,0...) custom-call(bf16[4,72,128]{2,1,0:T(8,128)(2,1)S(1)} %pad_maximum_fus, ...), custom_call_target="tpu_custom_call" | custom-call | flops 1006632960 | bytes 10485760 | tf_op jit(solution)/shard_map/pallas_call | solution.py:180
  47.9 0.1 collective-permute-start.7
  48.0 2.6 %collective-permute-start.8 = (bf16[4,32,128]{2,1,0:T(8,128)(2,1)S(1)}, bf16[4,32,128]{2,1,0:T(8,128)(2,1)S(1)}, u32[]{:S(2)}, u32[]{:S(2)}) collective-permute-start(bf16[4,32,128]{2,1,0:T(8,128)(2,1)S(1)} %get-tuple-element.33), channel_id=1, source_target_pairs={{0,96},{32,0},{64,32},{96,64},{1,97},{33,1},{65,33},{97,65},{2,98}... | collective-permute-start | bytes 98312 | tf_op jit(solution)/shard_map/ppermute | solution.py:353
  50.6 0.5 collective-permute-start.9
  51.2 0.7 collective-permute-start.10
  51.9 0.9 %shard_map.88.own = f32[2048,256]{1,0:T(8,128)S(1)} custom-call(bf16[4,72,128]{2,1,0:T(8,128)(2,1)S(1)} %pad_maximum_fusion.q0.refs_0_, bf16[4,72,128]{2,1,0:T(8,128)(2,1)S(1)} %collective-permute-done.3.q1.refs_1_, bf16[4,72,128]{2,1,0:T(8,128)(2,1)S(1)} %collective-permute-done.4.q2.refs_2_, bf16[4,72,128]{2,1,0:T(8,128)(2,1)S(1)} %collective-permute-done.5.q3.refs_3_, ...), custom_call_target="tpu_custom_call" | custom-call | flops 335544320 | bytes 5242880 | tf_op jit(solution)/shard_map/pallas_call | solution.py:206
  52.8 1.1 %shard_map.89 = bf16[2048,256]{1,0:T(8,128)(2,1)} custom-call(f32[2048,256]{1,0:T(8,128)S(1)} %shard_map.88.own, bf16[2048,256]{1,0:T(8,128)(2,1)S(1)} %collective-permute-done.7.mine), custom_call_target="tpu_custom_call" | custom-call | tf_op jit(solution)/shard_map/pallas_call | solution.py:342
  53.9 4.8 %all-to-all-start.1 = ((bf16[16,128,256]{2,1,0:T(8,128)(2,1)}), bf16[16,128,256]{2,1,0:T(8,128)(2,1)S(1)}, u32[]{:S(2)}, u32[]{:S(2)}) async-start(bf16[16,128,256]{2,1,0:T(8,128)(2,1)} %bitcast.2), calls=%async_computation.1 | async-start | bytes 2097152 | tf_op jit(solution)/shard_map/all_to_all | solution.py:377
  58.8 3.2 %collective-permute-start.11 = (bf16[4,32,128]{2,1,0:T(8,128)(2,1)S(1)}, bf16[4,32,128]{2,1,0:T(8,128)(2,1)S(1)}, u32[]{:S(2)}, u32[]{:S(2)}) collective-permute-start(bf16[4,32,128]{2,1,0:T(8,128)(2,1)S(1)} %pad_maximum_fusion.5), channel_id=1, source_target_pairs={{0,24},{8,0},{16,8},{24,16},{1,25},{9,1},{17,9},{25,17},{2,26},{10... | collective-permute-start | bytes 98312 | tf_op jit(solution)/shard_map/ppermute | solution.py:353
  62.0 0.9 %collective-permute-start.12 = (bf16[4,32,128]{2,1,0:T(8,128)(2,1)S(1)}, bf16[4,32,128]{2,1,0:T(8,128)(2,1)S(1)}, u32[]{:S(2)}, u32[]{:S(2)}) collective-permute-start(bf16[4,32,128]{2,1,0:T(8,128)(2,1)S(1)} %pad_maximum_fusion.6), channel_id=1, source_target_pairs={{0,16},{8,24},{16,0},{24,8},{1,17},{9,25},{17,1},{25,9},{2,18},{10... | collective-permute-start | bytes 98312 | tf_op jit(solution)/shard_map/ppermute | solution.py:353
  62.9 0.9 %collective-permute-start.13 = (bf16[4,32,128]{2,1,0:T(8,128)(2,1)S(1)}, bf16[4,32,128]{2,1,0:T(8,128)(2,1)S(1)}, u32[]{:S(2)}, u32[]{:S(2)}) collective-permute-start(bf16[4,32,128]{2,1,0:T(8,128)(2,1)S(1)} %pad_maximum_fusion.7), channel_id=1, source_target_pairs={{0,8},{8,16},{16,24},{24,0},{1,9},{9,17},{17,25},{25,1},{2,10},{10... | collective-permute-start | bytes 98312 | tf_op jit(solution)/shard_map/ppermute | solution.py:353
  63.8 9.3 %collective-permute-done.11.q1 = bf16[4,32,128]{2,1,0:T(8,128)(2,1)S(1)} collective-permute-done((bf16[4,32,128]{2,1,0:T(8,128)(2,1)S(1)}, bf16[4,32,128]{2,1,0:T(8,128)(2,1)S(1)}, u32[]{:S(2)}, u32[]{:S(2)}) %collective-permute-start.11) | collective-permute-done | bytes 32800 | tf_op jit(solution)/shard_map/ppermute | solution.py:353
  73.1 1.5 %collective-permute-done.12.q2 = bf16[4,32,128]{2,1,0:T(8,128)(2,1)S(1)} collective-permute-done((bf16[4,32,128]{2,1,0:T(8,128)(2,1)S(1)}, bf16[4,32,128]{2,1,0:T(8,128)(2,1)S(1)}, u32[]{:S(2)}, u32[]{:S(2)}) %collective-permute-start.12) | collective-permute-done | bytes 32800 | tf_op jit(solution)/shard_map/ppermute | solution.py:353
  74.5 0.1 collective-permute-done.13.q3
  74.6 2.0 %all-to-all-done.1.parts = bf16[16,128,256]{2,1,0:T(8,128)(2,1)S(1)} async-done(((bf16[16,128,256]{2,1,0:T(8,128)(2,1)}), bf16[16,128,256]{2,1,0:T(8,128)(2,1)S(1)}, u32[]{:S(2)}, u32[]{:S(2)}) %all-to-all-start.1) | async-done | bytes 1048608 | tf_op jit(solution)/shard_map/all_to_all | solution.py:377
  76.5 0.9 %shard_map.90 = (bf16[128,512]{1,0:T(8,128)(2,1)}, bf16[128,512]{1,0:T(8,128)(2,1)}, bf16[1,32,2048]{2,1,0:T(8,128)(2,1)}) custom-call(bf16[16,128,256]{2,1,0:T(8,128)(2,1)S(1)} %all-to-all-done.1.parts, bf16[4,32,128]{2,1,0:T(8,128)(2,1)S(1)} %pad_maximum_fusion.4.q0, bf16[4,32,128]{2,1,0:T(8,128)(2,1)S(1)} %collective-permute-done.11.q1, ...), custom_call_target="tpu_custom_call" | custom-call | tf_op jit(solution)/shard_map/pallas_call | solution.py:313
  (21 shorter events, 0.1 us)
Async XLA Ops:
  26.6 17.6 %collective-permute-start.6 = (bf16[2048,256]{1,0:T(8,128)(2,1)S(1)}, bf16[2048,256]{1,0:T(8,128)(2,1)S(1)}, u32[]{:S(2)}, u32[]{:S(2)}) collective-permute-start(bf16[2048,256]{1,0:T(8,128)(2,1)S(1)} %bitcast.3), channel_id=1, source_target_pairs={{0,1},{1,0},{2,3},{3,2},{4,5},{5,4},{6,7},{7,6},{8,9},{9,8},{10,11... | collective-permute-start | bytes 3145736 | tf_op jit(solution)/shard_map/ppermute | solution.py:357
  26.6 6.0 %collective-permute-start = (bf16[4,72,128]{2,1,0:T(8,128)(2,1)S(1)}, bf16[4,72,128]{2,1,0:T(8,128)(2,1)S(1)}, u32[]{:S(2)}, u32[]{:S(2)}) collective-permute-start(bf16[4,72,128]{2,1,0:T(8,128)(2,1)S(1)} %get-tuple-element.22), channel_id=1, source_target_pairs={{0,32},{32,64},{64,96},{96,0},{1,33},{33,65},{65,97},{97,1},{2,34}... | collective-permute-start | bytes 221192 | tf_op jit(solution)/shard_map/ppermute | solution.py:353
  28.2 7.1 %collective-permute-start.1 = (bf16[4,72,128]{2,1,0:T(8,128)(2,1)S(1)}, bf16[4,72,128]{2,1,0:T(8,128)(2,1)S(1)}, u32[]{:S(2)}, u32[]{:S(2)}) collective-permute-start(bf16[4,72,128]{2,1,0:T(8,128)(2,1)S(1)} %get-tuple-element.23), channel_id=1, source_target_pairs={{0,64},{32,96},{64,0},{96,32},{1,65},{33,97},{65,1},{97,33},{2,66}... | collective-permute-start | bytes 221192 | tf_op jit(solution)/shard_map/ppermute | solution.py:353
  31.1 4.4 %collective-permute-start.2 = (bf16[4,72,128]{2,1,0:T(8,128)(2,1)S(1)}, bf16[4,72,128]{2,1,0:T(8,128)(2,1)S(1)}, u32[]{:S(2)}, u32[]{:S(2)}) collective-permute-start(bf16[4,72,128]{2,1,0:T(8,128)(2,1)S(1)} %get-tuple-element.24), channel_id=1, source_target_pairs={{0,96},{32,0},{64,32},{96,64},{1,97},{33,1},{65,33},{97,65},{2,98}... | collective-permute-start | bytes 221192 | tf_op jit(solution)/shard_map/ppermute | solution.py:353
  35.4 6.6 %collective-permute-start.3 = (bf16[4,72,128]{2,1,0:T(8,128)(2,1)S(1)}, bf16[4,72,128]{2,1,0:T(8,128)(2,1)S(1)}, u32[]{:S(2)}, u32[]{:S(2)}) collective-permute-start(bf16[4,72,128]{2,1,0:T(8,128)(2,1)S(1)} %pad_maximum_fusion.1), channel_id=1, source_target_pairs={{0,8},{8,16},{16,24},{24,0},{1,9},{9,17},{17,25},{25,1},{2,10},{10... | collective-permute-start | bytes 221192 | tf_op jit(solution)/shard_map/ppermute | solution.py:353
  35.7 6.4 %collective-permute-start.4 = (bf16[4,72,128]{2,1,0:T(8,128)(2,1)S(1)}, bf16[4,72,128]{2,1,0:T(8,128)(2,1)S(1)}, u32[]{:S(2)}, u32[]{:S(2)}) collective-permute-start(bf16[4,72,128]{2,1,0:T(8,128)(2,1)S(1)} %pad_maximum_fusion.2), channel_id=1, source_target_pairs={{0,16},{8,24},{16,0},{24,8},{1,17},{9,25},{17,1},{25,9},{2,18},{10... | collective-permute-start | bytes 221192 | tf_op jit(solution)/shard_map/ppermute | solution.py:353
  38.5 4.4 %collective-permute-start.5 = (bf16[4,72,128]{2,1,0:T(8,128)(2,1)S(1)}, bf16[4,72,128]{2,1,0:T(8,128)(2,1)S(1)}, u32[]{:S(2)}, u32[]{:S(2)}) collective-permute-start(bf16[4,72,128]{2,1,0:T(8,128)(2,1)S(1)} %pad_maximum_fusion.3), channel_id=1, source_target_pairs={{0,24},{8,0},{16,8},{24,16},{1,25},{9,1},{17,9},{25,17},{2,26},{10... | collective-permute-start | bytes 221192 | tf_op jit(solution)/shard_map/ppermute | solution.py:353
  47.9 4.9 %collective-permute-start.7 = (bf16[2048,256]{1,0:T(8,128)(2,1)S(1)}, bf16[2048,256]{1,0:T(8,128)(2,1)S(1)}, u32[]{:S(2)}, u32[]{:S(2)}) collective-permute-start(bf16[2048,256]{1,0:T(8,128)(2,1)S(1)} %get-tuple-element.31), channel_id=1, source_target_pairs={{0,1},{1,0},{2,3},{3,2},{4,5},{5,4},{6,7},{7,6},{8,9},{9,8},{10,11... | collective-permute-start | bytes 3145736 | tf_op jit(solution)/shard_map/ppermute | solution.py:357
  48.0 10.7 %collective-permute-start.8 = (bf16[4,32,128]{2,1,0:T(8,128)(2,1)S(1)}, bf16[4,32,128]{2,1,0:T(8,128)(2,1)S(1)}, u32[]{:S(2)}, u32[]{:S(2)}) collective-permute-start(bf16[4,32,128]{2,1,0:T(8,128)(2,1)S(1)} %get-tuple-element.33), channel_id=1, source_target_pairs={{0,96},{32,0},{64,32},{96,64},{1,97},{33,1},{65,33},{97,65},{2,98}... | collective-permute-start | bytes 98312 | tf_op jit(solution)/shard_map/ppermute | solution.py:353
  50.6 8.1 %collective-permute-start.9 = (bf16[4,32,128]{2,1,0:T(8,128)(2,1)S(1)}, bf16[4,32,128]{2,1,0:T(8,128)(2,1)S(1)}, u32[]{:S(2)}, u32[]{:S(2)}) collective-permute-start(bf16[4,32,128]{2,1,0:T(8,128)(2,1)S(1)} %get-tuple-element.34), channel_id=1, source_target_pairs={{0,64},{32,96},{64,0},{96,32},{1,65},{33,97},{65,1},{97,33},{2,66}... | collective-permute-start | bytes 98312 | tf_op jit(solution)/shard_map/ppermute | solution.py:353
  51.2 7.6 %collective-permute-start.10 = (bf16[4,32,128]{2,1,0:T(8,128)(2,1)S(1)}, bf16[4,32,128]{2,1,0:T(8,128)(2,1)S(1)}, u32[]{:S(2)}, u32[]{:S(2)}) collective-permute-start(bf16[4,32,128]{2,1,0:T(8,128)(2,1)S(1)} %get-tuple-element.35), channel_id=1, source_target_pairs={{0,32},{32,64},{64,96},{96,0},{1,33},{33,65},{65,97},{97,1},{2,34}... | collective-permute-start | bytes 98312 | tf_op jit(solution)/shard_map/ppermute | solution.py:353
  53.9 22.6 %all-to-all-start.1 = ((bf16[16,128,256]{2,1,0:T(8,128)(2,1)}), bf16[16,128,256]{2,1,0:T(8,128)(2,1)S(1)}, u32[]{:S(2)}, u32[]{:S(2)}) async-start(bf16[16,128,256]{2,1,0:T(8,128)(2,1)} %bitcast.2), calls=%async_computation.1 | async-start | bytes 2097152 | tf_op jit(solution)/shard_map/all_to_all | solution.py:377
  58.8 14.3 %collective-permute-start.11 = (bf16[4,32,128]{2,1,0:T(8,128)(2,1)S(1)}, bf16[4,32,128]{2,1,0:T(8,128)(2,1)S(1)}, u32[]{:S(2)}, u32[]{:S(2)}) collective-permute-start(bf16[4,32,128]{2,1,0:T(8,128)(2,1)S(1)} %pad_maximum_fusion.5), channel_id=1, source_target_pairs={{0,24},{8,0},{16,8},{24,16},{1,25},{9,1},{17,9},{25,17},{2,26},{10... | collective-permute-start | bytes 98312 | tf_op jit(solution)/shard_map/ppermute | solution.py:353
  62.0 12.5 %collective-permute-start.12 = (bf16[4,32,128]{2,1,0:T(8,128)(2,1)S(1)}, bf16[4,32,128]{2,1,0:T(8,128)(2,1)S(1)}, u32[]{:S(2)}, u32[]{:S(2)}) collective-permute-start(bf16[4,32,128]{2,1,0:T(8,128)(2,1)S(1)} %pad_maximum_fusion.6), channel_id=1, source_target_pairs={{0,16},{8,24},{16,0},{24,8},{1,17},{9,25},{17,1},{25,9},{2,18},{10... | collective-permute-start | bytes 98312 | tf_op jit(solution)/shard_map/ppermute | solution.py:353
  62.9 11.7 %collective-permute-start.13 = (bf16[4,32,128]{2,1,0:T(8,128)(2,1)S(1)}, bf16[4,32,128]{2,1,0:T(8,128)(2,1)S(1)}, u32[]{:S(2)}, u32[]{:S(2)}) collective-permute-start(bf16[4,32,128]{2,1,0:T(8,128)(2,1)S(1)} %pad_maximum_fusion.7), channel_id=1, source_target_pairs={{0,8},{8,16},{16,24},{24,0},{1,9},{9,17},{17,25},{25,1},{2,10},{10... | collective-permute-start | bytes 98312 | tf_op jit(solution)/shard_map/ppermute | solution.py:353

commit v6 on v5

--- a/solution.py
+++ b/solution.py
@@ -220,32 +220,29 @@
     qg, (k_buf, v_buf, kv_buf, q_buf, g_buf, s_buf, c_buf, sems) = rest[0:4], rest[4:]
     depth = lax.axis_index("rec")
     ctx = lax.axis_index(X) * 8 + lax.axis_index(Z) * 2 + lax.axis_index(C)
-    mine = pl.ds(pl.multiple_of(depth * 4 * HEAD_DIM, 4 * HEAD_DIM), 4 * HEAD_DIM)
-    copies = [
-        pltpu.make_async_copy(src, dst, sems.at[n])
-        for n, (src, dst) in enumerate(
-            (
-                (keys.at[:, mine], k_buf),
-                (values.at[:, mine], v_buf),
-                (queries.at[0], q_buf),
-                (grad_out.at[0], g_buf),
-                (surv_index, s_buf),
-                (counts, c_buf),
-            )
-        )
-    ]
+    half = 2 * HEAD_DIM
+    pairs = []
+    for h in range(2):
+        mine = pl.ds(pl.multiple_of((2 * depth + h) * half, half), half)
+        pairs.append((keys.at[:, mine], k_buf.at[:, h * half : (h + 1) * half]))
+        pairs.append((values.at[:, mine], v_buf.at[:, h * half : (h + 1) * half]))
+    pairs += [(queries.at[0], q_buf), (grad_out.at[0], g_buf), (surv_index, s_buf), (counts, c_buf)]
+    copies = [pltpu.make_async_copy(src, dst, sems.at[n]) for n, (src, dst) in enumerate(pairs)]
     for copy in copies:
         copy.start()
-    copies[0].wait()
-    copies[1].wait()
-    for x in range(4):
-        cols = slice(x * HEAD_DIM, (x + 1) * HEAD_DIM)
-        kv_buf[x, :, 0:HEAD_DIM] = k_buf[:, cols]
-        kv_buf[x, :, HEAD_DIM:] = v_buf[:, cols]
-    out = [pltpu.make_async_copy(kv_buf, kv.at[:, z], sems.at[6 + z]) for z in range(4)]
-    for copy in out:
-        copy.start()
-    for copy in copies[2:]:
+    out = []
+    for h in range(2):
+        copies[2 * h].wait()
+        copies[2 * h + 1].wait()
+        for x in range(2 * h, 2 * h + 2):
+            cols = slice(x * HEAD_DIM, (x + 1) * HEAD_DIM)
+            kv_buf[x, :, 0:HEAD_DIM] = k_buf[:, cols]
+            kv_buf[x, :, HEAD_DIM:] = v_buf[:, cols]
+        part = slice(2 * h, 2 * h + 2)
+        for z in range(4):
+            out.append(pltpu.make_async_copy(kv_buf.at[part], kv.at[part, z], sems.at[8 + 4 * h + z]))
+            out[-1].start()
+    for copy in copies[4:]:
         copy.wait()
     live = lax.broadcasted_iota(jnp.int32, (CAP, HEAD_DIM), 0) < c_buf[0, ctx]
     quarter = lax.rem(ctx, 4)
@@ -282,7 +279,7 @@
             pltpu.VMEM((CAP, HEADS * HEAD_DIM), jnp.bfloat16),
             pltpu.VMEM(surv_index.shape, jnp.int32),
             pltpu.SMEM(counts.shape, jnp.int32),
-            pltpu.SemaphoreType.DMA((10,)),
+            pltpu.SemaphoreType.DMA((16,)),
         ],
         compiler_params=pltpu.CompilerParams(vmem_limit_bytes=8 * 2**20),
     )(*(pltpu.with_memory_space_constraint(a, pltpu.HBM) for a in (keys, values, queries, grad_out, surv_index, counts)))
@@ -375,8 +372,12 @@
     d_own = attention_third(qg, products)
     sums = added(d_own, mine)
     sums = lax.all_to_all(sums.reshape(16, TOK, 2 * HEAD_DIM), (X, Z), 0, 0, tiled=True)
-    dq = [moved(dq[o], "rec", -o) for o in range(4)]
-    dq = [moved(jnp.stack([dq[o][p] for o in range(4)]), X, -p) for p in range(4)]
+    back = []
+    for o in range(4):
+        back.append(moved(dq[o], "rec", -o))
+    dq = []
+    for p in range(4):
+        dq.append(moved(jnp.stack([back[o][p] for o in range(4)]), X, -p))
     key_grad, value_grad, query_grad = finish(sums, dq)
     return query_grad, key_grad, value_grad
 

time: 78.2 us -> 78.8 us (level)
  no operation moved by 1% of the time
where the time goes in v6:
time: 78.8 us; the launch traced here: 78 us
  blocking collectives  24.6 us (31%)
  starting transfers between devices  23.7 us (30%)
  waiting for transfers between devices  19.1 us (24%)
  Pallas kernels  9.65 us (12%)
    all_to_all x1, blocking collectives, gradients(): lax.all_to_all(kv, (X, Z), 0, 0, tiled=True).reshape(16 * TOK, 2 * HEAD_DIM)  24.6 us
    ppermute x12, starting transfers between devices, moved(): lax.ppermute(a, axis, [(i, (i + by) % 4) for i in range(4)])  18.8 us
    ppermute x12, waiting for transfers between devices, moved(): lax.ppermute(a, axis, [(i, (i + by) % 4) for i in range(4)])  17.1 us
    all_to_all x1, starting transfers between devices, gradients(): lax.all_to_all(sums.reshape(16, TOK, 2 * HEAD_DIM), (X, Z), 0, 0, tiled=T...  4.81 us
    pallas_call x1, Pallas kernels, attention_second(): pl.pallas_call(second_kernel, out_shape=(jax.ShapeDtypeStruct((4, CAP, HE...  3.72 us
    all_to_all x1, waiting for transfers between devices, gradients(): lax.all_to_all(sums.reshape(16, TOK, 2 * HEAD_DIM), (X, Z), 0, 0, tiled=T...  1.96 us
    pallas_call x1, Pallas kernels, pack(): pl.pallas_call(pack_kernel, out_shape=(jax.ShapeDtypeStruct((4, 4, TOK, 2...  1.87 us
  transfers between devices with their start and end apart: 15, of which 9 were waited for; matrix products, arithmetic and copies ran while one was open for 0% of the time, Pallas kernels for 4%

profile of v6, /device:TPU:0, one launch (start us, length us, event | category | flops | bytes accessed | tf_op | source)
XLA Modules:
  0.0 78.0 jit_solution(1394309667843758282)
XLA Ops:
  0.6 1.9 %shard_map.85 = (bf16[4,4,128,256]{3,2,1,0:T(8,128)(2,1)S(1)}, bf16[4,72,128]{2,1,0:T(8,128)(2,1)S(1)}, bf16[4,72,128]{2,1,0:T(8,128)(2,1)S(1)}, bf16[4,72,128]{2,1,0:T(8,128)(2,1)S(1)}, bf16[4,72,128]{2,1,0:T(8,128)(2,1)S(1)}) custom-call(bf16[128,2048]{1,0:T(8,128)(2,1)} %keys.1, bf16[128,2048]{1,0:T(8,128)(2,1)} %values.1, bf16[1,32,2048]{2,1,0:T(8,128)(2,1)} %queries.1, ...), custom_call_target="tpu_custom_call" | custom-call | tf_op jit(solution)/shard_map/pallas_call | solution.py:268
  2.5 24.6 %all_to_all.10 = bf16[16,128,256]{2,1,0:T(8,128)(2,1)S(1)} all-to-all(bf16[16,128,256]{2,1,0:T(8,128)(2,1)S(1)} %bitcast.6), channel_id=1, replica_groups=mesh['rec'=4,'ctx_0'=4,'ctx_1'=4,'ctx_2'=2] {'ctx_0','ctx_1'}, dimensions={0} | all-to-all | bytes 2097152 | tf_op jit(solution)/shard_map/all_to_all | solution.py:360
  27.1 1.6 %collective-permute-start = (bf16[4,72,128]{2,1,0:T(8,128)(2,1)S(1)}, bf16[4,72,128]{2,1,0:T(8,128)(2,1)S(1)}, u32[]{:S(2)}, u32[]{:S(2)}) collective-permute-start(bf16[4,72,128]{2,1,0:T(8,128)(2,1)S(1)} %get-tuple-element.22), channel_id=1, source_target_pairs={{0,32},{32,64},{64,96},{96,0},{1,33},{33,65},{65,97},{97,1},{2,34}... | collective-permute-start | bytes 221192 | tf_op jit(solution)/shard_map/ppermute | solution.py:350
  28.7 2.9 %collective-permute-start.1 = (bf16[4,72,128]{2,1,0:T(8,128)(2,1)S(1)}, bf16[4,72,128]{2,1,0:T(8,128)(2,1)S(1)}, u32[]{:S(2)}, u32[]{:S(2)}) collective-permute-start(bf16[4,72,128]{2,1,0:T(8,128)(2,1)S(1)} %get-tuple-element.23), channel_id=1, source_target_pairs={{0,64},{32,96},{64,0},{96,32},{1,65},{33,97},{65,1},{97,33},{2,66}... | collective-permute-start | bytes 221192 | tf_op jit(solution)/shard_map/ppermute | solution.py:350
  31.6 1.3 %collective-permute-start.2 = (bf16[4,72,128]{2,1,0:T(8,128)(2,1)S(1)}, bf16[4,72,128]{2,1,0:T(8,128)(2,1)S(1)}, u32[]{:S(2)}, u32[]{:S(2)}) collective-permute-start(bf16[4,72,128]{2,1,0:T(8,128)(2,1)S(1)} %get-tuple-element.24), channel_id=1, source_target_pairs={{0,96},{32,0},{64,32},{96,64},{1,97},{33,1},{65,33},{97,65},{2,98}... | collective-permute-start | bytes 221192 | tf_op jit(solution)/shard_map/ppermute | solution.py:350
  33.0 0.1 collective-permute-done
  33.1 2.8 %collective-permute-done.1 = bf16[4,72,128]{2,1,0:T(8,128)(2,1)S(1)} collective-permute-done((bf16[4,72,128]{2,1,0:T(8,128)(2,1)S(1)}, bf16[4,72,128]{2,1,0:T(8,128)(2,1)S(1)}, u32[]{:S(2)}, u32[]{:S(2)}) %collective-permute-start.1) | collective-permute-done | bytes 73760 | tf_op jit(solution)/shard_map/ppermute | solution.py:350
  35.9 0.1 collective-permute-done.2
  36.0 0.2 collective-permute-start.3
  36.2 2.9 %collective-permute-start.4 = (bf16[4,72,128]{2,1,0:T(8,128)(2,1)S(1)}, bf16[4,72,128]{2,1,0:T(8,128)(2,1)S(1)}, u32[]{:S(2)}, u32[]{:S(2)}) collective-permute-start(bf16[4,72,128]{2,1,0:T(8,128)(2,1)S(1)} %pad_maximum_fusion.2), channel_id=1, source_target_pairs={{0,16},{8,24},{16,0},{24,8},{1,17},{9,25},{17,1},{25,9},{2,18},{10... | collective-permute-start | bytes 221192 | tf_op jit(solution)/shard_map/ppermute | solution.py:350
  39.1 1.1 %collective-permute-start.5 = (bf16[4,72,128]{2,1,0:T(8,128)(2,1)S(1)}, bf16[4,72,128]{2,1,0:T(8,128)(2,1)S(1)}, u32[]{:S(2)}, u32[]{:S(2)}) collective-permute-start(bf16[4,72,128]{2,1,0:T(8,128)(2,1)S(1)} %pad_maximum_fusion.3), channel_id=1, source_target_pairs={{0,24},{8,0},{16,8},{24,16},{1,25},{9,1},{17,9},{25,17},{2,26},{10... | collective-permute-start | bytes 221192 | tf_op jit(solution)/shard_map/ppermute | solution.py:350
  40.2 2.4 %collective-permute-done.3.q1.refs_1_ = bf16[4,72,128]{2,1,0:T(8,128)(2,1)S(1)} collective-permute-done((bf16[4,72,128]{2,1,0:T(8,128)(2,1)S(1)}, bf16[4,72,128]{2,1,0:T(8,128)(2,1)S(1)}, u32[]{:S(2)}, u32[]{:S(2)}) %collective-permute-start.3) | collective-permute-done | bytes 73760 | tf_op jit(solution)/shard_map/ppermute | solution.py:350
  42.6 0.9 %collective-permute-done.5.q3.refs_3_ = bf16[4,72,128]{2,1,0:T(8,128)(2,1)S(1)} collective-permute-done((bf16[4,72,128]{2,1,0:T(8,128)(2,1)S(1)}, bf16[4,72,128]{2,1,0:T(8,128)(2,1)S(1)}, u32[]{:S(2)}, u32[]{:S(2)}) %collective-permute-start.5) | collective-permute-done | bytes 73760 | tf_op jit(solution)/shard_map/ppermute | solution.py:350
  43.5 1.2 %shard_map.86 = (f32[5120,128]{1,0:T(8,128)S(1)}, f32[5120,128]{1,0:T(8,128)S(1)}, f32[32,128]{1,0:T(8,128)S(1)}) custom-call(bf16[4,72,128]{2,1,0:T(8,128)(2,1)S(1)} %pad_maximum_fusion.q0.refs_0_, bf16[4,72,128]{2,1,0:T(8,128)(2,1)S(1)} %collective-permute-done.3.q1.refs_1_, bf16[4,72,128]{2,1,0:T(8,128)(2,1)S(1)} %collective-permute-done.4.q2.refs_2_, ...), custom_call_target="tpu_custom_call" | custom-call | flops 335544320 | bytes 4194304 | tf_op jit(solution)/shard_map/pallas_call | solution.py:161
  44.8 3.7 %shard_map.87 = (bf16[4,32,128]{2,1,0:T(8,128)(2,1)S(1)}, bf16[4,32,128]{2,1,0:T(8,128)(2,1)S(1)}, bf16[4,32,128]{2,1,0:T(8,128)(2,1)S(1)}, bf16[4,32,128]{2,1,0...) custom-call(bf16[4,72,128]{2,1,0:T(8,128)(2,1)S(1)} %pad_maximum_fus, ...), custom_call_target="tpu_custom_call" | custom-call | flops 1006632960 | bytes 10485760 | tf_op jit(solution)/shard_map/pallas_call | solution.py:180
  48.5 0.1 collective-permute-start.7
  48.6 2.6 %collective-permute-start.8 = (bf16[4,32,128]{2,1,0:T(8,128)(2,1)S(1)}, bf16[4,32,128]{2,1,0:T(8,128)(2,1)S(1)}, u32[]{:S(2)}, u32[]{:S(2)}) collective-permute-start(bf16[4,32,128]{2,1,0:T(8,128)(2,1)S(1)} %get-tuple-element.33), channel_id=1, source_target_pairs={{0,96},{32,0},{64,32},{96,64},{1,97},{33,1},{65,33},{97,65},{2,98}... | collective-permute-start | bytes 98312 | tf_op jit(solution)/shard_map/ppermute | solution.py:350
  51.2 0.5 collective-permute-start.9
  51.7 0.7 collective-permute-start.10
  52.5 0.9 %shard_map.88.own = f32[2048,256]{1,0:T(8,128)S(1)} custom-call(bf16[4,72,128]{2,1,0:T(8,128)(2,1)S(1)} %pad_maximum_fusion.q0.refs_0_, bf16[4,72,128]{2,1,0:T(8,128)(2,1)S(1)} %collective-permute-done.3.q1.refs_1_, bf16[4,72,128]{2,1,0:T(8,128)(2,1)S(1)} %collective-permute-done.4.q2.refs_2_, bf16[4,72,128]{2,1,0:T(8,128)(2,1)S(1)} %collective-permute-done.5.q3.refs_3_, ...), custom_call_target="tpu_custom_call" | custom-call | flops 335544320 | bytes 5242880 | tf_op jit(solution)/shard_map/pallas_call | solution.py:206
  53.3 0.0 collective-permute-done.7.mine
  53.3 1.1 %shard_map.89 = bf16[2048,256]{1,0:T(8,128)(2,1)} custom-call(f32[2048,256]{1,0:T(8,128)S(1)} %shard_map.88.own, bf16[2048,256]{1,0:T(8,128)(2,1)S(1)} %collective-permute-done.7.mine), custom_call_target="tpu_custom_call" | custom-call | tf_op jit(solution)/shard_map/pallas_call | solution.py:339
  54.5 4.8 %all-to-all-start.1 = ((bf16[16,128,256]{2,1,0:T(8,128)(2,1)}), bf16[16,128,256]{2,1,0:T(8,128)(2,1)S(1)}, u32[]{:S(2)}, u32[]{:S(2)}) async-start(bf16[16,128,256]{2,1,0:T(8,128)(2,1)} %bitcast.2), calls=%async_computation.1 | async-start | bytes 2097152 | tf_op jit(solution)/shard_map/all_to_all | solution.py:374
  59.3 0.0 collective-permute-done.10
  59.4 3.2 %collective-permute-start.11 = (bf16[4,32,128]{2,1,0:T(8,128)(2,1)S(1)}, bf16[4,32,128]{2,1,0:T(8,128)(2,1)S(1)}, u32[]{:S(2)}, u32[]{:S(2)}) collective-permute-start(bf16[4,32,128]{2,1,0:T(8,128)(2,1)S(1)} %pad_maximum_fusion.5), channel_id=1, source_target_pairs={{0,24},{8,0},{16,8},{24,16},{1,25},{9,1},{17,9},{25,17},{2,26},{10... | collective-permute-start | bytes 98312 | tf_op jit(solution)/shard_map/ppermute | solution.py:350
  62.6 0.9 %collective-permute-start.12 = (bf16[4,32,128]{2,1,0:T(8,128)(2,1)S(1)}, bf16[4,32,128]{2,1,0:T(8,128)(2,1)S(1)}, u32[]{:S(2)}, u32[]{:S(2)}) collective-permute-start(bf16[4,32,128]{2,1,0:T(8,128)(2,1)S(1)} %pad_maximum_fusion.6), channel_id=1, source_target_pairs={{0,16},{8,24},{16,0},{24,8},{1,17},{9,25},{17,1},{25,9},{2,18},{10... | collective-permute-start | bytes 98312 | tf_op jit(solution)/shard_map/ppermute | solution.py:350
  63.4 0.9 %collective-permute-start.13 = (bf16[4,32,128]{2,1,0:T(8,128)(2,1)S(1)}, bf16[4,32,128]{2,1,0:T(8,128)(2,1)S(1)}, u32[]{:S(2)}, u32[]{:S(2)}) collective-permute-start(bf16[4,32,128]{2,1,0:T(8,128)(2,1)S(1)} %pad_maximum_fusion.7), channel_id=1, source_target_pairs={{0,8},{8,16},{16,24},{24,0},{1,9},{9,17},{17,25},{25,1},{2,10},{10... | collective-permute-start | bytes 98312 | tf_op jit(solution)/shard_map/ppermute | solution.py:350
  64.3 9.3 %collective-permute-done.11.q1 = bf16[4,32,128]{2,1,0:T(8,128)(2,1)S(1)} collective-permute-done((bf16[4,32,128]{2,1,0:T(8,128)(2,1)S(1)}, bf16[4,32,128]{2,1,0:T(8,128)(2,1)S(1)}, u32[]{:S(2)}, u32[]{:S(2)}) %collective-permute-start.11) | collective-permute-done | bytes 32800 | tf_op jit(solution)/shard_map/ppermute | solution.py:350
  73.6 1.5 %collective-permute-done.12.q2 = bf16[4,32,128]{2,1,0:T(8,128)(2,1)S(1)} collective-permute-done((bf16[4,32,128]{2,1,0:T(8,128)(2,1)S(1)}, bf16[4,32,128]{2,1,0:T(8,128)(2,1)S(1)}, u32[]{:S(2)}, u32[]{:S(2)}) %collective-permute-start.12) | collective-permute-done | bytes 32800 | tf_op jit(solution)/shard_map/ppermute | solution.py:350
  75.1 0.1 collective-permute-done.13.q3
  75.1 2.0 %all-to-all-done.1.parts = bf16[16,128,256]{2,1,0:T(8,128)(2,1)S(1)} async-done(((bf16[16,128,256]{2,1,0:T(8,128)(2,1)}), bf16[16,128,256]{2,1,0:T(8,128)(2,1)S(1)}, u32[]{:S(2)}, u32[]{:S(2)}) %all-to-all-start.1) | async-done | bytes 1048608 | tf_op jit(solution)/shard_map/all_to_all | solution.py:374
  77.1 0.9 %shard_map.90 = (bf16[128,512]{1,0:T(8,128)(2,1)}, bf16[128,512]{1,0:T(8,128)(2,1)}, bf16[1,32,2048]{2,1,0:T(8,128)(2,1)}) custom-call(bf16[16,128,256]{2,1,0:T(8,128)(2,1)S(1)} %all-to-all-done.1.parts, bf16[4,32,128]{2,1,0:T(8,128)(2,1)S(1)} %pad_maximum_fusion.4.q0, bf16[4,32,128]{2,1,0:T(8,128)(2,1)S(1)} %collective-permute-done.11.q1, ...), custom_call_target="tpu_custom_call" | custom-call | tf_op jit(solution)/shard_map/pallas_call | solution.py:310
  (21 shorter events, 0.1 us)
Async XLA Ops:
  27.1 17.6 %collective-permute-start.6 = (bf16[2048,256]{1,0:T(8,128)(2,1)S(1)}, bf16[2048,256]{1,0:T(8,128)(2,1)S(1)}, u32[]{:S(2)}, u32[]{:S(2)}) collective-permute-start(bf16[2048,256]{1,0:T(8,128)(2,1)S(1)} %bitcast.3), channel_id=1, source_target_pairs={{0,1},{1,0},{2,3},{3,2},{4,5},{5,4},{6,7},{7,6},{8,9},{9,8},{10,11... | collective-permute-start | bytes 3145736 | tf_op jit(solution)/shard_map/ppermute | solution.py:354
  27.1 6.0 %collective-permute-start = (bf16[4,72,128]{2,1,0:T(8,128)(2,1)S(1)}, bf16[4,72,128]{2,1,0:T(8,128)(2,1)S(1)}, u32[]{:S(2)}, u32[]{:S(2)}) collective-permute-start(bf16[4,72,128]{2,1,0:T(8,128)(2,1)S(1)} %get-tuple-element.22), channel_id=1, source_target_pairs={{0,32},{32,64},{64,96},{96,0},{1,33},{33,65},{65,97},{97,1},{2,34}... | collective-permute-start | bytes 221192 | tf_op jit(solution)/shard_map/ppermute | solution.py:350
  28.7 7.1 %collective-permute-start.1 = (bf16[4,72,128]{2,1,0:T(8,128)(2,1)S(1)}, bf16[4,72,128]{2,1,0:T(8,128)(2,1)S(1)}, u32[]{:S(2)}, u32[]{:S(2)}) collective-permute-start(bf16[4,72,128]{2,1,0:T(8,128)(2,1)S(1)} %get-tuple-element.23), channel_id=1, source_target_pairs={{0,64},{32,96},{64,0},{96,32},{1,65},{33,97},{65,1},{97,33},{2,66}... | collective-permute-start | bytes 221192 | tf_op jit(solution)/shard_map/ppermute | solution.py:350
  31.6 4.4 %collective-permute-start.2 = (bf16[4,72,128]{2,1,0:T(8,128)(2,1)S(1)}, bf16[4,72,128]{2,1,0:T(8,128)(2,1)S(1)}, u32[]{:S(2)}, u32[]{:S(2)}) collective-permute-start(bf16[4,72,128]{2,1,0:T(8,128)(2,1)S(1)} %get-tuple-element.24), channel_id=1, source_target_pairs={{0,96},{32,0},{64,32},{96,64},{1,97},{33,1},{65,33},{97,65},{2,98}... | collective-permute-start | bytes 221192 | tf_op jit(solution)/shard_map/ppermute | solution.py:350
  36.0 6.6 %collective-permute-start.3 = (bf16[4,72,128]{2,1,0:T(8,128)(2,1)S(1)}, bf16[4,72,128]{2,1,0:T(8,128)(2,1)S(1)}, u32[]{:S(2)}, u32[]{:S(2)}) collective-permute-start(bf16[4,72,128]{2,1,0:T(8,128)(2,1)S(1)} %pad_maximum_fusion.1), channel_id=1, source_target_pairs={{0,8},{8,16},{16,24},{24,0},{1,9},{9,17},{17,25},{25,1},{2,10},{10... | collective-permute-start | bytes 221192 | tf_op jit(solution)/shard_map/ppermute | solution.py:350
  36.2 6.4 %collective-permute-start.4 = (bf16[4,72,128]{2,1,0:T(8,128)(2,1)S(1)}, bf16[4,72,128]{2,1,0:T(8,128)(2,1)S(1)}, u32[]{:S(2)}, u32[]{:S(2)}) collective-permute-start(bf16[4,72,128]{2,1,0:T(8,128)(2,1)S(1)} %pad_maximum_fusion.2), channel_id=1, source_target_pairs={{0,16},{8,24},{16,0},{24,8},{1,17},{9,25},{17,1},{25,9},{2,18},{10... | collective-permute-start | bytes 221192 | tf_op jit(solution)/shard_map/ppermute | solution.py:350
  39.1 4.4 %collective-permute-start.5 = (bf16[4,72,128]{2,1,0:T(8,128)(2,1)S(1)}, bf16[4,72,128]{2,1,0:T(8,128)(2,1)S(1)}, u32[]{:S(2)}, u32[]{:S(2)}) collective-permute-start(bf16[4,72,128]{2,1,0:T(8,128)(2,1)S(1)} %pad_maximum_fusion.3), channel_id=1, source_target_pairs={{0,24},{8,0},{16,8},{24,16},{1,25},{9,1},{17,9},{25,17},{2,26},{10... | collective-permute-start | bytes 221192 | tf_op jit(solution)/shard_map/ppermute | solution.py:350
  48.5 4.8 %collective-permute-start.7 = (bf16[2048,256]{1,0:T(8,128)(2,1)S(1)}, bf16[2048,256]{1,0:T(8,128)(2,1)S(1)}, u32[]{:S(2)}, u32[]{:S(2)}) collective-permute-start(bf16[2048,256]{1,0:T(8,128)(2,1)S(1)} %get-tuple-element.31), channel_id=1, source_target_pairs={{0,1},{1,0},{2,3},{3,2},{4,5},{5,4},{6,7},{7,6},{8,9},{9,8},{10,11... | collective-permute-start | bytes 3145736 | tf_op jit(solution)/shard_map/ppermute | solution.py:354
  48.6 10.7 %collective-permute-start.8 = (bf16[4,32,128]{2,1,0:T(8,128)(2,1)S(1)}, bf16[4,32,128]{2,1,0:T(8,128)(2,1)S(1)}, u32[]{:S(2)}, u32[]{:S(2)}) collective-permute-start(bf16[4,32,128]{2,1,0:T(8,128)(2,1)S(1)} %get-tuple-element.33), channel_id=1, source_target_pairs={{0,96},{32,0},{64,32},{96,64},{1,97},{33,1},{65,33},{97,65},{2,98}... | collective-permute-start | bytes 98312 | tf_op jit(solution)/shard_map/ppermute | solution.py:350
  51.2 8.1 %collective-permute-start.9 = (bf16[4,32,128]{2,1,0:T(8,128)(2,1)S(1)}, bf16[4,32,128]{2,1,0:T(8,128)(2,1)S(1)}, u32[]{:S(2)}, u32[]{:S(2)}) collective-permute-start(bf16[4,32,128]{2,1,0:T(8,128)(2,1)S(1)} %get-tuple-element.34), channel_id=1, source_target_pairs={{0,64},{32,96},{64,0},{96,32},{1,65},{33,97},{65,1},{97,33},{2,66}... | collective-permute-start | bytes 98312 | tf_op jit(solution)/shard_map/ppermute | solution.py:350
  51.7 7.6 %collective-permute-start.10 = (bf16[4,32,128]{2,1,0:T(8,128)(2,1)S(1)}, bf16[4,32,128]{2,1,0:T(8,128)(2,1)S(1)}, u32[]{:S(2)}, u32[]{:S(2)}) collective-permute-start(bf16[4,32,128]{2,1,0:T(8,128)(2,1)S(1)} %get-tuple-element.35), channel_id=1, source_target_pairs={{0,32},{32,64},{64,96},{96,0},{1,33},{33,65},{65,97},{97,1},{2,34}... | collective-permute-start | bytes 98312 | tf_op jit(solution)/shard_map/ppermute | solution.py:350
  54.5 22.6 %all-to-all-start.1 = ((bf16[16,128,256]{2,1,0:T(8,128)(2,1)}), bf16[16,128,256]{2,1,0:T(8,128)(2,1)S(1)}, u32[]{:S(2)}, u32[]{:S(2)}) async-start(bf16[16,128,256]{2,1,0:T(8,128)(2,1)} %bitcast.2), calls=%async_computation.1 | async-start | bytes 2097152 | tf_op jit(solution)/shard_map/all_to_all | solution.py:374
  59.4 14.2 %collective-permute-start.11 = (bf16[4,32,128]{2,1,0:T(8,128)(2,1)S(1)}, bf16[4,32,128]{2,1,0:T(8,128)(2,1)S(1)}, u32[]{:S(2)}, u32[]{:S(2)}) collective-permute-start(bf16[4,32,128]{2,1,0:T(8,128)(2,1)S(1)} %pad_maximum_fusion.5), channel_id=1, source_target_pairs={{0,24},{8,0},{16,8},{24,16},{1,25},{9,1},{17,9},{25,17},{2,26},{10... | collective-permute-start | bytes 98312 | tf_op jit(solution)/shard_map/ppermute | solution.py:350
  62.6 12.5 %collective-permute-start.12 = (bf16[4,32,128]{2,1,0:T(8,128)(2,1)S(1)}, bf16[4,32,128]{2,1,0:T(8,128)(2,1)S(1)}, u32[]{:S(2)}, u32[]{:S(2)}) collective-permute-start(bf16[4,32,128]{2,1,0:T(8,128)(2,1)S(1)} %pad_maximum_fusion.6), channel_id=1, source_target_pairs={{0,16},{8,24},{16,0},{24,8},{1,17},{9,25},{17,1},{25,9},{2,18},{10... | collective-permute-start | bytes 98312 | tf_op jit(solution)/shard_map/ppermute | solution.py:350
  63.4 11.7 %collective-permute-start.13 = (bf16[4,32,128]{2,1,0:T(8,128)(2,1)S(1)}, bf16[4,32,128]{2,1,0:T(8,128)(2,1)S(1)}, u32[]{:S(2)}, u32[]{:S(2)}) collective-permute-start(bf16[4,32,128]{2,1,0:T(8,128)(2,1)S(1)} %pad_maximum_fusion.7), channel_id=1, source_target_pairs={{0,8},{8,16},{16,24},{24,0},{1,9},{9,17},{17,25},{25,1},{2,10},{10... | collective-permute-start | bytes 98312 | tf_op jit(solution)/shard_map/ppermute | solution.py:350
